TPU v7x, 32 devices: a whole 2x2x4 slice. The times are simulated.
32 devices in a mesh: stream: 2 (over x), group: 8 (over z, y), dp: 2 (over core).
Axes of the slice: x: 2, y: 2, z: 4, core: 2. Of those that a mesh axis runs over, the one named last changes fastest.
Arguments:
- tokens: bfloat16 [2, 8192, 768], P('stream', ('group', 'dp')), may hold values from -6 to 6
- cotangent: bfloat16 [2, 8192, 768], P('stream', ('group', 'dp')), may hold values from -6 to 6
- box_bins: int32 [2, 2, 16, 512], P(None, None, ('group', 'dp')), may hold values from 0 to 127
- segment_ids: int32 [2, 16, 512], P(None, ('group', 'dp')), may hold values from 0 to 63, never falling along the last dimension, each value on 1 to 16 neighbouring positions
- key_mask: int32 [2, 16, 512], P(None, ('group', 'dp')), may hold values from 0 to 1, as said below
- ln1_gain: float32 [2, 768], P('stream'), may hold values from 0.5 to 1.5
- ln1_bias: float32 [2, 768], P('stream'), may hold values from -1.75 to 1.75
- w_qkv: bfloat16 [2, 768, 2304], P('stream'), may hold values from -0.21875 to 0.21875
- bias_q: float32 [2, 768], P('stream'), may hold values from -1.75 to 1.75
- bias_v: float32 [2, 768], P('stream'), may hold values from -1.75 to 1.75
- w_out: bfloat16 [2, 768, 768], P('stream'), may hold values from -1.75 to 1.75
- bias_out: float32 [2, 768], P('stream'), may hold values from -1.75 to 1.75
- ln2_gain: float32 [2, 768], P('stream'), may hold values from 0.5 to 1.5
- ln2_bias: float32 [2, 768], P('stream'), may hold values from -1.75 to 1.75
- w_in: bfloat16 [2, 768, 3072], P('stream'), may hold values from -0.21875 to 0.21875
- bias_in: float32 [2, 3072], P('stream'), may hold values from -3 to 3
- w_back: bfloat16 [2, 3072, 768], P('stream'), may hold values from -0.109375 to 0.109375
- bias_back: float32 [2, 768], P('stream'), may hold values from -1.75 to 1.75
- rel_table: float32 [2, 4608], P('stream'), may hold values from -3 to 3
Outputs:
- output: bfloat16 [2, 8192, 768], P('stream', ('group', 'dp'))
- g_tokens: bfloat16 [2, 8192, 768], P('stream', ('group', 'dp'))
- g_ln1_gain: float32 [2, 768], P('stream', 'dp')
- g_ln1_bias: float32 [2, 768], P('stream', 'dp')
- g_w_qkv: float32 [2, 768, 2304], P('stream', 'dp')
- g_bias_q: float32 [2, 768], P('stream', 'dp')
- g_bias_v: float32 [2, 768], P('stream', 'dp')
- g_w_out: float32 [2, 768, 768], P('stream', 'dp')
- g_bias_out: float32 [2, 768], P('stream', 'dp')
- g_ln2_gain: float32 [2, 768], P('stream', 'dp')
- g_ln2_bias: float32 [2, 768], P('stream', 'dp')
- g_w_in: float32 [2, 768, 3072], P('stream', 'dp')
- g_bias_in: float32 [2, 3072], P('stream', 'dp')
- g_w_back: float32 [2, 3072, 768], P('stream', 'dp')
- g_bias_back: float32 [2, 768], P('stream', 'dp')
- g_rel_table: float32 [2, 4608], P('stream', 'dp')
Inputs may be any that keep to these rules, and one draw needn't show every extreme that they name: `key_mask`: the first token of every page is 1 in each stream. `segment_ids`: within a page the segment number never falls, every one of the 64 segments is present, each with 1 to 16 tokens.
All inputs are finite; a program needn't handle non-finite values.
Results may differ from a plain program's by a relative error of at most 0.012.
Values may be sent and summed in bfloat16 or wider, within the bound.
No kernel may reach another device: no remote copies, remote signals or barrier semaphores. Data moves between devices by JAX's collectives and lax.ppermute only.
A program may use at most 256 MiB of HBM per device.

v0:
```python
import functools
import jax
import jax.numpy as jnp
from jax import lax
from jax.experimental import pallas as pl
from jax.experimental.pallas import tpu as pltpu
from jax.sharding import PartitionSpec as P

EPSILON = 1e-05
STRIP = 64
HEADS = 12
BINS = 128
GROUPS = 3
NEGATIVE = -1000000000.0
HIGHEST = lax.Precision.HIGHEST
RING = 8
RING_ORDER = (0, 2, 4, 6, 7, 5, 3, 1)
ROOT_HALF = 0.7071067811865476
DENSITY = 0.3989422804014327


def dot_plain(a, b):
    return lax.dot_general(a, b, (((1,), (0,)), ((), ())), preferred_element_type=jnp.float32)


def dot_across(a, b):
    return lax.dot_general(a, b, (((0,), (0,)), ((), ())), preferred_element_type=jnp.float32)


def dot_back(a, b):
    return lax.dot_general(a, b, (((1,), (1,)), ((), ())), preferred_element_type=jnp.float32)


def row_stats(rows):
    center = rows - jnp.mean(rows, axis=-1, keepdims=True)
    spread = jnp.mean(center * center, axis=-1, keepdims=True)
    rate = lax.rsqrt(spread + EPSILON)
    return center * rate, rate


def fold(rows):
    return jnp.sum(rows.reshape(rows.shape[0] // 8, 8, rows.shape[1]), axis=0)


def strips(count, body):
    for index in range(count // STRIP):
        body(pl.ds(index * STRIP, STRIP))


def place_chunk(target, mine_ref, other_ref, value, rows=slice(None)):
    @pl.when(target < 8)
    def _():
        mine_ref[target, rows, :] = value

    @pl.when(target >= 8)
    def _():
        other_ref[target - 8, rows, :] = value


def put_halves(small_ref, row, vector):
    half = vector.shape[1] // 2
    width = small_ref.shape[2]
    for side in range(2):
        for piece in range(half // width):
            start = side * half + piece * width
            small_ref[side, row + piece : row + piece + 1, :] = vector[:, start : start + width]


def feed_kernel(
    order_ref,
    tokens_ref,
    context_0_ref,
    context_1_ref,
    context_2_ref,
    cot_ref,
    w_out_ref,
    b_out_ref,
    gain_ref,
    shift_ref,
    w_in_ref,
    b_in_ref,
    w_back_ref,
    b_back_ref,
    out_ref,
    d_middle_ref,
    d_branch_ref,
    d_context_ref,
    mine_ref,
    other_ref,
    small_ref,
    middle_ref,
    normed_ref,
    turned_ref,
    pre_ref,
    d_act_ref,
    act_ref,
    d_pre_ref,
    total_ref,
    d_normed_ref,
    sums_ref,
    in_sum_ref,
):
    step = pl.program_id(0)
    last = pl.num_programs(0) - 1
    rows = tokens_ref.shape[0]
    block = w_in_ref.shape[1]

    @pl.when(step == 0)
    def _():
        part = context_0_ref.shape[1]
        middle_ref[...] = (
            dot_plain(context_0_ref[...], w_out_ref[:part])
            + dot_plain(context_1_ref[...], w_out_ref[part : 2 * part])
            + dot_plain(context_2_ref[...], w_out_ref[2 * part :])
        )
        sums_ref[...] = jnp.zeros_like(sums_ref)
        small_ref[...] = jnp.zeros_like(small_ref)
        total_ref[...] = jnp.zeros_like(total_ref)
        d_normed_ref[...] = jnp.zeros_like(d_normed_ref)

        def first(at):
            value = middle_ref[at, :] + tokens_ref[at, :].astype(jnp.float32) + b_out_ref[...]
            middle_ref[at, :] = value
            hat, _ = row_stats(value)
            normed_ref[at, :] = (hat * gain_ref[...] + shift_ref[...]).astype(jnp.bfloat16)
            sums_ref[0] += fold(cot_ref[at, :].astype(jnp.float32))

        strips(rows, first)
        turned_ref[...] = normed_ref[...].T

    pre_ref[...] = dot_plain(normed_ref[...], w_in_ref[...])
    d_act_ref[...] = dot_back(cot_ref[...], w_back_ref[...])
    in_sum_ref[...] = jnp.zeros_like(in_sum_ref)

    def middle_part(at):
        value = pre_ref[at, :] + b_in_ref[...]
        chance = 0.5 + 0.5 * lax.erf(value * ROOT_HALF)
        slope = chance + value * (DENSITY * jnp.exp(-0.5 * value * value))
        act_ref[at, :] = (value * chance).astype(jnp.bfloat16)
        d_pre = (d_act_ref[at, :] * slope).astype(jnp.bfloat16)
        d_pre_ref[at, :] = d_pre
        in_sum_ref[...] += fold(d_pre.astype(jnp.float32))

    strips(rows, middle_part)
    total_ref[...] += dot_plain(act_ref[...], w_back_ref[...])
    d_normed_ref[...] += dot_back(d_pre_ref[...], w_in_ref[...])
    per_block = block // 192
    back = dot_across(act_ref[...], cot_ref[...]).astype(jnp.bfloat16)
    for piece in range(per_block):
        place_chunk(
            order_ref[step * per_block + piece],
            mine_ref,
            other_ref,
            back[piece * 192 : piece * 192 + 192],
            slice(0, 192),
        )
    inward = dot_plain(turned_ref[...], d_pre_ref[...]).astype(jnp.bfloat16)
    at_rows = pl.ds(pl.multiple_of(192 + step * 48, 16), 48)
    for piece in range(16):
        place_chunk(
            order_ref[piece], mine_ref, other_ref, inward[piece * 48 : piece * 48 + 48], at_rows
        )
    in_sum = jnp.sum(in_sum_ref[...], axis=0, keepdims=True)
    side = step // 2
    row = 8 + 2 * (step % 2)
    small_ref[side, pl.ds(row, 1), :] = in_sum[:, :384]
    small_ref[side, pl.ds(row + 1, 1), :] = in_sum[:, 384:]

    @pl.when(step == last)
    def _():
        def final(at):
            value = middle_ref[at, :]
            out_ref[at, :] = (value + total_ref[at, :] + b_back_ref[...]).astype(jnp.bfloat16)
            hat, rate = row_stats(value)
            d_normed = d_normed_ref[at, :]
            sums_ref[1] += fold(d_normed * hat)
            sums_ref[2] += fold(d_normed)
            scaled = d_normed * gain_ref[...]
            inner = (
                scaled
                - jnp.mean(scaled, axis=-1, keepdims=True)
                - hat * jnp.mean(scaled * hat, axis=-1, keepdims=True)
            )
            d_middle = cot_ref[at, :].astype(jnp.float32) + rate * inner
            d_middle_ref[at, :] = d_middle
            branch = d_middle.astype(jnp.bfloat16)
            d_branch_ref[at, :] = branch
            sums_ref[3] += fold(branch.astype(jnp.float32))

        strips(rows, final)
        d_context_ref[...] = dot_back(d_branch_ref[...], w_out_ref[...]).astype(jnp.bfloat16)
        for index, row in ((0, 7), (1, 5), (2, 6), (3, 4)):
            put_halves(small_ref, row, jnp.sum(sums_ref[index], axis=0, keepdims=True))


def feed_call(order, tokens, contexts, cot, w_out, b_out, gain, shift, w_in, b_in, w_back, b_back):
    rows, width = tokens.shape
    inner = w_in.shape[1]
    block = 768
    fixed = lambda shape: pl.BlockSpec(shape, lambda j, o: (0,) * len(shape), pipeline_mode=pl.Buffered(1))
    wide = lambda dtype: jax.ShapeDtypeStruct((rows, width), dtype)
    ring = jax.ShapeDtypeStruct((RING, 384, width), jnp.bfloat16)
    f32, bf16 = jnp.float32, jnp.bfloat16
    vmem = pltpu.VMEM
    return pl.pallas_call(
        feed_kernel,
        out_shape=(wide(bf16), wide(f32), wide(bf16), wide(bf16), ring, ring,
                   jax.ShapeDtypeStruct((2, 24, 384), f32)),
        grid_spec=pltpu.PrefetchScalarGridSpec(
            num_scalar_prefetch=1,
            grid=(inner // block,),
            in_specs=[
                fixed((rows, width)),
                fixed((rows, width // GROUPS)), fixed((rows, width // GROUPS)), fixed((rows, width // GROUPS)),
                fixed((rows, width)),
                fixed((width, width)), fixed((1, width)), fixed((1, width)), fixed((1, width)),
                pl.BlockSpec((width, block), lambda j, o: (0, j)),
                pl.BlockSpec((1, block), lambda j, o: (0, j)),
                pl.BlockSpec((block, width), lambda j, o: (j, 0)),
                fixed((1, width)),
            ],
            out_specs=[fixed((rows, width))] * 4 + [fixed((RING, 384, width))] * 2 + [fixed((2, 24, 384))],
            scratch_shapes=[
                vmem((rows, width), f32), vmem((rows, width), bf16), vmem((width, rows), bf16),
                vmem((rows, block), f32), vmem((rows, block), f32),
                vmem((rows, block), bf16), vmem((rows, block), bf16),
                vmem((rows, width), f32), vmem((rows, width), f32),
                vmem((4, 8, width), f32), vmem((8, block), f32),
            ],
        ),
        compiler_params=pltpu.CompilerParams(vmem_limit_bytes=60 << 20),
        cost_estimate=price(30),
        name="feed",
    )(order, tokens, *contexts, cot, w_out, b_out, gain, shift, w_in, b_in, w_back, b_back)


def first_kernel(tokens_ref, gain_ref, shift_ref, w_ref, bias_ref, normed_ref, *sent_refs):
    rows, width = tokens_ref.shape

    def norm(at):
        hat, _ = row_stats(tokens_ref[at, :].astype(jnp.float32))
        normed_ref[at, :] = (hat * gain_ref[...] + shift_ref[...]).astype(jnp.bfloat16)

    strips(rows, norm)
    part = width // GROUPS
    for group, sent_ref in enumerate(sent_refs):
        at = group * part
        sent_ref[0] = dot_plain(normed_ref[...], w_ref[:, width + at : width + at + part]).astype(jnp.bfloat16)
        sent_ref[1] = (
            dot_plain(normed_ref[...], w_ref[:, 2 * width + at : 2 * width + at + part])
            + bias_ref[:, at : at + part]
        ).astype(jnp.bfloat16)


def whole_specs(count):
    return [pl.BlockSpec(memory_space=pltpu.VMEM)] * count


def price(micros):
    return pl.CostEstimate(flops=int(micros * 1e9), transcendentals=0, bytes_accessed=0)


def kernel_call(kernel, name, micros, outs, *args, scratch=(), smem=0, aliases={}):
    specs = [pl.BlockSpec(memory_space=pltpu.SMEM)] * smem + whole_specs(len(args) - smem)
    return pl.pallas_call(
        kernel,
        out_shape=tuple(outs),
        in_specs=specs,
        out_specs=tuple(whole_specs(len(outs))),
        scratch_shapes=list(scratch),
        input_output_aliases=aliases,
        cost_estimate=price(micros),
        compiler_params=pltpu.CompilerParams(vmem_limit_bytes=60 << 20),
        name=name,
    )(*args)


def first_call(tokens, gain, shift, w_qkv, bias_v):
    rows, width = tokens.shape
    outs = [jax.ShapeDtypeStruct((rows, width), jnp.bfloat16)]
    outs += [jax.ShapeDtypeStruct((2, rows, width // GROUPS), jnp.bfloat16)] * GROUPS
    return kernel_call(first_kernel, "first", 5, outs, tokens, gain, shift, w_qkv, bias_v)


def code_columns(rows_of_codes, rows):
    blank = jnp.zeros((5, rows), jnp.float32)
    return jnp.concatenate([r.astype(jnp.float32) for r in rows_of_codes] + [blank], axis=0).T


def prep_kernel(
    stream_ref, box_ref, segment_ref, mask_ref, normed_ref, w_ref, bias_ref, table_ref,
    queries_ref, hot_ref, turned_hot_ref, key_hot_ref, live_ref, tiles_ref,
):
    rows = normed_ref.shape[0]
    own = stream_ref[0]
    far = 1 - own
    queries_ref[...] = (dot_plain(normed_ref[...], w_ref[:, : normed_ref.shape[1]]) + bias_ref[...]).astype(jnp.bfloat16)
    live_ref[...] = mask_ref[far]
    own_codes = code_columns([box_ref[own, 0], box_ref[own, 1], segment_ref[own]], rows)
    far_codes = code_columns([box_ref[far, 0], box_ref[far, 1], segment_ref[far]], rows)
    levels = lax.broadcasted_iota(jnp.int32, (rows, BINS), 1).astype(jnp.float32)
    for axis in range(3):
        lanes = slice(axis * BINS, axis * BINS + BINS)
        column = own_codes[:, axis : axis + 1]
        hot_ref[:, lanes] = jnp.where(column == levels, 1.0, 0.0).astype(jnp.bfloat16)
        turned_hot_ref[:, lanes] = jnp.where(BINS - 1 - column == levels, 1.0, 0.0).astype(jnp.bfloat16)
        key_hot_ref[:, lanes] = jnp.where(far_codes[:, axis : axis + 1] == levels, 1.0, 0.0).astype(jnp.bfloat16)
    half = BINS // 2
    entry = lax.broadcasted_iota(jnp.int32, (BINS, 2 * BINS), 0)
    gap = lax.broadcasted_iota(jnp.int32, (BINS, 2 * BINS), 1)
    gap = jnp.where(gap < BINS, -gap, 2 * BINS - gap)
    pick = jnp.where(jnp.clip(gap, -half, half - 1) + half == entry, 1.0, 0.0).astype(jnp.bfloat16)
    spread = dot_plain(table_ref[...].astype(jnp.bfloat16), pick)
    for index in range(3 * HEADS):
        wide = jnp.broadcast_to(spread[index : index + 1, :], (BINS, 2 * BINS))
        rolled = pltpu.roll(wide, 0, 1, stride=1, stride_axis=0)
        tiles_ref[index] = rolled[:, :BINS].astype(jnp.bfloat16)


def prep_call(stream, box_bins, segment_ids, key_mask, normed, w_qkv, bias_q, table):
    rows, width = normed.shape
    hot = jax.ShapeDtypeStruct((rows, 3 * BINS), jnp.bfloat16)
    outs = [
        jax.ShapeDtypeStruct((rows, width), jnp.bfloat16), hot, hot, hot,
        jax.ShapeDtypeStruct((1, rows), jnp.int32),
        jax.ShapeDtypeStruct((3 * HEADS, BINS, BINS), jnp.bfloat16),
    ]
    return kernel_call(prep_kernel, "prep", 5, outs, stream, box_bins, segment_ids, key_mask, normed, w_qkv, bias_q, table, smem=1)


def half_of(slab, odd):
    lane = lax.broadcasted_iota(jnp.int32, slab.shape, 1)
    keep = (lane >= 64) if odd else (lane < 64)
    return jnp.where(keep, slab, jnp.zeros_like(slab))


def attend_kernel(group, queries_ref, pair_ref, hot_ref, key_hot_ref, live_ref, tiles_ref,
                  context_ref, probs_ref, left_ref, right_ref, scores_ref):
    rows = queries_ref.shape[0]
    part = pair_ref.shape[2]
    for slab in range(part // 128):
        lanes = slice(slab * 128, slab * 128 + 128)
        wide = slice(group * part + slab * 128, group * part + slab * 128 + 128)
        right_ref[slab, :, :128] = pair_ref[0, :, lanes]
        right_ref[slab, :, 128:] = key_hot_ref[...]
        halves = []
        for odd in range(2):
            head = slab * 2 + odd
            left_ref[head, :, :128] = half_of(queries_ref[:, wide].astype(jnp.float32) * 0.125, odd).astype(jnp.bfloat16)
            for axis in range(3):
                cut = slice(axis * BINS, axis * BINS + BINS)
                tile = tiles_ref[axis * HEADS + group * (part // 64) + head]
                left_ref[head, :, 128 + axis * BINS : 256 + axis * BINS] = dot_plain(hot_ref[:, cut], tile).astype(jnp.bfloat16)
            scores_ref[head] = dot_back(left_ref[head], right_ref[slab])

            def soft(at):
                scores = jnp.where(live_ref[...] > 0, scores_ref[head, at, :], NEGATIVE)
                top = jnp.max(scores, axis=-1, keepdims=True)
                weights = jnp.exp(scores - top)
                rate = 1.0 / jnp.sum(weights, axis=-1, keepdims=True)
                probs_ref[head, at, :] = (weights * rate).astype(jnp.bfloat16)

            strips(rows, soft)
            halves.append(half_of(dot_plain(probs_ref[head], pair_ref[1, :, lanes]), odd))
        context_ref[:, lanes] = (halves[0] + halves[1]).astype(jnp.bfloat16)


def attend_call(group, queries, pair, hot, key_hot, live, tiles):
    rows = queries.shape[0]
    part = pair.shape[2]
    heads = part // 64
    outs = [
        jax.ShapeDtypeStruct((rows, part), jnp.bfloat16),
        jax.ShapeDtypeStruct((heads, rows, rows), jnp.bfloat16),
    ]
    scratch = [
        pltpu.VMEM((heads, rows, 512), jnp.bfloat16),
        pltpu.VMEM((part // 128, rows, 512), jnp.bfloat16),
        pltpu.VMEM((heads, rows, rows), jnp.float32),
    ]
    return kernel_call(functools.partial(attend_kernel, group), f"attend_{group}", 7, outs,
                       queries, pair, hot, key_hot, live, tiles, scratch=scratch)


def attend_back_kernel(group, queries_ref, pair_ref, turned_hot_ref, key_hot_ref, probs_ref, d_context_ref,
                       d_queries_ref, d_pair_ref, diagonal_ref, right_ref, slope_ref, d_scores_ref):
    rows = queries_ref.shape[0]
    part = pair_ref.shape[2]
    for slab in range(part // 128):
        lanes = slice(slab * 128, slab * 128 + 128)
        wide = slice(group * part + slab * 128, group * part + slab * 128 + 128)
        right_ref[slab, :, :128] = pair_ref[0, :, lanes]
        right_ref[slab, :, 128:] = key_hot_ref[...]
        d_query = d_key = d_value = 0.0
        for odd in range(2):
            head = slab * 2 + odd
            query = half_of(queries_ref[:, wide], odd)
            d_context = half_of(d_context_ref[:, wide], odd)
            slope_ref[head] = dot_back(d_context, pair_ref[1, :, lanes])

            def soft(at):
                probs = probs_ref[head, at, :].astype(jnp.float32)
                slope = slope_ref[head, at, :]
                centre = jnp.sum(probs * slope, axis=-1, keepdims=True)
                d_scores_ref[head, at, :] = (probs * (slope - centre)).astype(jnp.bfloat16)

            strips(rows, soft)
            d_value = d_value + dot_across(probs_ref[head], d_context)
            d_key = d_key + dot_across(d_scores_ref[head], query)
            both = dot_plain(d_scores_ref[head], right_ref[slab])
            d_query = d_query + half_of(both[:, :128], odd)
            spread = both[:, 128:].astype(jnp.bfloat16)
            for axis in range(3):
                cut = slice(axis * BINS, axis * BINS + BINS)
                tile = dot_across(turned_hot_ref[:, cut], spread[:, cut])
                padded = jnp.concatenate([tile, jnp.zeros_like(tile)], axis=1)
                rolled = pltpu.roll(padded, 0, 1, stride=1, stride_axis=0)
                diagonal_ref[axis, head : head + 1, :] = jnp.sum(rolled, axis=0, keepdims=True)
        d_queries_ref[:, lanes] = (d_query * 0.125).astype(jnp.bfloat16)
        d_pair_ref[0, :, lanes] = (d_key * 0.125).astype(jnp.bfloat16)
        d_pair_ref[1, :, lanes] = d_value.astype(jnp.bfloat16)


def attend_back_call(group, queries, pair, turned_hot, key_hot, probs, d_context):
    rows = queries.shape[0]
    part = pair.shape[2]
    heads = part // 64
    outs = [
        jax.ShapeDtypeStruct((rows, part), jnp.bfloat16),
        jax.ShapeDtypeStruct((2, rows, part), jnp.bfloat16),
        jax.ShapeDtypeStruct((3, heads, 2 * BINS), jnp.float32),
    ]
    scratch = [
        pltpu.VMEM((part // 128, rows, 512), jnp.bfloat16),
        pltpu.VMEM((heads, rows, rows), jnp.float32),
        pltpu.VMEM((heads, rows, rows), jnp.bfloat16),
    ]
    return kernel_call(functools.partial(attend_back_kernel, group), f"attend_back_{group}", 8, outs,
                       queries, pair, turned_hot, key_hot, probs, d_context, scratch=scratch)


def weights_kernel(
    order_ref, normed_ref, d_branch_ref, context_0_ref, context_1_ref, context_2_ref,
    d_query_0_ref, d_query_1_ref, d_query_2_ref, back_0_ref, back_1_ref, back_2_ref,
    mine_ref, other_ref, joined_ref,
):
    part = context_0_ref.shape[1]
    queries = (d_query_0_ref, d_query_1_ref, d_query_2_ref)
    backs = (back_0_ref, back_1_ref, back_2_ref)
    contexts = (context_0_ref, context_1_ref, context_2_ref)
    for group in range(GROUPS):
        lanes = slice(group * part, group * part + part)
        joined_ref[0, :, lanes] = queries[group][...]
        joined_ref[1, :, lanes] = backs[group][0]
        joined_ref[2, :, lanes] = backs[group][1]
        joined_ref[3, :, lanes] = contexts[group][...]
    for block in range(4):
        if block < 3:
            value = dot_across(normed_ref[...], joined_ref[block]).astype(jnp.bfloat16)
        else:
            value = dot_across(joined_ref[3], d_branch_ref[...]).astype(jnp.bfloat16)
        for piece in range(16):
            place_chunk(
                order_ref[piece], mine_ref, other_ref, value[piece * 48 : piece * 48 + 48],
                slice(block * 48, block * 48 + 48),
            )


def weights_call(order, normed, d_branch, contexts, d_queries, backs):
    rows, width = normed.shape
    ring = jax.ShapeDtypeStruct((RING, 192, width), jnp.bfloat16)
    scratch = [pltpu.VMEM((4, rows, width), jnp.bfloat16)]
    return kernel_call(weights_kernel, "weights", 7, [ring, ring], order, normed, d_branch,
                       *contexts, *d_queries, *backs, scratch=scratch, smem=1)


def last_kernel(
    tokens_ref, gain_ref, w_ref, d_middle_ref, d_query_0_ref, d_query_1_ref, d_query_2_ref,
    back_0_ref, back_1_ref, back_2_ref, diagonal_0_ref, diagonal_1_ref, diagonal_2_ref, start_ref,
    g_tokens_ref, small_ref, d_normed_ref, sums_ref,
):
    rows, width = tokens_ref.shape
    part = width // GROUPS
    queries = (d_query_0_ref, d_query_1_ref, d_query_2_ref)
    backs = (back_0_ref, back_1_ref, back_2_ref)
    small_ref[...] = start_ref[...]
    sums_ref[...] = jnp.zeros_like(sums_ref)
    total = 0.0
    for group in range(GROUPS):
        at = group * part
        total = total + dot_back(queries[group][...], w_ref[:, at : at + part])
        total = total + dot_back(backs[group][0], w_ref[:, width + at : width + at + part])
        total = total + dot_back(backs[group][1], w_ref[:, 2 * width + at : 2 * width + at + part])
    d_normed_ref[...] = total

    def final(at):
        hat, rate = row_stats(tokens_ref[at, :].astype(jnp.float32))
        d_normed = d_normed_ref[at, :]
        sums_ref[0] += fold(d_normed * hat)
        sums_ref[1] += fold(d_normed)
        for group in range(GROUPS):
            lanes = slice(group * part, group * part + part)
            sums_ref[2, :, lanes] += fold(queries[group][at, :].astype(jnp.float32))
            sums_ref[3, :, lanes] += fold(backs[group][1, at, :].astype(jnp.float32))
        scaled = d_normed * gain_ref[...]
        inner = (
            scaled
            - jnp.mean(scaled, axis=-1, keepdims=True)
            - hat * jnp.mean(scaled * hat, axis=-1, keepdims=True)
        )
        g_tokens_ref[at, :] = (d_middle_ref[at, :] + rate * inner).astype(jnp.bfloat16)

    strips(rows, final)
    for row in range(4):
        put_halves(small_ref, row, jnp.sum(sums_ref[row], axis=0, keepdims=True))
    half = BINS // 2
    gap = BINS - 1 - lax.broadcasted_iota(jnp.int32, (2 * BINS, BINS), 0)
    entry = lax.broadcasted_iota(jnp.int32, (2 * BINS, BINS), 1)
    pick = jnp.where(jnp.clip(gap, -half, half - 1) + half == entry, 1.0, 0.0)
    for group, diagonal_ref in enumerate((diagonal_0_ref, diagonal_1_ref, diagonal_2_ref)):
        for axis in range(3):
            table = lax.dot_general(
                diagonal_ref[axis], pick, (((1,), (0,)), ((), ())),
                precision=HIGHEST, preferred_element_type=jnp.float32,
            )
            for head in range(part // 64):
                index = axis * HEADS + group * (part // 64) + head
                side, place = divmod(index, 18)
                row, lane = divmod(place, 3)
                small_ref[side, 12 + row : 13 + row, lane * BINS : lane * BINS + BINS] = table[head : head + 1, :]


def last_call(tokens, gain, w_qkv, d_middle, d_queries, backs, diagonals, start):
    rows, width = tokens.shape
    outs = [jax.ShapeDtypeStruct((rows, width), jnp.bfloat16), jax.ShapeDtypeStruct(start.shape, jnp.float32)]
    scratch = [pltpu.VMEM((rows, width), jnp.float32), pltpu.VMEM((4, 8, width), jnp.float32)]
    return kernel_call(last_kernel, "last", 8, outs, tokens, gain, w_qkv, d_middle,
                       *d_queries, *backs, *diagonals, start, scratch=scratch)


def open_kernel(layout, place_ref, *refs):
    width = refs[0].shape[1]
    for out_ref, (start, blocks) in zip(refs[RING:], layout):
        size = out_ref.shape[0] // RING
        for index in range(RING):
            to = pl.ds(pl.multiple_of(place_ref[index] * size, size), size)
            for block in range(blocks):
                at = start + block * size
                out_ref[to, block * width : block * width + width] = refs[index][at : at + size, :].astype(jnp.float32)


OPEN_LAYOUTS = {"back": ((0, 1),), "inward": ((0, 4),), "rest": ((0, 3), (144, 1))}


def open_call(name, places, chunks):
    layout = OPEN_LAYOUTS[name]
    width = chunks[0].shape[1]
    outs = [
        jax.ShapeDtypeStruct((RING * (192 if name == "back" else 48), blocks * width), jnp.float32)
        for _, blocks in layout
    ]
    return kernel_call(functools.partial(open_kernel, layout), f"open_{name}", 4, outs, places, *chunks, smem=1)


def open_small_kernel(side_ref, small_ref, *outs):
    side = side_ref[0]
    for row in range(8):
        outs[row][...] = small_ref[side, row : row + 1, :]
    for row in range(4):
        outs[8][:, row * 384 : row * 384 + 384] = small_ref[side, 8 + row : 9 + row, :]
    for row in range(6):
        outs[9][:, row * 384 : row * 384 + 384] = small_ref[side, 12 + row : 13 + row, :]


def partner_2(shard, axis, distance):
    return lax.ppermute(shard, axis, [(i, i ^ 1 << distance) for i in range(lax.axis_size(axis))])


def ring_send(chunk):
    pairs = []
    for place in range(RING):
        ahead = RING_ORDER[(place + 1) % RING]
        behind = RING_ORDER[(place - 1) % RING]
        pairs.append((RING_ORDER[place] * 2, ahead * 2))
        pairs.append((RING_ORDER[place] * 2 + 1, behind * 2 + 1))
    return lax.ppermute(chunk, ("group", "dp"), pairs)


def ring_place():
    group = lax.axis_index("group")
    place = jnp.int32(0)
    for position, member in enumerate(RING_ORDER):
        place = jnp.where(group == member, position, place)
    return place


def ring_plan(ringed):
    index = lax.iota(jnp.int32, 2 * RING)
    steps = lax.iota(jnp.int32, RING)
    if not ringed:
        return index, steps
    dp = lax.axis_index("dp")
    place = ring_place()
    side = index // RING
    start = jnp.where(side == 0, place, RING - place)
    order = (start - index % RING + RING) % RING + jnp.where(side == dp, 0, RING)
    start = jnp.where(dp == 0, place, RING - place)
    return order, (start + 1 - steps + RING) % RING


def add_low(*terms):
    return sum(term.astype(jnp.float32) for term in terms).astype(jnp.bfloat16)


def unringed_total(mine, other):
    return lax.psum(jnp.concatenate([mine, other]).astype(jnp.float32), ("group", "dp"))


def unringed_rows(packed):
    blocks = packed.shape[1] // 48
    rows = packed.reshape(2 * RING, blocks, 48, packed.shape[2])
    return jnp.swapaxes(rows, 1, 2).reshape(2 * RING * 48, blocks * packed.shape[2])


def own_share(whole):
    share = whole.shape[0] // lax.axis_size("dp")
    return lax.dynamic_slice_in_dim(whole, lax.axis_index("dp") * share, share, 0)[None]


def unringed_grads(feed, rest, small):
    feed = unringed_total(*feed)
    rest = unringed_total(*rest)
    small = lax.psum(small, ("group", "dp"))
    vectors = [small[:, row].reshape(-1) for row in range(8)]
    vectors += [small[:, 8:12].reshape(-1), small[:, 12:18].reshape(-1)]
    weights = (
        feed[:, :192].reshape(-1, feed.shape[2]),
        unringed_rows(feed[:, 192:]),
        unringed_rows(rest[:, :144]),
        unringed_rows(rest[:, 144:]),
    )
    return [own_share(weight) for weight in weights], [own_share(vector) for vector in vectors]


class Ordered:
    def __init__(self):
        self.mark = None
        self.free = False

    def after(self, value):
        if self.mark is None or self.free:
            return value
        return lax.optimization_barrier((value, self.mark))[0]

    def wait(self, *values):
        self.mark = (self.mark, *values)


class Ring:
    def __init__(self, order, mine, other):
        self.order, self.mine = order, mine
        self.met = lax.ppermute(order.after(other), "dp", [(0, 1), (1, 0)])
        self.arrived, self.step = None, 0

    def reduce(self):
        step, order = self.step, self.order
        if step == 0:
            held = add_low(self.mine[0], order.after(self.met)[0])
        else:
            held = add_low(order.after(self.arrived), self.mine[step], self.met[step])
        order.mark = held
        if step < RING - 1:
            self.arrived = ring_send(held)
        self.step += 1
        return held


def gather(held, waits={}):
    chunks = [held]
    for step in range(1, RING):
        held = ring_send(held)
        if step in waits:
            held = waits[step](held)
        chunks.append(held)
    return chunks


SMALL_EARLY = (4, 6)
SMALL_PAIRS = (("dp", 0), ("group", 0), ("group", 1), ("group", 2))


class Small:
    def __init__(self, order, small):
        self.order, self.small, self.step = order, small, 0
        self.send()

    def send(self):
        self.arrived = partner_2(self.small, *SMALL_PAIRS[self.step])

    def advance(self):
        self.small = self.small + self.order.after(self.arrived)
        self.order.mark = self.small
        self.step += 1
        if self.step < len(SMALL_PAIRS):
            self.send()


def on_device(
    tokens, cotangent, box_bins, segment_ids, key_mask, ln1_gain, ln1_bias, w_qkv, bias_q, bias_v,
    w_out, bias_out, ln2_gain, ln2_bias, w_in, bias_in, w_back, bias_back, rel_table,
):
    ringed = lax.axis_size("group") == RING and lax.axis_size("dp") == 2
    width = tokens.shape[2]
    order, places = ring_plan(ringed)
    queue = Ordered()
    stream = lax.axis_index("stream").reshape(1)
    normed, *sent = first_call(tokens[0], ln1_gain, ln1_bias, w_qkv[0], bias_v)
    pairs = [partner_2(pair, "stream", 0) for pair in sent]
    queries, hot, turned_hot, key_hot, live, tiles = prep_call(
        stream, box_bins, segment_ids, key_mask, normed, w_qkv[0], bias_q, rel_table.reshape(3 * HEADS, BINS)
    )
    contexts, probs = [], []
    for group in range(GROUPS):
        context, prob = attend_call(group, queries, queue.after(pairs[group]), hot, key_hot, live, tiles)
        queue.mark = context
        contexts.append(context)
        probs.append(prob)
    output, d_middle, d_branch, d_context, feed_mine, feed_other, small = feed_call(
        order, tokens[0], contexts, cotangent[0], w_out[0], bias_out, ln2_gain, ln2_bias,
        w_in[0], bias_in, w_back[0], bias_back,
    )
    if ringed:
        feed = Ring(queue, feed_mine, feed_other)
    d_queries, backs, diagonals = [None] * GROUPS, [None] * GROUPS, [None] * GROUPS
    for group in range(GROUPS):
        d_queries[group], d_pair, diagonals[group] = attend_back_call(
            group, queries, pairs[group], turned_hot, key_hot, probs[group], queue.after(d_context)
        )
        queue.mark = d_queries[group]
        if ringed:
            if group == GROUPS - 1:
                feed.reduce()
                d_pair = queue.after(d_pair)
            backs[group] = partner_2(d_pair, "stream", 0)
            if group < GROUPS - 1:
                feed.reduce()
            if group:
                queue.wait(backs[group - 1])
        else:
            backs[group] = partner_2(d_pair, "stream", 0)
    rest_mine, rest_other = weights_call(order, queue.after(normed), d_branch, contexts, d_queries, backs)
    if ringed:
        queue.mark = rest_mine
        feed.reduce()
        rest = Ring(queue, rest_mine, rest_other)
    g_tokens, small = last_call(
        tokens[0], ln1_gain, w_qkv[0], queue.after(d_middle), d_queries, backs, diagonals, small
    )
    if ringed:
        queue.mark = g_tokens
        feed.reduce()
        rest.reduce()
        queue.free = True
        minor = Small(queue, small)

        def small_turn(value):
            minor.advance()
            value, minor.small = lax.optimization_barrier((value, minor.small))
            return value

        while feed.step < RING:
            feed_held = feed.reduce()
        back_chunks = gather(feed_held[:192])
        in_chunks = gather(feed_held[192:])
        g_w_back = open_call("back", places, back_chunks)
        g_w_in = open_call("inward", places, in_chunks)
        opened = [*g_w_back, *g_w_in]

        def back_turn(value):
            value, opened[0] = lax.optimization_barrier((value, opened[0]))
            return value

        def in_turn(value):
            value, opened[1] = lax.optimization_barrier((value, opened[1]))
            return value

        while rest.step < RING:
            if rest.step in SMALL_EARLY:
                rest.arrived = small_turn(rest.arrived)
            rest_held = rest.reduce()
        rest_chunks = gather(rest_held, {1: small_turn, 3: small_turn, 6: back_turn, 7: in_turn})
        opened += open_call("rest", places, rest_chunks)
        weights = [value[None] for value in opened]
        half = width // 2
        side = lax.axis_index("dp").reshape(1)
        shapes = [(1, half)] * 8 + [(1, 2 * width), (1, 3 * width)]
        outs = [jax.ShapeDtypeStruct(shape, jnp.float32) for shape in shapes]
        vectors = kernel_call(open_small_kernel, "open_small", 1, outs, side, minor.small, smem=1)
    else:
        weights, vectors = unringed_grads(
            (feed_mine, feed_other), (rest_mine, rest_other), small
        )
    g_w_back, g_w_in, g_w_qkv, g_w_out = weights
    (
        g_ln1_gain, g_ln1_bias, g_bias_q, g_bias_v, g_bias_out, g_ln2_gain, g_ln2_bias, g_bias_back, g_bias_in, g_rel_table,
    ) = vectors
    return (
        output[None], g_tokens[None], g_ln1_gain, g_ln1_bias, g_w_qkv, g_bias_q, g_bias_v, g_w_out,
        g_bias_out, g_ln2_gain, g_ln2_bias, g_w_in, g_bias_in, g_w_back, g_bias_back, g_rel_table,
    )


def solution(mesh):
    placed = (
        P("stream", ("group", "dp"), None),
        P("stream", ("group", "dp"), None),
        P(None, None, ("group", "dp"), None),
        P(None, ("group", "dp"), None),
        P(None, ("group", "dp"), None),
        P("stream", None),
        P("stream", None),
        P("stream", None, None),
        P("stream", None),
        P("stream", None),
        P("stream", None, None),
        P("stream", None),
        P("stream", None),
        P("stream", None),
        P("stream", None, None),
        P("stream", None),
        P("stream", None, None),
        P("stream", None),
        P("stream", None),
    )
    return jax.shard_map(
        on_device,
        mesh=mesh,
        in_specs=placed,
        out_specs=(
            P("stream", ("group", "dp"), None),
            P("stream", ("group", "dp"), None),
            P("stream", "dp"),
            P("stream", "dp"),
            P("stream", "dp", None),
            P("stream", "dp"),
            P("stream", "dp"),
            P("stream", "dp", None),
            P("stream", "dp"),
            P("stream", "dp"),
            P("stream", "dp"),
            P("stream", "dp", None),
            P("stream", "dp"),
            P("stream", "dp", None),
            P("stream", "dp"),
            P("stream", "dp"),
        ),
        check_vma=False,
    )
```

profile of v0, /device:TPU:0, one launch (start us, length us, event | category | flops | bytes accessed | tf_op | source)
XLA Modules:
  0.0 300.0 jit_solution(13277373727212609734)
XLA Ops:
  0.7 4.7 %first.1 = (bf16[512,768]{1,0:T(8,128)(2,1)}, bf16[2,512,256]{2,1,0:T(8,128)(2,1)}, bf16[2,512,256]{2,1,0:T(8,128)(2,1)}, bf16[2,512,256]{2,1,0:T(8,128)(2,1)}) custom-call(bf16[512,768]{1,0:T(8,128)(2,1)} %bitcast.139, f32[1,768]{1,0:T(1,128)} %gain_ref.5, f32[1,768]{1,0:T(1,128)} %shift_ref.2, bf16[768,2304]{1,0:T(8,128)(2,1)} %bitcast.134, f32[1,768]{1,0:T(1,128)} %bias_ref.2), custom_call_target="tpu_custom_call" | custom-call | flops 5000000000 | tf_op jit(solution)/shard_map/first/pallas_call | solution.py:265
  5.4 3.0 collective-permute-start
  8.4 2.0 collective-permute-start.2
  11.6 5.3 %prep.1 = (bf16[512,768]{1,0:T(8,128)(2,1)}, bf16[512,384]{1,0:T(8,128)(2,1)}, bf16[512,384]{1,0:T(8,128)(2,1)}, bf16[512,384]{1,0:T(8,128)(2,1)}, s32[1,512]{1,0:T(1,128)}, /*index=5*/bf16[36,128,128]{2,1,0:T(8,128)(2,1)}) custom-call(s32[1]{0:T(128)} %bitcast.1.stream_ref, s32[2,2,1,512]{3,2,1,0:T(1,128)} %box_ref.1, s32[2,1,512]{2,1,0:T(1,128)} %segment_ref.1, ...), custom_call_target="tpu_custom_call" | custom-call | flops 5000000000 | tf_op jit(solution)/shard_map/prep/pallas_call | solution.py:265
  16.9 4.5 %collective-permute-done.pair_ref = bf16[2,512,256]{2,1,0:T(8,128)(2,1)S(1)} collective-permute-done((bf16[2,512,256]{2,1,0:T(8,128)(2,1)}, bf16[2,512,256]{2,1,0:T(8,128)(2,1)S(1)}, u32[]{:S(2)}, u32[]{:S(2)}) %collective-permute-start) | collective-permute-done | bytes 524320 | tf_op jit(solution)/shard_map/ppermute | solution.py:576
  22.2 6.8 %attend_0.1 = (bf16[512,256]{1,0:T(8,128)(2,1)}, bf16[4,512,512]{2,1,0:T(8,128)(2,1)}) custom-call(bf16[512,768]{1,0:T(8,128)(2,1)} %get-tuple-element.93.queries_ref, bf16[2,512,256]{2,1,0:T(8,128)(2,1)} %copy-done.8, bf16[512,384]{1,0:T(8,128)(2,1)} %get-tuple-element.95.hot_ref, bf16[512,384]{1,0:T(8,128)(2,1)} %get-tuple-element.96.key_hot_ref, ...), custom_call_target="tpu_custom_call" | custom-call | flops 7000000000 | tf_op jit(solution)/shard_map/attend_0/pallas_call | solution.py:265
  29.0 3.6 %collective-permute-done.1.pair_ref = bf16[2,512,256]{2,1,0:T(8,128)(2,1)S(1)} collective-permute-done((bf16[2,512,256]{2,1,0:T(8,128)(2,1)}, bf16[2,512,256]{2,1,0:T(8,128)(2,1)S(1)}, u32[]{:S(2)}, u32[]{:S(2)}) %collective-permute-start.1) | collective-permute-done | bytes 524320 | tf_op jit(solution)/shard_map/ppermute | solution.py:576
  33.4 6.9 %attend_1.1 = (bf16[512,256]{1,0:T(8,128)(2,1)}, bf16[4,512,512]{2,1,0:T(8,128)(2,1)}) custom-call(bf16[512,768]{1,0:T(8,128)(2,1)} %get-tuple-element.93.queries_ref, bf16[2,512,256]{2,1,0:T(8,128)(2,1)} %copy-done.7, bf16[512,384]{1,0:T(8,128)(2,1)} %get-tuple-element.95.hot_ref, bf16[512,384]{1,0:T(8,128)(2,1)} %get-tuple-element.96.key_hot_ref, ...), custom_call_target="tpu_custom_call" | custom-call | flops 7000000000 | tf_op jit(solution)/shard_map/attend_1/pallas_call | solution.py:265
  40.3 2.6 collective-permute-done.2.pair_ref
  43.8 16.4 %attend_2.1 = (bf16[512,256]{1,0:T(8,128)(2,1)}, bf16[4,512,512]{2,1,0:T(8,128)(2,1)}) custom-call(bf16[512,768]{1,0:T(8,128)(2,1)} %get-tuple-element.93.queries_ref, bf16[2,512,256]{2,1,0:T(8,128)(2,1)} %copy-done.6, bf16[512,384]{1,0:T(8,128)(2,1)} %get-tuple-element.95.hot_ref, bf16[512,384]{1,0:T(8,128)(2,1)} %get-tuple-element.96.key_hot_ref, ...), custom_call_target="tpu_custom_call" | custom-call | flops 7000000000 | tf_op jit(solution)/shard_map/attend_2/pallas_call | solution.py:265
  60.1 31.7 %feed.1 = (bf16[512,768]{1,0:T(8,128)(2,1)}, f32[512,768]{1,0:T(8,128)}, bf16[512,768]{1,0:T(8,128)(2,1)}, bf16[512,768]{1,0:T(8,128)(2,1)}, bf16[8,384,768]{2,1...) custom-call(s32[16]{0:T(128)} %fusion.17.order_ref, bf16[512,768]{1,0:T(8,128)(2,1)} %bitcast.140, ...), custom_call_target="tpu_custom_call" | custom-call | flops 30000001024 | tf_op jit(solution)/shard_map/feed/pallas_call | solution.py:205
  91.9 7.7 %attend_back_0.1 = (bf16[512,256]{1,0:T(8,128)(2,1)}, bf16[2,512,256]{2,1,0:T(8,128)(2,1)}, f32[3,4,256]{2,1,0:T(4,128)}) custom-call(bf16[512,768]{1,0:T(8,128)(2,1)} %get-tuple-element.93.queries_ref, bf16[2,512,256]{2,1,0:T(8,128)(2,1)} %copy-done.8, bf16[512,384]{1,0:T(8,128)(2,1)} %get-tuple-element.111.turned_hot_ref, ...), custom_call_target="tpu_custom_call" | custom-call | flops 8000000000 | tf_op jit(solution)/shard_map/attend_back_0/pallas_call | solution.py:265
  99.6 1.7 collective-permute-start.6
  102.7 2.0 collective-permute-start.4
  104.7 7.6 %attend_back_1.1 = (bf16[512,256]{1,0:T(8,128)(2,1)}, bf16[2,512,256]{2,1,0:T(8,128)(2,1)}, f32[3,4,256]{2,1,0:T(4,128)}) custom-call(bf16[512,768]{1,0:T(8,128)(2,1)} %get-tuple-element.93.queries_ref, bf16[2,512,256]{2,1,0:T(8,128)(2,1)} %copy-done.7, bf16[512,384]{1,0:T(8,128)(2,1)} %get-tuple-element.111.turned_hot_ref, ...), custom_call_target="tpu_custom_call" | custom-call | flops 8000000000 | tf_op jit(solution)/shard_map/attend_back_1/pallas_call | solution.py:265
  114.5 1.6 collective-permute-start.5
  116.1 7.8 %attend_back_2.1 = (bf16[512,256]{1,0:T(8,128)(2,1)}, bf16[2,512,256]{2,1,0:T(8,128)(2,1)}, f32[3,4,256]{2,1,0:T(4,128)}) custom-call(bf16[512,768]{1,0:T(8,128)(2,1)} %get-tuple-element.93.queries_ref, bf16[2,512,256]{2,1,0:T(8,128)(2,1)} %copy-done.6, bf16[512,384]{1,0:T(8,128)(2,1)} %get-tuple-element.111.turned_hot_ref, ...), custom_call_target="tpu_custom_call" | custom-call | flops 8000000000 | tf_op jit(solution)/shard_map/attend_back_2/pallas_call | solution.py:265
  128.9 9.6 %collective-permute-done.9.back_2_ref = bf16[2,512,256]{2,1,0:T(8,128)(2,1)S(1)} collective-permute-done((bf16[2,512,256]{2,1,0:T(8,128)(2,1)S(1)}, bf16[2,512,256]{2,1,0:T(8,128)(2,1)S(1)}, u32[]{:S(2)}, u32[]{:S(2)}) %collective-permute-start.9) | collective-permute-done | bytes 524320 | tf_op jit(solution)/shard_map/ppermute | solution.py:576
  139.3 9.9 %weights.1 = (bf16[8,192,768]{2,1,0:T(8,128)(2,1)}, bf16[8,192,768]{2,1,0:T(8,128)(2,1)}) custom-call(s32[16]{0:T(128)} %fusion.17.order_ref, bf16[512,768]{1,0:T(8,128)(2,1)} %get-tuple-element.127.normed_ref, bf16[512,768]{1,0:T(8,128)(2,1)} %get-tuple-element.128.d_branch_ref, bf16[512,256]{1,0:T(8,128)(2,1)} %get-tuple-element.99.context_0_ref, ...), custom_call_target="tpu_custom_call" | custom-call | flops 7000000000 | tf_op jit(solution)/shard_map/weights/pallas_call | solution.py:265
  152.2 7.5 %last.1 = (bf16[512,768]{1,0:T(8,128)(2,1)}, f32[2,24,384]{2,1,0:T(8,128)}) custom-call(bf16[512,768]{1,0:T(8,128)(2,1)} %bitcast.141, f32[1,768]{1,0:T(1,128)} %gain_ref.5, bf16[768,2304]{1,0:T(8,128)(2,1)} %bitcast.136, f32[512,768]{1,0:T(8,128)} %get-tuple-element.133.d_middle_ref, bf16[512,256]{1,0:T(8,128)(2,1)} %get-tuple-element.115.d_query_0_ref, ...), custom_call_target="tpu_custom_call" | custom-call | flops 8000000000 | tf_op jit(solution)/shard_map/last/pallas_call | solution.py:265
  165.3 10.0 %collective-permute-done.12 = bf16[192,768]{1,0:T(8,128)(2,1)S(1)} collective-permute-done((bf16[192,768]{1,0:T(8,128)(2,1)S(1)}, bf16[192,768]{1,0:T(8,128)(2,1)S(1)}, u32[]{:S(2)}, u32[]{:S(2)}) %collective-permute-start.12) | collective-permute-done | bytes 294944 | tf_op jit(solution)/shard_map/ppermute | solution.py:586
  179.9 2.3 collective-permute-done.13
  183.7 8.0 %collective-permute-done.14 = bf16[192,768]{1,0:T(8,128)(2,1)S(1)} collective-permute-done((bf16[192,768]{1,0:T(8,128)(2,1)S(1)}, bf16[192,768]{1,0:T(8,128)(2,1)S(1)}, u32[]{:S(2)}, u32[]{:S(2)}) %collective-permute-start.14) | collective-permute-done | bytes 294944 | tf_op jit(solution)/shard_map/ppermute | solution.py:586
  194.7 1.6 collective-permute-start.31
  196.3 2.3 collective-permute-done.15
  200.7 8.1 %collective-permute-done.17 = bf16[192,768]{1,0:T(8,128)(2,1)S(1)} collective-permute-done((bf16[192,768]{1,0:T(8,128)(2,1)S(1)}, bf16[192,768]{1,0:T(8,128)(2,1)S(1)}, u32[]{:S(2)}, u32[]{:S(2)}) %collective-permute-start.17) | collective-permute-done | bytes 294944 | tf_op jit(solution)/shard_map/ppermute | solution.py:586
  211.1 1.6 collective-permute-start.40
  216.8 5.3 %collective-permute-done.32.refs_1_ = bf16[192,768]{1,0:T(8,128)(2,1)S(1)} collective-permute-done((bf16[192,768]{1,0:T(8,128)(2,1)S(1)}, bf16[192,768]{1,0:T(8,128)(2,1)S(1)}, u32[]{:S(2)}, u32[]{:S(2)}) %collective-permute-start.32) | collective-permute-done | bytes 294944 | tf_op jit(solution)/shard_map/ppermute | solution.py:586
  226.7 2.1 collective-permute-done.33.refs_2_
  229.9 1.6 collective-permute-start.22
  233.3 4.6 %collective-permute-done.22 = f32[2,24,384]{2,1,0:T(8,128)S(1)} collective-permute-done((f32[2,24,384]{2,1,0:T(8,128)S(1)}, f32[2,24,384]{2,1,0:T(8,128)S(1)}, u32[]{:S(2)}, u32[]{:S(2)}) %collective-permute-start.22) | collective-permute-done | bytes 73760 | tf_op jit(solution)/shard_map/ppermute | solution.py:576
  237.9 2.5 collective-permute-start.23
  241.9 2.5 collective-permute-start.43
  245.4 1.8 collective-permute-start.24
  248.6 2.3 collective-permute-start.36
  250.9 3.3 %collective-permute-start.25 = (f32[2,24,384]{2,1,0:T(8,128)S(1)}, f32[2,24,384]{2,1,0:T(8,128)S(1)}, u32[]{:S(2)}, u32[]{:S(2)}) collective-permute-start(f32[2,24,384]{2,1,0:T(8,128)S(1)} %add.163), channel_id=1, source_target_pairs={{0,8},{2,10},{4,12},{6,14},{8,0},{10,2},{12,4},{14,6},{1,9},{3,11}... | collective-permute-start | bytes 221192 | tf_op jit(solution)/shard_map/ppermute | solution.py:576
  254.3 4.6 %collective-permute-done.25 = f32[2,24,384]{2,1,0:T(8,128)S(1)} collective-permute-done((f32[2,24,384]{2,1,0:T(8,128)S(1)}, f32[2,24,384]{2,1,0:T(8,128)S(1)}, u32[]{:S(2)}, u32[]{:S(2)}) %collective-permute-start.25) | collective-permute-done | bytes 73760 | tf_op jit(solution)/shard_map/ppermute | solution.py:576
  259.6 3.0 %collective-permute-start.26 = (bf16[192,768]{1,0:T(8,128)(2,1)S(1)}, bf16[192,768]{1,0:T(8,128)(2,1)S(1)}, u32[]{:S(2)}, u32[]{:S(2)}) collective-permute-start(bf16[192,768]{1,0:T(8,128)(2,1)S(1)} %collective-permute-done.24.refs_3_), channel_id=1, source_target_pairs={{0,4},{1,3},{4,8},{5,1},{8,12},{9,5},{12,14},{13,9},{14,10},{15,13... | collective-permute-start | bytes 884744 | tf_op jit(solution)/shard_map/ppermute | solution.py:586
  263.7 3.0 collective-permute-start.45
  266.7 2.6 collective-permute-done.26.refs_4_
  269.4 3.2 %collective-permute-done.37.refs_6_ = bf16[192,768]{1,0:T(8,128)(2,1)} collective-permute-done((bf16[192,768]{1,0:T(8,128)(2,1)S(1)}, bf16[192,768]{1,0:T(8,128)(2,1)}, u32[]{:S(2)}, u32[]{:S(2)}) %collective-permute-start.37) | collective-permute-done | bytes 294944 | tf_op jit(solution)/shard_map/ppermute | solution.py:586
  273.1 2.6 collective-permute-done.45.refs_6_
  275.8 3.2 %collective-permute-done.27.refs_5_ = bf16[192,768]{1,0:T(8,128)(2,1)} collective-permute-done((bf16[192,768]{1,0:T(8,128)(2,1)S(1)}, bf16[192,768]{1,0:T(8,128)(2,1)}, u32[]{:S(2)}, u32[]{:S(2)}) %collective-permute-start.27) | collective-permute-done | bytes 294944 | tf_op jit(solution)/shard_map/ppermute | solution.py:586
  278.9 3.2 %collective-permute-done.38.refs_7_ = bf16[192,768]{1,0:T(8,128)(2,1)} collective-permute-done((bf16[192,768]{1,0:T(8,128)(2,1)}, bf16[192,768]{1,0:T(8,128)(2,1)}, u32[]{:S(2)}, u32[]{:S(2)}) %collective-permute-start.38) | collective-permute-done | bytes 294944 | tf_op jit(solution)/shard_map/ppermute | solution.py:586
  282.1 4.1 %open_back.1 = f32[1536,768]{1,0:T(8,128)} custom-call(s32[8]{0:T(128)} %and_select_fusion.place_ref, bf16[192,768]{1,0:T(8,128)(2,1)} %copy-done.2, bf16[192,768]{1,0:T(8,128)(2,1)} %copy-done.15, bf16[192,768]{1,0:T(8,128)(2,1)} %copy-done.17, bf16[192,768]{1,0:T(8,128)(2,1)} %copy-done.21, bf16[192,768]{1,0:T(8,128)(2,1)} %copy-done.24, ...), custom_call_target="tpu_custom_call" | custom-call | flops 4000000000 | tf_op jit(solution)/shard_map/open_back/pallas_call | solution.py:265
  286.3 2.0 collective-permute-done.28.refs_6_
  288.3 4.2 %open_inward.1 = f32[384,3072]{1,0:T(8,128)} custom-call(s32[8]{0:T(128)} %and_select_fusion.place_ref, bf16[192,768]{1,0:T(8,128)(2,1)} %copy-done.1, bf16[192,768]{1,0:T(8,128)(2,1)} %copy-done.13, bf16[192,768]{1,0:T(8,128)(2,1)} %copy-done.16, bf16[192,768]{1,0:T(8,128)(2,1)} %copy-done.19, bf16[192,768]{1,0:T(8,128)(2,1)} %copy-done.22, ...), custom_call_target="tpu_custom_call" | custom-call | flops 4000000000 | tf_op jit(solution)/shard_map/open_inward/pallas_call | solution.py:265
  295.7 4.1 %open_rest.1 = (f32[384,2304]{1,0:T(8,128)}, f32[384,768]{1,0:T(8,128)}) custom-call(s32[8]{0:T(128)} %and_select_fusion.place_ref, bf16[192,768]{1,0:T(8,128)(2,1)} %copy-done.3, bf16[192,768]{1,0:T(8,128)(2,1)} %copy-done.14, bf16[192,768]{1,0:T(8,128)(2,1)} %copy-done.18, bf16[192,768]{1,0:T(8,128)(2,1)} %copy-done.20, bf16[192,768]{1,0:T(8,128)(2,1)} %copy-done.23, ...), custom_call_target="tpu_custom_call" | custom-call | flops 4000000000 | tf_op jit(solution)/shard_map/open_rest/pallas_call | solution.py:265
  (141 shorter events, 56.2 us)
Async XLA Ops:
  5.4 16.0 %collective-permute-start = (bf16[2,512,256]{2,1,0:T(8,128)(2,1)}, bf16[2,512,256]{2,1,0:T(8,128)(2,1)S(1)}, u32[]{:S(2)}, u32[]{:S(2)}) collective-permute-start(bf16[2,512,256]{2,1,0:T(8,128)(2,1)} %get-tuple-element.94), channel_id=1, source_target_pairs={{0,16},{16,0},{1,17},{17,1},{2,18},{18,2},{3,19},{19,3},{4,20},{20... | collective-permute-start | bytes 1572872 | tf_op jit(solution)/shard_map/ppermute | solution.py:576
  8.4 24.2 %collective-permute-start.1 = (bf16[2,512,256]{2,1,0:T(8,128)(2,1)}, bf16[2,512,256]{2,1,0:T(8,128)(2,1)S(1)}, u32[]{:S(2)}, u32[]{:S(2)}) collective-permute-start(bf16[2,512,256]{2,1,0:T(8,128)(2,1)} %get-tuple-element.100), channel_id=1, source_target_pairs={{0,16},{16,0},{1,17},{17,1},{2,18},{18,2},{3,19},{19,3},{4,20},{20... | collective-permute-start | bytes 1572872 | tf_op jit(solution)/shard_map/ppermute | solution.py:576
  8.4 34.6 %collective-permute-start.2 = (bf16[2,512,256]{2,1,0:T(8,128)(2,1)}, bf16[2,512,256]{2,1,0:T(8,128)(2,1)S(1)}, u32[]{:S(2)}, u32[]{:S(2)}) collective-permute-start(bf16[2,512,256]{2,1,0:T(8,128)(2,1)} %get-tuple-element.103), channel_id=1, source_target_pairs={{0,16},{16,0},{1,17},{17,1},{2,18},{18,2},{3,19},{19,3},{4,20},{20... | collective-permute-start | bytes 1572872 | tf_op jit(solution)/shard_map/ppermute | solution.py:576
  91.8 9.5 %collective-permute-start.3 = (bf16[8,384,768]{2,1,0:T(8,128)(2,1)}, bf16[8,384,768]{2,1,0:T(8,128)(2,1)}, u32[]{:S(2)}, u32[]{:S(2)}) collective-permute-start(bf16[8,384,768]{2,1,0:T(8,128)(2,1)} %get-tuple-element.110), channel_id=1, source_target_pairs={{0,1},{1,0},{2,3},{3,2},{4,5},{5,4},{6,7},{7,6},{8,9},{9,8},{10,11... | collective-permute-start | bytes 14155784 | tf_op jit(solution)/shard_map/ppermute | solution.py:662
  99.6 16.5 %collective-permute-start.6 = (bf16[2,512,256]{2,1,0:T(8,128)(2,1)}, bf16[2,512,256]{2,1,0:T(8,128)(2,1)S(1)}, u32[]{:S(2)}, u32[]{:S(2)}) collective-permute-start(bf16[2,512,256]{2,1,0:T(8,128)(2,1)} %get-tuple-element.122), channel_id=1, source_target_pairs={{0,16},{16,0},{1,17},{17,1},{2,18},{18,2},{3,19},{19,3},{4,20},{20... | collective-permute-start | bytes 1572872 | tf_op jit(solution)/shard_map/ppermute | solution.py:576
  102.7 10.3 %collective-permute-start.4 = (bf16[384,768]{1,0:T(8,128)(2,1)S(1)}, bf16[384,768]{1,0:T(8,128)(2,1)S(1)}, u32[]{:S(2)}, u32[]{:S(2)}) collective-permute-start(bf16[384,768]{1,0:T(8,128)(2,1)S(1)} %fusion.7), channel_id=1, source_target_pairs={{0,4},{1,3},{4,8},{5,1},{8,12},{9,5},{12,14},{13,9},{14,10},{15,13... | collective-permute-start | bytes 1769480 | tf_op jit(solution)/shard_map/ppermute | solution.py:586
  112.4 16.5 %collective-permute-start.8 = (bf16[2,512,256]{2,1,0:T(8,128)(2,1)}, bf16[2,512,256]{2,1,0:T(8,128)(2,1)S(1)}, u32[]{:S(2)}, u32[]{:S(2)}) collective-permute-start(bf16[2,512,256]{2,1,0:T(8,128)(2,1)} %get-tuple-element.126), channel_id=1, source_target_pairs={{0,16},{16,0},{1,17},{17,1},{2,18},{18,2},{3,19},{19,3},{4,20},{20... | collective-permute-start | bytes 1572872 | tf_op jit(solution)/shard_map/ppermute | solution.py:576
  114.5 9.9 %collective-permute-start.5 = (bf16[384,768]{1,0:T(8,128)(2,1)S(1)}, bf16[384,768]{1,0:T(8,128)(2,1)S(1)}, u32[]{:S(2)}, u32[]{:S(2)}) collective-permute-start(bf16[384,768]{1,0:T(8,128)(2,1)S(1)} %fusion.6), channel_id=1, source_target_pairs={{0,4},{1,3},{4,8},{5,1},{8,12},{9,5},{12,14},{13,9},{14,10},{15,13... | collective-permute-start | bytes 1769480 | tf_op jit(solution)/shard_map/ppermute | solution.py:586
  125.9 12.6 %collective-permute-start.9 = (bf16[2,512,256]{2,1,0:T(8,128)(2,1)S(1)}, bf16[2,512,256]{2,1,0:T(8,128)(2,1)S(1)}, u32[]{:S(2)}, u32[]{:S(2)}) collective-permute-start(bf16[2,512,256]{2,1,0:T(8,128)(2,1)S(1)} %copy-done.12), channel_id=1, source_target_pairs={{0,16},{16,0},{1,17},{17,1},{2,18},{18,2},{3,19},{19,3},{4,20},{20... | collective-permute-start | bytes 1572872 | tf_op jit(solution)/shard_map/ppermute | solution.py:576
  127.3 21.9 %collective-permute-start.7 = (bf16[384,768]{1,0:T(8,128)(2,1)S(1)}, bf16[384,768]{1,0:T(8,128)(2,1)S(1)}, u32[]{:S(2)}, u32[]{:S(2)}) collective-permute-start(bf16[384,768]{1,0:T(8,128)(2,1)S(1)} %fusion.5), channel_id=1, source_target_pairs={{0,4},{1,3},{4,8},{5,1},{8,12},{9,5},{12,14},{13,9},{14,10},{15,13... | collective-permute-start | bytes 1769480 | tf_op jit(solution)/shard_map/ppermute | solution.py:586
  150.7 12.9 %collective-permute-start.10 = (bf16[8,192,768]{2,1,0:T(8,128)(2,1)}, bf16[8,192,768]{2,1,0:T(8,128)(2,1)S(1)}, u32[]{:S(2)}, u32[]{:S(2)}) collective-permute-start(bf16[8,192,768]{2,1,0:T(8,128)(2,1)} %get-tuple-element.140), channel_id=1, source_target_pairs={{0,1},{1,0},{2,3},{3,2},{4,5},{5,4},{6,7},{7,6},{8,9},{9,8},{10,11... | collective-permute-start | bytes 7077896 | tf_op jit(solution)/shard_map/ppermute | solution.py:662
  150.8 9.9 %collective-permute-start.11 = (bf16[384,768]{1,0:T(8,128)(2,1)S(1)}, bf16[384,768]{1,0:T(8,128)(2,1)S(1)}, u32[]{:S(2)}, u32[]{:S(2)}) collective-permute-start(bf16[384,768]{1,0:T(8,128)(2,1)S(1)} %fusion.4), channel_id=1, source_target_pairs={{0,4},{1,3},{4,8},{5,1},{8,12},{9,5},{12,14},{13,9},{14,10},{15,13... | collective-permute-start | bytes 1769480 | tf_op jit(solution)/shard_map/ppermute | solution.py:586
  162.2 14.6 %collective-permute-start.29 = (bf16[384,768]{1,0:T(8,128)(2,1)S(1)}, bf16[384,768]{1,0:T(8,128)(2,1)S(1)}, u32[]{:S(2)}, u32[]{:S(2)}) collective-permute-start(bf16[384,768]{1,0:T(8,128)(2,1)S(1)} %fusion.3), channel_id=1, source_target_pairs={{0,4},{1,3},{4,8},{5,1},{8,12},{9,5},{12,14},{13,9},{14,10},{15,13... | collective-permute-start | bytes 1769480 | tf_op jit(solution)/shard_map/ppermute | solution.py:586
  163.7 11.6 %collective-permute-start.12 = (bf16[192,768]{1,0:T(8,128)(2,1)S(1)}, bf16[192,768]{1,0:T(8,128)(2,1)S(1)}, u32[]{:S(2)}, u32[]{:S(2)}) collective-permute-start(bf16[192,768]{1,0:T(8,128)(2,1)S(1)} %fusion.15), channel_id=1, source_target_pairs={{0,4},{1,3},{4,8},{5,1},{8,12},{9,5},{12,14},{13,9},{14,10},{15,13... | collective-permute-start | bytes 884744 | tf_op jit(solution)/shard_map/ppermute | solution.py:586
  175.4 6.8 %collective-permute-start.13 = (bf16[192,768]{1,0:T(8,128)(2,1)S(1)}, bf16[192,768]{1,0:T(8,128)(2,1)S(1)}, u32[]{:S(2)}, u32[]{:S(2)}) collective-permute-start(bf16[192,768]{1,0:T(8,128)(2,1)S(1)} %fusion.14), channel_id=1, source_target_pairs={{0,4},{1,3},{4,8},{5,1},{8,12},{9,5},{12,14},{13,9},{14,10},{15,13... | collective-permute-start | bytes 884744 | tf_op jit(solution)/shard_map/ppermute | solution.py:586
  178.3 14.9 %collective-permute-start.30 = (bf16[384,768]{1,0:T(8,128)(2,1)S(1)}, bf16[384,768]{1,0:T(8,128)(2,1)S(1)}, u32[]{:S(2)}, u32[]{:S(2)}) collective-permute-start(bf16[384,768]{1,0:T(8,128)(2,1)S(1)} %fusion.2), channel_id=1, source_target_pairs={{0,4},{1,3},{4,8},{5,1},{8,12},{9,5},{12,14},{13,9},{14,10},{15,13... | collective-permute-start | bytes 1769480 | tf_op jit(solution)/shard_map/ppermute | solution.py:586
  182.3 9.4 %collective-permute-start.14 = (bf16[192,768]{1,0:T(8,128)(2,1)S(1)}, bf16[192,768]{1,0:T(8,128)(2,1)S(1)}, u32[]{:S(2)}, u32[]{:S(2)}) collective-permute-start(bf16[192,768]{1,0:T(8,128)(2,1)S(1)} %fusion.13), channel_id=1, source_target_pairs={{0,4},{1,3},{4,8},{5,1},{8,12},{9,5},{12,14},{13,9},{14,10},{15,13... | collective-permute-start | bytes 884744 | tf_op jit(solution)/shard_map/ppermute | solution.py:586
  183.7 9.5 %collective-permute-start.16 = (f32[2,24,384]{2,1,0:T(8,128)S(1)}, f32[2,24,384]{2,1,0:T(8,128)S(1)}, u32[]{:S(2)}, u32[]{:S(2)}) collective-permute-start(f32[2,24,384]{2,1,0:T(8,128)S(1)} %copy-done.4), channel_id=1, source_target_pairs={{0,1},{1,0},{2,3},{3,2},{4,5},{5,4},{6,7},{7,6},{8,9},{9,8},{10,11... | collective-permute-start | bytes 221192 | tf_op jit(solution)/shard_map/ppermute | solution.py:576
  191.8 6.8 %collective-permute-start.15 = (bf16[192,768]{1,0:T(8,128)(2,1)S(1)}, bf16[192,768]{1,0:T(8,128)(2,1)S(1)}, u32[]{:S(2)}, u32[]{:S(2)}) collective-permute-start(bf16[192,768]{1,0:T(8,128)(2,1)S(1)} %fusion.12), channel_id=1, source_target_pairs={{0,4},{1,3},{4,8},{5,1},{8,12},{9,5},{12,14},{13,9},{14,10},{15,13... | collective-permute-start | bytes 884744 | tf_op jit(solution)/shard_map/ppermute | solution.py:586
  194.7 14.9 %collective-permute-start.31 = (bf16[384,768]{1,0:T(8,128)(2,1)S(1)}, bf16[384,768]{1,0:T(8,128)(2,1)S(1)}, u32[]{:S(2)}, u32[]{:S(2)}) collective-permute-start(bf16[384,768]{1,0:T(8,128)(2,1)S(1)} %fusion.1), channel_id=1, source_target_pairs={{0,4},{1,3},{4,8},{5,1},{8,12},{9,5},{12,14},{13,9},{14,10},{15,13... | collective-permute-start | bytes 1769480 | tf_op jit(solution)/shard_map/ppermute | solution.py:586
  198.7 10.2 %collective-permute-start.17 = (bf16[192,768]{1,0:T(8,128)(2,1)S(1)}, bf16[192,768]{1,0:T(8,128)(2,1)S(1)}, u32[]{:S(2)}, u32[]{:S(2)}) collective-permute-start(bf16[192,768]{1,0:T(8,128)(2,1)S(1)} %fusion.11), channel_id=1, source_target_pairs={{0,4},{1,3},{4,8},{5,1},{8,12},{9,5},{12,14},{13,9},{14,10},{15,13... | collective-permute-start | bytes 884744 | tf_op jit(solution)/shard_map/ppermute | solution.py:586
  200.1 14.2 %collective-permute-start.19 = (f32[2,24,384]{2,1,0:T(8,128)S(1)}, f32[2,24,384]{2,1,0:T(8,128)S(1)}, u32[]{:S(2)}, u32[]{:S(2)}) collective-permute-start(f32[2,24,384]{2,1,0:T(8,128)S(1)} %add.153), channel_id=1, source_target_pairs={{0,2},{2,0},{4,6},{6,4},{8,10},{10,8},{12,14},{14,12},{1,3},{3,1},... | collective-permute-start | bytes 221192 | tf_op jit(solution)/shard_map/ppermute | solution.py:576
  208.9 6.8 %collective-permute-start.18 = (bf16[192,768]{1,0:T(8,128)(2,1)S(1)}, bf16[192,768]{1,0:T(8,128)(2,1)S(1)}, u32[]{:S(2)}, u32[]{:S(2)}) collective-permute-start(bf16[192,768]{1,0:T(8,128)(2,1)S(1)} %fusion.10), channel_id=1, source_target_pairs={{0,4},{1,3},{4,8},{5,1},{8,12},{9,5},{12,14},{13,9},{14,10},{15,13... | collective-permute-start | bytes 884744 | tf_op jit(solution)/shard_map/ppermute | solution.py:586
  211.1 75.1 %copy-start.1 = (bf16[192,768]{1,0:T(8,128)(2,1)}, bf16[192,768]{1,0:T(8,128)(2,1)S(1)}, u32[]{:S(2)}) copy-start(bf16[192,768]{1,0:T(8,128)(2,1)S(1)} %get-tuple-element.168.refs_0_) | copy-start | bytes 884740
  211.1 11.5 %collective-permute-start.40 = (bf16[192,768]{1,0:T(8,128)(2,1)S(1)}, bf16[192,768]{1,0:T(8,128)(2,1)S(1)}, u32[]{:S(2)}, u32[]{:S(2)}) collective-permute-start(bf16[192,768]{1,0:T(8,128)(2,1)S(1)} %get-tuple-element.168.refs_0_), channel_id=1, source_target_pairs={{0,4},{1,3},{4,8},{5,1},{8,12},{9,5},{12,14},{13,9},{14,10},{15,13... | collective-permute-start | bytes 884744 | tf_op jit(solution)/shard_map/ppermute | solution.py:586
  212.7 9.3 %collective-permute-start.32 = (bf16[192,768]{1,0:T(8,128)(2,1)S(1)}, bf16[192,768]{1,0:T(8,128)(2,1)S(1)}, u32[]{:S(2)}, u32[]{:S(2)}) collective-permute-start(bf16[192,768]{1,0:T(8,128)(2,1)S(1)} %get-tuple-element.169.refs_0_), channel_id=1, source_target_pairs={{0,4},{1,3},{4,8},{5,1},{8,12},{9,5},{12,14},{13,9},{14,10},{15,13... | collective-permute-start | bytes 884744 | tf_op jit(solution)/shard_map/ppermute | solution.py:586
  215.8 9.4 %collective-permute-start.20 = (bf16[192,768]{1,0:T(8,128)(2,1)S(1)}, bf16[192,768]{1,0:T(8,128)(2,1)S(1)}, u32[]{:S(2)}, u32[]{:S(2)}) collective-permute-start(bf16[192,768]{1,0:T(8,128)(2,1)S(1)} %fusion.9), channel_id=1, source_target_pairs={{0,4},{1,3},{4,8},{5,1},{8,12},{9,5},{12,14},{13,9},{14,10},{15,13... | collective-permute-start | bytes 884744 | tf_op jit(solution)/shard_map/ppermute | solution.py:586
  222.0 6.7 %collective-permute-start.33 = (bf16[192,768]{1,0:T(8,128)(2,1)S(1)}, bf16[192,768]{1,0:T(8,128)(2,1)S(1)}, u32[]{:S(2)}, u32[]{:S(2)}) collective-permute-start(bf16[192,768]{1,0:T(8,128)(2,1)S(1)} %collective-permute-done.32.refs_1_), channel_id=1, source_target_pairs={{0,4},{1,3},{4,8},{5,1},{8,12},{9,5},{12,14},{13,9},{14,10},{15,13... | collective-permute-start | bytes 884744 | tf_op jit(solution)/shard_map/ppermute | solution.py:586
  222.6 9.3 %collective-permute-start.41 = (bf16[192,768]{1,0:T(8,128)(2,1)S(1)}, bf16[192,768]{1,0:T(8,128)(2,1)S(1)}, u32[]{:S(2)}, u32[]{:S(2)}) collective-permute-start(bf16[192,768]{1,0:T(8,128)(2,1)S(1)} %collective-permute-done.40.refs_1_), channel_id=1, source_target_pairs={{0,4},{1,3},{4,8},{5,1},{8,12},{9,5},{12,14},{13,9},{14,10},{15,13... | collective-permute-start | bytes 884744 | tf_op jit(solution)/shard_map/ppermute | solution.py:586
  225.3 12.6 %collective-permute-start.21 = (bf16[192,768]{1,0:T(8,128)(2,1)S(1)}, bf16[192,768]{1,0:T(8,128)(2,1)S(1)}, u32[]{:S(2)}, u32[]{:S(2)}) collective-permute-start(bf16[192,768]{1,0:T(8,128)(2,1)S(1)} %fusion.8.refs_0_), channel_id=1, source_target_pairs={{0,4},{1,3},{4,8},{5,1},{8,12},{9,5},{12,14},{13,9},{14,10},{15,13... | collective-permute-start | bytes 884744 | tf_op jit(solution)/shard_map/ppermute | solution.py:586
  228.8 11.7 %collective-permute-start.34 = (bf16[192,768]{1,0:T(8,128)(2,1)S(1)}, bf16[192,768]{1,0:T(8,128)(2,1)S(1)}, u32[]{:S(2)}, u32[]{:S(2)}) collective-permute-start(bf16[192,768]{1,0:T(8,128)(2,1)S(1)} %collective-permute-done.33.refs_2_), channel_id=1, source_target_pairs={{0,4},{1,3},{4,8},{5,1},{8,12},{9,5},{12,14},{13,9},{14,10},{15,13... | collective-permute-start | bytes 884744 | tf_op jit(solution)/shard_map/ppermute | solution.py:586
  229.9 8.0 %collective-permute-start.22 = (f32[2,24,384]{2,1,0:T(8,128)S(1)}, f32[2,24,384]{2,1,0:T(8,128)S(1)}, u32[]{:S(2)}, u32[]{:S(2)}) collective-permute-start(f32[2,24,384]{2,1,0:T(8,128)S(1)} %add.158), channel_id=1, source_target_pairs={{0,4},{2,6},{4,0},{6,2},{8,12},{10,14},{12,8},{14,10},{1,5},{3,7},... | collective-permute-start | bytes 221192 | tf_op jit(solution)/shard_map/ppermute | solution.py:576
  231.9 9.9 %collective-permute-start.42 = (bf16[192,768]{1,0:T(8,128)(2,1)S(1)}, bf16[192,768]{1,0:T(8,128)(2,1)S(1)}, u32[]{:S(2)}, u32[]{:S(2)}) collective-permute-start(bf16[192,768]{1,0:T(8,128)(2,1)S(1)} %collective-permute-done.41.refs_2_), channel_id=1, source_target_pairs={{0,4},{1,3},{4,8},{5,1},{8,12},{9,5},{12,14},{13,9},{14,10},{15,13... | collective-permute-start | bytes 884744 | tf_op jit(solution)/shard_map/ppermute | solution.py:586
  237.9 7.5 %collective-permute-start.23 = (bf16[192,768]{1,0:T(8,128)(2,1)S(1)}, bf16[192,768]{1,0:T(8,128)(2,1)S(1)}, u32[]{:S(2)}, u32[]{:S(2)}) collective-permute-start(bf16[192,768]{1,0:T(8,128)(2,1)S(1)} %collective-permute-done.21.refs_1_), channel_id=1, source_target_pairs={{0,4},{1,3},{4,8},{5,1},{8,12},{9,5},{12,14},{13,9},{14,10},{15,13... | collective-permute-start | bytes 884744 | tf_op jit(solution)/shard_map/ppermute | solution.py:586
  240.5 8.1 %collective-permute-start.35 = (bf16[192,768]{1,0:T(8,128)(2,1)S(1)}, bf16[192,768]{1,0:T(8,128)(2,1)S(1)}, u32[]{:S(2)}, u32[]{:S(2)}) collective-permute-start(bf16[192,768]{1,0:T(8,128)(2,1)S(1)} %collective-permute-done.34.refs_3_), channel_id=1, source_target_pairs={{0,4},{1,3},{4,8},{5,1},{8,12},{9,5},{12,14},{13,9},{14,10},{15,13... | collective-permute-start | bytes 884744 | tf_op jit(solution)/shard_map/ppermute | solution.py:586
  241.9 12.3 %collective-permute-start.43 = (bf16[192,768]{1,0:T(8,128)(2,1)S(1)}, bf16[192,768]{1,0:T(8,128)(2,1)S(1)}, u32[]{:S(2)}, u32[]{:S(2)}) collective-permute-start(bf16[192,768]{1,0:T(8,128)(2,1)S(1)} %collective-permute-done.42.refs_3_), channel_id=1, source_target_pairs={{0,4},{1,3},{4,8},{5,1},{8,12},{9,5},{12,14},{13,9},{14,10},{15,13... | collective-permute-start | bytes 884744 | tf_op jit(solution)/shard_map/ppermute | solution.py:586
  245.4 14.1 %collective-permute-start.24 = (bf16[192,768]{1,0:T(8,128)(2,1)S(1)}, bf16[192,768]{1,0:T(8,128)(2,1)S(1)}, u32[]{:S(2)}, u32[]{:S(2)}) collective-permute-start(bf16[192,768]{1,0:T(8,128)(2,1)S(1)} %collective-permute-done.23.refs_2_), channel_id=1, source_target_pairs={{0,4},{1,3},{4,8},{5,1},{8,12},{9,5},{12,14},{13,9},{14,10},{15,13... | collective-permute-start | bytes 884744 | tf_op jit(solution)/shard_map/ppermute | solution.py:586
  248.6 14.0 %collective-permute-start.36 = (bf16[192,768]{1,0:T(8,128)(2,1)S(1)}, bf16[192,768]{1,0:T(8,128)(2,1)S(1)}, u32[]{:S(2)}, u32[]{:S(2)}) collective-permute-start(bf16[192,768]{1,0:T(8,128)(2,1)S(1)} %collective-permute-done.35.refs_4_), channel_id=1, source_target_pairs={{0,4},{1,3},{4,8},{5,1},{8,12},{9,5},{12,14},{13,9},{14,10},{15,13... | collective-permute-start | bytes 884744 | tf_op jit(solution)/shard_map/ppermute | solution.py:586
  250.9 8.1 %collective-permute-start.25 = (f32[2,24,384]{2,1,0:T(8,128)S(1)}, f32[2,24,384]{2,1,0:T(8,128)S(1)}, u32[]{:S(2)}, u32[]{:S(2)}) collective-permute-start(f32[2,24,384]{2,1,0:T(8,128)S(1)} %add.163), channel_id=1, source_target_pairs={{0,8},{2,10},{4,12},{6,14},{8,0},{10,2},{12,4},{14,6},{1,9},{3,11}... | collective-permute-start | bytes 221192 | tf_op jit(solution)/shard_map/ppermute | solution.py:576
  254.2 9.6 %collective-permute-start.44 = (bf16[192,768]{1,0:T(8,128)(2,1)S(1)}, bf16[192,768]{1,0:T(8,128)(2,1)}, u32[]{:S(2)}, u32[]{:S(2)}) collective-permute-start(bf16[192,768]{1,0:T(8,128)(2,1)S(1)} %collective-permute-done.43.refs_4_), channel_id=1, source_target_pairs={{0,4},{1,3},{4,8},{5,1},{8,12},{9,5},{12,14},{13,9},{14,10},{15,13... | collective-permute-start | bytes 884744 | tf_op jit(solution)/shard_map/ppermute | solution.py:586
  259.6 9.8 %collective-permute-start.26 = (bf16[192,768]{1,0:T(8,128)(2,1)S(1)}, bf16[192,768]{1,0:T(8,128)(2,1)S(1)}, u32[]{:S(2)}, u32[]{:S(2)}) collective-permute-start(bf16[192,768]{1,0:T(8,128)(2,1)S(1)} %collective-permute-done.24.refs_3_), channel_id=1, source_target_pairs={{0,4},{1,3},{4,8},{5,1},{8,12},{9,5},{12,14},{13,9},{14,10},{15,13... | collective-permute-start | bytes 884744 | tf_op jit(solution)/shard_map/ppermute | solution.py:586
  262.6 10.0 %collective-permute-start.37 = (bf16[192,768]{1,0:T(8,128)(2,1)S(1)}, bf16[192,768]{1,0:T(8,128)(2,1)}, u32[]{:S(2)}, u32[]{:S(2)}) collective-permute-start(bf16[192,768]{1,0:T(8,128)(2,1)S(1)} %collective-permute-done.36.refs_5_), channel_id=1, source_target_pairs={{0,4},{1,3},{4,8},{5,1},{8,12},{9,5},{12,14},{13,9},{14,10},{15,13... | collective-permute-start | bytes 884744 | tf_op jit(solution)/shard_map/ppermute | solution.py:586
  263.7 12.0 %collective-permute-start.45 = (bf16[192,768]{1,0:T(8,128)(2,1)}, bf16[192,768]{1,0:T(8,128)(2,1)}, u32[]{:S(2)}, u32[]{:S(2)}) collective-permute-start(bf16[192,768]{1,0:T(8,128)(2,1)} %collective-permute-done.44.refs_5_), channel_id=1, source_target_pairs={{0,4},{1,3},{4,8},{5,1},{8,12},{9,5},{12,14},{13,9},{14,10},{15,13... | collective-permute-start | bytes 884744 | tf_op jit(solution)/shard_map/ppermute | solution.py:586
  269.3 9.6 %collective-permute-start.27 = (bf16[192,768]{1,0:T(8,128)(2,1)S(1)}, bf16[192,768]{1,0:T(8,128)(2,1)}, u32[]{:S(2)}, u32[]{:S(2)}) collective-permute-start(bf16[192,768]{1,0:T(8,128)(2,1)S(1)} %collective-permute-done.26.refs_4_), channel_id=1, source_target_pairs={{0,4},{1,3},{4,8},{5,1},{8,12},{9,5},{12,14},{13,9},{14,10},{15,13... | collective-permute-start | bytes 884744 | tf_op jit(solution)/shard_map/ppermute | solution.py:586
  272.6 9.5 %collective-permute-start.38 = (bf16[192,768]{1,0:T(8,128)(2,1)}, bf16[192,768]{1,0:T(8,128)(2,1)}, u32[]{:S(2)}, u32[]{:S(2)}) collective-permute-start(bf16[192,768]{1,0:T(8,128)(2,1)} %collective-permute-done.37.refs_6_), channel_id=1, source_target_pairs={{0,4},{1,3},{4,8},{5,1},{8,12},{9,5},{12,14},{13,9},{14,10},{15,13... | collective-permute-start | bytes 884744 | tf_op jit(solution)/shard_map/ppermute | solution.py:586
  275.8 12.5 %collective-permute-start.46 = (bf16[192,768]{1,0:T(8,128)(2,1)}, bf16[192,768]{1,0:T(8,128)(2,1)}, u32[]{:S(2)}, u32[]{:S(2)}) collective-permute-start(bf16[192,768]{1,0:T(8,128)(2,1)} %collective-permute-done.45.refs_6_), channel_id=1, source_target_pairs={{0,4},{1,3},{4,8},{5,1},{8,12},{9,5},{12,14},{13,9},{14,10},{15,13... | collective-permute-start | bytes 884744 | tf_op jit(solution)/shard_map/ppermute | solution.py:586
  278.9 9.4 %collective-permute-start.28 = (bf16[192,768]{1,0:T(8,128)(2,1)}, bf16[192,768]{1,0:T(8,128)(2,1)S(1)}, u32[]{:S(2)}, u32[]{:S(2)}) collective-permute-start(bf16[192,768]{1,0:T(8,128)(2,1)} %collective-permute-done.27.refs_5_), channel_id=1, source_target_pairs={{0,4},{1,3},{4,8},{5,1},{8,12},{9,5},{12,14},{13,9},{14,10},{15,13... | collective-permute-start | bytes 884744 | tf_op jit(solution)/shard_map/ppermute | solution.py:586
  288.3 6.7 %collective-permute-start.39 = (bf16[192,768]{1,0:T(8,128)(2,1)S(1)}, bf16[192,768]{1,0:T(8,128)(2,1)S(1)}, u32[]{:S(2)}, u32[]{:S(2)}) collective-permute-start(bf16[192,768]{1,0:T(8,128)(2,1)S(1)} %collective-permute-done.28.refs_6_), channel_id=1, source_target_pairs={{0,4},{1,3},{4,8},{5,1},{8,12},{9,5},{12,14},{13,9},{14,10},{15,13... | collective-permute-start | bytes 884744 | tf_op jit(solution)/shard_map/ppermute | solution.py:586
  (27 other events, 634.6 us)
where the time goes:
time: 304 us; the launch traced here: 300 us
  Pallas kernels  126 us (41%)
  waiting for transfers between devices  92.4 us (30%)
  starting transfers between devices  61.4 us (20%)
  other arithmetic  14.8 us (5%)
  local copies, waits for them, and re-layouts  4.05 us (1%)
    pallas_call x14, Pallas kernels, kernel_call(): pl.pallas_call(kernel, out_shape=tuple(outs), in_specs=specs, out_specs=t...  94.5 us
    ppermute x35, waiting for transfers between devices, ring_send(): return lax.ppermute(chunk, ('group', 'dp'), pairs)  62.8 us
    ppermute x35, starting transfers between devices, ring_send(): return lax.ppermute(chunk, ('group', 'dp'), pairs)  46.9 us
    pallas_call x1, Pallas kernels, feed_call(): pl.pallas_call(feed_kernel, out_shape=(wide(bf16), wide(f32), wide(bf16),...  31.7 us
    ppermute x10, waiting for transfers between devices, partner_2(): lax.ppermute(shard, axis, [(i, i ^ 1 << distance) for i in range(lax.axis...  29.6 us
    ppermute x10, starting transfers between devices, partner_2(): lax.ppermute(shard, axis, [(i, i ^ 1 << distance) for i in range(lax.axis...  14.4 us
    convert_element_type x16, other arithmetic, add_low(): sum((term.astype(jnp.float32) for term in terms)).astype(jnp.bfloat16)  12.4 us
  transfers between devices with their start and end apart: 47, of which 28 were waited for; matrix products, arithmetic and copies ran while one was open for 4% of the time, Pallas kernels for 23%

commit v1 on v0

--- a/solution.py
+++ b/solution.py
@@ -338,9 +338,9 @@
                   context_ref, probs_ref, left_ref, right_ref, scores_ref):
     rows = queries_ref.shape[0]
     part = pair_ref.shape[2]
-    for slab in range(part // 128):
-        lanes = slice(slab * 128, slab * 128 + 128)
-        wide = slice(group * part + slab * 128, group * part + slab * 128 + 128)
+    def slab_step(slab, carry):
+        lanes = pl.ds(pl.multiple_of(slab * 128, 128), 128)
+        wide = pl.ds(pl.multiple_of(group * part + slab * 128, 128), 128)
         right_ref[slab, :, :128] = pair_ref[0, :, lanes]
         right_ref[slab, :, 128:] = key_hot_ref[...]
         halves = []
@@ -363,6 +363,9 @@
             strips(rows, soft)
             halves.append(half_of(dot_plain(probs_ref[head], pair_ref[1, :, lanes]), odd))
         context_ref[:, lanes] = (halves[0] + halves[1]).astype(jnp.bfloat16)
+        return carry
+
+    lax.fori_loop(0, part // 128, slab_step, 0)
 
 
 def attend_call(group, queries, pair, hot, key_hot, live, tiles):
@@ -386,9 +389,9 @@
                        d_queries_ref, d_pair_ref, diagonal_ref, right_ref, slope_ref, d_scores_ref):
     rows = queries_ref.shape[0]
     part = pair_ref.shape[2]
-    for slab in range(part // 128):
-        lanes = slice(slab * 128, slab * 128 + 128)
-        wide = slice(group * part + slab * 128, group * part + slab * 128 + 128)
+    def slab_step(slab, carry):
+        lanes = pl.ds(pl.multiple_of(slab * 128, 128), 128)
+        wide = pl.ds(pl.multiple_of(group * part + slab * 128, 128), 128)
         right_ref[slab, :, :128] = pair_ref[0, :, lanes]
         right_ref[slab, :, 128:] = key_hot_ref[...]
         d_query = d_key = d_value = 0.0
@@ -415,10 +418,13 @@
                 tile = dot_across(turned_hot_ref[:, cut], spread[:, cut])
                 padded = jnp.concatenate([tile, jnp.zeros_like(tile)], axis=1)
                 rolled = pltpu.roll(padded, 0, 1, stride=1, stride_axis=0)
-                diagonal_ref[axis, head : head + 1, :] = jnp.sum(rolled, axis=0, keepdims=True)
+                diagonal_ref[axis, pl.ds(head, 1), :] = jnp.sum(rolled, axis=0, keepdims=True)
         d_queries_ref[:, lanes] = (d_query * 0.125).astype(jnp.bfloat16)
         d_pair_ref[0, :, lanes] = (d_key * 0.125).astype(jnp.bfloat16)
         d_pair_ref[1, :, lanes] = d_value.astype(jnp.bfloat16)
+        return carry
+
+    lax.fori_loop(0, part // 128, slab_step, 0)
 
 
 def attend_back_call(group, queries, pair, turned_hot, key_hot, probs, d_context):
@@ -442,7 +448,7 @@
 def weights_kernel(
     order_ref, normed_ref, d_branch_ref, context_0_ref, context_1_ref, context_2_ref,
     d_query_0_ref, d_query_1_ref, d_query_2_ref, back_0_ref, back_1_ref, back_2_ref,
-    mine_ref, other_ref, joined_ref,
+    mine_ref, other_ref, joined_ref, left_ref,
 ):
     part = context_0_ref.shape[1]
     queries = (d_query_0_ref, d_query_1_ref, d_query_2_ref)
@@ -454,30 +460,32 @@
         joined_ref[1, :, lanes] = backs[group][0]
         joined_ref[2, :, lanes] = backs[group][1]
         joined_ref[3, :, lanes] = contexts[group][...]
-    for block in range(4):
-        if block < 3:
-            value = dot_across(normed_ref[...], joined_ref[block]).astype(jnp.bfloat16)
-        else:
-            value = dot_across(joined_ref[3], d_branch_ref[...]).astype(jnp.bfloat16)
+    left_ref[0] = normed_ref[...]
+    left_ref[1] = joined_ref[3]
+    joined_ref[3] = d_branch_ref[...]
+
+    def block_step(block, carry):
+        value = dot_across(left_ref[block // 3], joined_ref[block]).astype(jnp.bfloat16)
+        rows = pl.ds(pl.multiple_of(block * 48, 16), 48)
         for piece in range(16):
-            place_chunk(
-                order_ref[piece], mine_ref, other_ref, value[piece * 48 : piece * 48 + 48],
-                slice(block * 48, block * 48 + 48),
-            )
+            place_chunk(order_ref[piece], mine_ref, other_ref, value[piece * 48 : piece * 48 + 48], rows)
+        return carry
+
+    lax.fori_loop(0, 4, block_step, 0)
 
 
 def weights_call(order, normed, d_branch, contexts, d_queries, backs):
     rows, width = normed.shape
     ring = jax.ShapeDtypeStruct((RING, 192, width), jnp.bfloat16)
-    scratch = [pltpu.VMEM((4, rows, width), jnp.bfloat16)]
+    scratch = [pltpu.VMEM((4, rows, width), jnp.bfloat16), pltpu.VMEM((2, rows, width), jnp.bfloat16)]
     return kernel_call(weights_kernel, "weights", 7, [ring, ring], order, normed, d_branch,
                        *contexts, *d_queries, *backs, scratch=scratch, smem=1)
 
 
 def last_kernel(
-    tokens_ref, gain_ref, w_ref, d_middle_ref, d_query_0_ref, d_query_1_ref, d_query_2_ref,
+    side_ref, tokens_ref, gain_ref, w_ref, d_middle_ref, d_query_0_ref, d_query_1_ref, d_query_2_ref,
     back_0_ref, back_1_ref, back_2_ref, diagonal_0_ref, diagonal_1_ref, diagonal_2_ref, start_ref,
-    g_tokens_ref, small_ref, d_normed_ref, sums_ref,
+    g_tokens_ref, mine_ref, other_ref, small_ref, d_normed_ref, sums_ref,
 ):
     rows, width = tokens_ref.shape
     part = width // GROUPS
@@ -528,14 +536,19 @@
                 side, place = divmod(index, 18)
                 row, lane = divmod(place, 3)
                 small_ref[side, 12 + row : 13 + row, lane * BINS : lane * BINS + BINS] = table[head : head + 1, :]
-
-
-def last_call(tokens, gain, w_qkv, d_middle, d_queries, backs, diagonals, start):
+    for out_ref, side in ((mine_ref, side_ref[0]), (other_ref, 1 - side_ref[0])):
+        out_ref[...] = jnp.zeros_like(out_ref)
+        out_ref[:12, :384] = small_ref[side, :12, :]
+        out_ref[:12, 384:] = small_ref[side, 12:, :]
+
+
+def last_call(side, tokens, gain, w_qkv, d_middle, d_queries, backs, diagonals, start):
     rows, width = tokens.shape
-    outs = [jax.ShapeDtypeStruct((rows, width), jnp.bfloat16), jax.ShapeDtypeStruct(start.shape, jnp.float32)]
-    scratch = [pltpu.VMEM((rows, width), jnp.float32), pltpu.VMEM((4, 8, width), jnp.float32)]
-    return kernel_call(last_kernel, "last", 8, outs, tokens, gain, w_qkv, d_middle,
-                       *d_queries, *backs, *diagonals, start, scratch=scratch)
+    packed = jax.ShapeDtypeStruct((16, width), jnp.float32)
+    outs = [jax.ShapeDtypeStruct((rows, width), jnp.bfloat16), packed, packed]
+    scratch = [pltpu.VMEM(start.shape, jnp.float32), pltpu.VMEM((rows, width), jnp.float32), pltpu.VMEM((4, 8, width), jnp.float32)]
+    return kernel_call(last_kernel, "last", 8, outs, side, tokens, gain, w_qkv, d_middle,
+                       *d_queries, *backs, *diagonals, start, scratch=scratch, smem=1)
 
 
 def open_kernel(layout, place_ref, *refs):
@@ -549,27 +562,34 @@
                 out_ref[to, block * width : block * width + width] = refs[index][at : at + size, :].astype(jnp.float32)
 
 
-OPEN_LAYOUTS = {"back": ((0, 1),), "inward": ((0, 4),), "rest": ((0, 3), (144, 1))}
+def open_rest_kernel(place_ref, *refs):
+    chunks, outs, parts_ref = refs[:RING], refs[RING:-1], refs[-1]
+    open_kernel(((0, 3), (144, 1)), place_ref, *chunks, outs[0], outs[1])
+    for index in range(RING):
+        parts_ref[place_ref[index]] = chunks[index][192:, :].astype(jnp.float32)
+    total = parts_ref[0]
+    for index in range(1, RING):
+        total = total + parts_ref[index]
+    parts_ref[0] = total
+    for row in range(8):
+        outs[2 + row][...] = parts_ref[0, row : row + 1, :384]
+    for row in range(4):
+        outs[10][:, row * 384 : row * 384 + 384] = parts_ref[0, 8 + row : 9 + row, :384]
+    for row in range(6):
+        outs[11][:, row * 384 : row * 384 + 384] = parts_ref[0, row : row + 1, 384:]
 
 
 def open_call(name, places, chunks):
-    layout = OPEN_LAYOUTS[name]
     width = chunks[0].shape[1]
-    outs = [
-        jax.ShapeDtypeStruct((RING * (192 if name == "back" else 48), blocks * width), jnp.float32)
-        for _, blocks in layout
-    ]
-    return kernel_call(functools.partial(open_kernel, layout), f"open_{name}", 4, outs, places, *chunks, smem=1)
-
-
-def open_small_kernel(side_ref, small_ref, *outs):
-    side = side_ref[0]
-    for row in range(8):
-        outs[row][...] = small_ref[side, row : row + 1, :]
-    for row in range(4):
-        outs[8][:, row * 384 : row * 384 + 384] = small_ref[side, 8 + row : 9 + row, :]
-    for row in range(6):
-        outs[9][:, row * 384 : row * 384 + 384] = small_ref[side, 12 + row : 13 + row, :]
+    half = width // 2
+    if name == "rest":
+        shapes = [(half, 3 * width), (half, width)] + [(1, half)] * 8 + [(1, 2 * width), (1, 3 * width)]
+        kernel, scratch = open_rest_kernel, [pltpu.VMEM((RING, 16, width), jnp.float32)]
+    else:
+        shapes = [(2 * width, width)] if name == "back" else [(half, 4 * width)]
+        kernel, scratch = functools.partial(open_kernel, ((0, shapes[0][1] // width),)), []
+    outs = [jax.ShapeDtypeStruct(shape, jnp.float32) for shape in shapes]
+    return kernel_call(kernel, f"open_{name}", 4, outs, places, *chunks, smem=1, scratch=scratch)
 
 
 def partner_2(shard, axis, distance):
@@ -630,7 +650,8 @@
 def unringed_grads(feed, rest, small):
     feed = unringed_total(*feed)
     rest = unringed_total(*rest)
-    small = lax.psum(small, ("group", "dp"))
+    small = lax.psum(jnp.stack(small)[:, :12], ("group", "dp"))
+    small = jnp.concatenate([small[:, :, :384], small[:, :, 384:]], axis=1)
     vectors = [small[:, row].reshape(-1) for row in range(8)]
     vectors += [small[:, 8:12].reshape(-1), small[:, 12:18].reshape(-1)]
     weights = (
@@ -674,6 +695,16 @@
         self.step += 1
         return held
 
+    def split(self, cuts):
+        pieces = []
+        for start, stop in zip(cuts, cuts[1:]):
+            piece = Ring.__new__(Ring)
+            piece.order, piece.step = self.order, self.step
+            piece.mine, piece.met = self.mine[:, start:stop], self.met[:, start:stop]
+            piece.arrived = None if self.arrived is None else self.arrived[start:stop]
+            pieces.append(piece)
+        return pieces
+
 
 def gather(held, waits={}):
     chunks = [held]
@@ -683,26 +714,6 @@
             held = waits[step](held)
         chunks.append(held)
     return chunks
-
-
-SMALL_EARLY = (4, 6)
-SMALL_PAIRS = (("dp", 0), ("group", 0), ("group", 1), ("group", 2))
-
-
-class Small:
-    def __init__(self, order, small):
-        self.order, self.small, self.step = order, small, 0
-        self.send()
-
-    def send(self):
-        self.arrived = partner_2(self.small, *SMALL_PAIRS[self.step])
-
-    def advance(self):
-        self.small = self.small + self.order.after(self.arrived)
-        self.order.mark = self.small
-        self.step += 1
-        if self.step < len(SMALL_PAIRS):
-            self.send()
 
 
 def on_device(
@@ -753,25 +764,22 @@
         queue.mark = rest_mine
         feed.reduce()
         rest = Ring(queue, rest_mine, rest_other)
-    g_tokens, small = last_call(
-        tokens[0], ln1_gain, w_qkv[0], queue.after(d_middle), d_queries, backs, diagonals, small
+    side = lax.axis_index("dp").reshape(1)
+    g_tokens, *small = last_call(
+        side if ringed else jnp.zeros_like(side), tokens[0], ln1_gain, w_qkv[0], queue.after(d_middle), d_queries, backs, diagonals, small
     )
     if ringed:
         queue.mark = g_tokens
         feed.reduce()
         rest.reduce()
         queue.free = True
-        minor = Small(queue, small)
-
-        def small_turn(value):
-            minor.advance()
-            value, minor.small = lax.optimization_barrier((value, minor.small))
-            return value
-
-        while feed.step < RING:
-            feed_held = feed.reduce()
-        back_chunks = gather(feed_held[:192])
-        in_chunks = gather(feed_held[192:])
+        held_parts = []
+        for piece in feed.split((0, 192, 384)):
+            while piece.step < RING:
+                held = piece.reduce()
+            held_parts.append(held)
+        back_chunks = gather(held_parts[0])
+        in_chunks = gather(held_parts[1])
         g_w_back = open_call("back", places, back_chunks)
         g_w_in = open_call("inward", places, in_chunks)
         opened = [*g_w_back, *g_w_in]
@@ -785,17 +793,13 @@
             return value
 
         while rest.step < RING:
-            if rest.step in SMALL_EARLY:
-                rest.arrived = small_turn(rest.arrived)
             rest_held = rest.reduce()
-        rest_chunks = gather(rest_held, {1: small_turn, 3: small_turn, 6: back_turn, 7: in_turn})
+        small_held = add_low(small[0], lax.ppermute(small[1], "dp", [(0, 1), (1, 0)]))
+        rest_held = jnp.concatenate([rest_held, small_held], axis=0)
+        rest_chunks = gather(rest_held, {6: back_turn, 7: in_turn})
         opened += open_call("rest", places, rest_chunks)
-        weights = [value[None] for value in opened]
-        half = width // 2
-        side = lax.axis_index("dp").reshape(1)
-        shapes = [(1, half)] * 8 + [(1, 2 * width), (1, 3 * width)]
-        outs = [jax.ShapeDtypeStruct(shape, jnp.float32) for shape in shapes]
-        vectors = kernel_call(open_small_kernel, "open_small", 1, outs, side, minor.small, smem=1)
+        weights = [value[None] for value in opened[:4]]
+        vectors = opened[4:]
     else:
         weights, vectors = unringed_grads(
             (feed_mine, feed_other), (rest_mine, rest_other), small

time: 304 us -> 288 us (0.947); the launches traced: 300 us -> 287 us
  starting transfers between devices: 61.4 us -> 38.5 us
  waiting for transfers between devices: 92.4 us -> 112 us
  Pallas kernels: 126 us -> 117 us
    ppermute x35 -> x37, waiting for transfers between devices: 62.8 us -> 90.8 us  [ring_send(): return lax.ppermute(chunk, ('group', 'dp'), pairs)]
    ppermute x35 -> x37, starting transfers between devices: 46.9 us -> 29.6 us  [ring_send(): return lax.ppermute(chunk, ('group', 'dp'), pairs)]
    ppermute x10 -> x6, waiting for transfers between devices: 29.6 us -> 19.9 us  [partner_2(): lax.ppermute(shard, axis, [(i, i ^ 1 << distance) for i in range(lax.axis...]
    pallas_call x14 -> x13, Pallas kernels: 94.5 us -> 85.3 us  [kernel_call(): pl.pallas_call(kernel, out_shape=tuple(outs), in_specs=specs, out_specs=t...]
    ppermute x10 -> x6, starting transfers between devices: 14.4 us -> 8.83 us  [partner_2(): lax.ppermute(shard, axis, [(i, i ^ 1 << distance) for i in range(lax.axis...]
    convert_element_type x16 -> x17, other arithmetic: 12.4 us -> 12.4 us  [add_low(): sum((term.astype(jnp.float32) for term in terms)).astype(jnp.bfloat16)]
  transfers between devices with their start and end apart: 47 -> 46, of which waited for: 28 -> 35; matrix products, arithmetic and copies ran while one was open for 4% -> 4% of each run, Pallas kernels for 23% -> 24%
where the time goes in v1:
time: 288 us; the launch traced here: 287 us
  Pallas kernels  117 us (41%)
  waiting for transfers between devices  112 us (39%)
  starting transfers between devices  38.5 us (13%)
  other arithmetic  14.2 us (5%)
  local copies, waits for them, and re-layouts  4.01 us (1%)
    ppermute x37, waiting for transfers between devices, ring_send(): return lax.ppermute(chunk, ('group', 'dp'), pairs)  90.8 us
    pallas_call x13, Pallas kernels, kernel_call(): pl.pallas_call(kernel, out_shape=tuple(outs), in_specs=specs, out_specs=t...  85.3 us
    pallas_call x1, Pallas kernels, feed_call(): pl.pallas_call(feed_kernel, out_shape=(wide(bf16), wide(f32), wide(bf16),...  31.9 us
    ppermute x37, starting transfers between devices, ring_send(): return lax.ppermute(chunk, ('group', 'dp'), pairs)  29.6 us
    ppermute x6, waiting for transfers between devices, partner_2(): lax.ppermute(shard, axis, [(i, i ^ 1 << distance) for i in range(lax.axis...  19.9 us
    convert_element_type x17, other arithmetic, add_low(): sum((term.astype(jnp.float32) for term in terms)).astype(jnp.bfloat16)  12.4 us
    ppermute x6, starting transfers between devices, partner_2(): lax.ppermute(shard, axis, [(i, i ^ 1 << distance) for i in range(lax.axis...  8.83 us
  transfers between devices with their start and end apart: 46, of which 35 were waited for; matrix products, arithmetic and copies ran while one was open for 4% of the time, Pallas kernels for 24%

profile of v1, /device:TPU:0, one launch (start us, length us, event | category | flops | bytes accessed | tf_op | source)
XLA Modules:
  0.0 287.1 jit_solution(11074486259308464087)
XLA Ops:
  0.7 4.7 %first.1 = (bf16[512,768]{1,0:T(8,128)(2,1)}, bf16[2,512,256]{2,1,0:T(8,128)(2,1)}, bf16[2,512,256]{2,1,0:T(8,128)(2,1)}, bf16[2,512,256]{2,1,0:T(8,128)(2,1)}) custom-call(bf16[512,768]{1,0:T(8,128)(2,1)} %bitcast.163, f32[1,768]{1,0:T(1,128)} %gain_ref.5, f32[1,768]{1,0:T(1,128)} %shift_ref.2, bf16[768,2304]{1,0:T(8,128)(2,1)} %bitcast.158, f32[1,768]{1,0:T(1,128)} %bias_ref.2), custom_call_target="tpu_custom_call" | custom-call | flops 5000000000 | tf_op jit(solution)/shard_map/first/pallas_call | solution.py:265
  5.4 3.0 %collective-permute-start = (bf16[2,512,256]{2,1,0:T(8,128)(2,1)}, bf16[2,512,256]{2,1,0:T(8,128)(2,1)S(1)}, u32[]{:S(2)}, u32[]{:S(2)}) collective-permute-start(bf16[2,512,256]{2,1,0:T(8,128)(2,1)} %get-tuple-element.87), channel_id=1, source_target_pairs={{0,16},{16,0},{1,17},{17,1},{2,18},{18,2},{3,19},{19,3},{4,20},{20... | collective-permute-start | bytes 1572872 | tf_op jit(solution)/shard_map/ppermute | solution.py:596
  8.4 2.0 collective-permute-start.2
  11.6 5.3 %prep.1 = (bf16[512,768]{1,0:T(8,128)(2,1)}, bf16[512,384]{1,0:T(8,128)(2,1)}, bf16[512,384]{1,0:T(8,128)(2,1)}, bf16[512,384]{1,0:T(8,128)(2,1)}, s32[1,512]{1,0:T(1,128)}, /*index=5*/bf16[36,128,128]{2,1,0:T(8,128)(2,1)}) custom-call(s32[1]{0:T(128)} %bitcast.1.stream_ref, s32[2,2,1,512]{3,2,1,0:T(1,128)} %box_ref.1, s32[2,1,512]{2,1,0:T(1,128)} %segment_ref.1, ...), custom_call_target="tpu_custom_call" | custom-call | flops 5000000000 | tf_op jit(solution)/shard_map/prep/pallas_call | solution.py:265
  16.9 4.5 %collective-permute-done.pair_ref = bf16[2,512,256]{2,1,0:T(8,128)(2,1)S(1)} collective-permute-done((bf16[2,512,256]{2,1,0:T(8,128)(2,1)}, bf16[2,512,256]{2,1,0:T(8,128)(2,1)S(1)}, u32[]{:S(2)}, u32[]{:S(2)}) %collective-permute-start) | collective-permute-done | bytes 524320 | tf_op jit(solution)/shard_map/ppermute | solution.py:596
  22.2 7.3 %attend_0.1 = (bf16[512,256]{1,0:T(8,128)(2,1)}, bf16[4,512,512]{2,1,0:T(8,128)(2,1)}) custom-call(bf16[512,768]{1,0:T(8,128)(2,1)} %get-tuple-element.86.queries_ref, bf16[2,512,256]{2,1,0:T(8,128)(2,1)} %copy-done.8, bf16[512,384]{1,0:T(8,128)(2,1)} %get-tuple-element.88.hot_ref, bf16[512,384]{1,0:T(8,128)(2,1)} %get-tuple-element.89.key_hot_ref, ...), custom_call_target="tpu_custom_call" | custom-call | flops 7000000000 | tf_op jit(solution)/shard_map/attend_0/pallas_call | solution.py:265
  29.5 3.1 %collective-permute-done.1.pair_ref = bf16[2,512,256]{2,1,0:T(8,128)(2,1)S(1)} collective-permute-done((bf16[2,512,256]{2,1,0:T(8,128)(2,1)}, bf16[2,512,256]{2,1,0:T(8,128)(2,1)S(1)}, u32[]{:S(2)}, u32[]{:S(2)}) %collective-permute-start.1) | collective-permute-done | bytes 524320 | tf_op jit(solution)/shard_map/ppermute | solution.py:596
  33.4 7.4 %attend_1.1 = (bf16[512,256]{1,0:T(8,128)(2,1)}, bf16[4,512,512]{2,1,0:T(8,128)(2,1)}) custom-call(bf16[512,768]{1,0:T(8,128)(2,1)} %get-tuple-element.86.queries_ref, bf16[2,512,256]{2,1,0:T(8,128)(2,1)} %copy-done.7, bf16[512,384]{1,0:T(8,128)(2,1)} %get-tuple-element.88.hot_ref, bf16[512,384]{1,0:T(8,128)(2,1)} %get-tuple-element.89.key_hot_ref, ...), custom_call_target="tpu_custom_call" | custom-call | flops 7000000000 | tf_op jit(solution)/shard_map/attend_1/pallas_call | solution.py:265
  40.8 2.2 collective-permute-done.2.pair_ref
  43.8 7.3 %attend_2.1 = (bf16[512,256]{1,0:T(8,128)(2,1)}, bf16[4,512,512]{2,1,0:T(8,128)(2,1)}) custom-call(bf16[512,768]{1,0:T(8,128)(2,1)} %get-tuple-element.86.queries_ref, bf16[2,512,256]{2,1,0:T(8,128)(2,1)} %copy-done.6, bf16[512,384]{1,0:T(8,128)(2,1)} %get-tuple-element.88.hot_ref, bf16[512,384]{1,0:T(8,128)(2,1)} %get-tuple-element.89.key_hot_ref, ...), custom_call_target="tpu_custom_call" | custom-call | flops 7000000000 | tf_op jit(solution)/shard_map/attend_2/pallas_call | solution.py:265
  51.1 31.9 %feed.1 = (bf16[512,768]{1,0:T(8,128)(2,1)}, f32[512,768]{1,0:T(8,128)}, bf16[512,768]{1,0:T(8,128)(2,1)}, bf16[512,768]{1,0:T(8,128)(2,1)}, bf16[8,384,768]{2,1...) custom-call(s32[16]{0:T(128)} %fusion.20.order_ref, bf16[512,768]{1,0:T(8,128)(2,1)} %bitcast.164, ...), custom_call_target="tpu_custom_call" | custom-call | flops 30000001024 | tf_op jit(solution)/shard_map/feed/pallas_call | solution.py:205
  83.0 8.0 %attend_back_0.1 = (bf16[512,256]{1,0:T(8,128)(2,1)}, bf16[2,512,256]{2,1,0:T(8,128)(2,1)}, f32[3,4,256]{2,1,0:T(4,128)}) custom-call(bf16[512,768]{1,0:T(8,128)(2,1)} %get-tuple-element.86.queries_ref, bf16[2,512,256]{2,1,0:T(8,128)(2,1)} %copy-done.8, bf16[512,384]{1,0:T(8,128)(2,1)} %get-tuple-element.104.turned_hot_ref, ...), custom_call_target="tpu_custom_call" | custom-call | flops 8000000000 | tf_op jit(solution)/shard_map/attend_back_0/pallas_call | solution.py:265
  91.1 1.8 collective-permute-start.6
  95.8 8.1 %attend_back_1.1 = (bf16[512,256]{1,0:T(8,128)(2,1)}, bf16[2,512,256]{2,1,0:T(8,128)(2,1)}, f32[3,4,256]{2,1,0:T(4,128)}) custom-call(bf16[512,768]{1,0:T(8,128)(2,1)} %get-tuple-element.86.queries_ref, bf16[2,512,256]{2,1,0:T(8,128)(2,1)} %copy-done.7, bf16[512,384]{1,0:T(8,128)(2,1)} %get-tuple-element.104.turned_hot_ref, ...), custom_call_target="tpu_custom_call" | custom-call | flops 8000000000 | tf_op jit(solution)/shard_map/attend_back_1/pallas_call | solution.py:265
  105.9 1.6 collective-permute-start.5
  107.5 8.3 %attend_back_2.1 = (bf16[512,256]{1,0:T(8,128)(2,1)}, bf16[2,512,256]{2,1,0:T(8,128)(2,1)}, f32[3,4,256]{2,1,0:T(4,128)}) custom-call(bf16[512,768]{1,0:T(8,128)(2,1)} %get-tuple-element.86.queries_ref, bf16[2,512,256]{2,1,0:T(8,128)(2,1)} %copy-done.6, bf16[512,384]{1,0:T(8,128)(2,1)} %get-tuple-element.104.turned_hot_ref, ...), custom_call_target="tpu_custom_call" | custom-call | flops 8000000000 | tf_op jit(solution)/shard_map/attend_back_2/pallas_call | solution.py:265
  120.5 10.1 %collective-permute-done.9.back_2_ref = bf16[2,512,256]{2,1,0:T(8,128)(2,1)S(1)} collective-permute-done((bf16[2,512,256]{2,1,0:T(8,128)(2,1)S(1)}, bf16[2,512,256]{2,1,0:T(8,128)(2,1)S(1)}, u32[]{:S(2)}, u32[]{:S(2)}) %collective-permute-start.9) | collective-permute-done | bytes 524320 | tf_op jit(solution)/shard_map/ppermute | solution.py:596
  131.3 9.4 %weights.1 = (bf16[8,192,768]{2,1,0:T(8,128)(2,1)}, bf16[8,192,768]{2,1,0:T(8,128)(2,1)}) custom-call(s32[16]{0:T(128)} %fusion.20.order_ref, bf16[512,768]{1,0:T(8,128)(2,1)} %get-tuple-element.120.normed_ref, bf16[512,768]{1,0:T(8,128)(2,1)} %get-tuple-element.121.d_branch_ref, bf16[512,256]{1,0:T(8,128)(2,1)} %get-tuple-element.92.context_0_ref, ...), custom_call_target="tpu_custom_call" | custom-call | flops 7000000000 | tf_op jit(solution)/shard_map/weights/pallas_call | solution.py:265
  142.8 7.5 %last.1 = (bf16[512,768]{1,0:T(8,128)(2,1)}, f32[16,768]{1,0:T(8,128)}, f32[16,768]{1,0:T(8,128)}) custom-call(s32[1]{0:T(128)} %bitcast.8.side_ref, bf16[512,768]{1,0:T(8,128)(2,1)} %bitcast.165, f32[1,768]{1,0:T(1,128)} %gain_ref.5, bf16[768,2304]{1,0:T(8,128)(2,1)} %bitcast.160, f32[512,768]{1,0:T(8,128)} %get-tuple-element.126.d_middle_ref, ...), custom_call_target="tpu_custom_call" | custom-call | flops 8000000000 | tf_op jit(solution)/shard_map/last/pallas_call | solution.py:265
  150.3 1.9 collective-permute-done.11
  154.3 6.2 %collective-permute-done.12 = bf16[192,768]{1,0:T(8,128)(2,1)S(1)} collective-permute-done((bf16[192,768]{1,0:T(8,128)(2,1)S(1)}, bf16[192,768]{1,0:T(8,128)(2,1)S(1)}, u32[]{:S(2)}, u32[]{:S(2)}) %collective-permute-start.12) | collective-permute-done | bytes 294944 | tf_op jit(solution)/shard_map/ppermute | solution.py:606
  162.7 4.7 %collective-permute-done.13 = bf16[192,768]{1,0:T(8,128)(2,1)S(1)} collective-permute-done((bf16[192,768]{1,0:T(8,128)(2,1)S(1)}, bf16[192,768]{1,0:T(8,128)(2,1)S(1)}, u32[]{:S(2)}, u32[]{:S(2)}) %collective-permute-start.13) | collective-permute-done | bytes 294944 | tf_op jit(solution)/shard_map/ppermute | solution.py:606
  168.1 8.8 %collective-permute-done.14 = bf16[192,768]{1,0:T(8,128)(2,1)S(1)} collective-permute-done((bf16[192,768]{1,0:T(8,128)(2,1)S(1)}, bf16[192,768]{1,0:T(8,128)(2,1)S(1)}, u32[]{:S(2)}, u32[]{:S(2)}) %collective-permute-start.14) | collective-permute-done | bytes 294944 | tf_op jit(solution)/shard_map/ppermute | solution.py:606
  184.4 2.5 collective-permute-done.37
  186.9 3.2 %collective-permute-done.27 = bf16[192,768]{1,0:T(8,128)(2,1)S(1)} collective-permute-done((bf16[192,768]{1,0:T(8,128)(2,1)S(1)}, bf16[192,768]{1,0:T(8,128)(2,1)S(1)}, u32[]{:S(2)}, u32[]{:S(2)}) %collective-permute-start.27) | collective-permute-done | bytes 294944 | tf_op jit(solution)/shard_map/ppermute | solution.py:606
  195.4 3.0 %collective-permute-done.38 = bf16[192,768]{1,0:T(8,128)(2,1)S(1)} collective-permute-done((bf16[192,768]{1,0:T(8,128)(2,1)S(1)}, bf16[192,768]{1,0:T(8,128)(2,1)S(1)}, u32[]{:S(2)}, u32[]{:S(2)}) %collective-permute-start.38) | collective-permute-done | bytes 294944 | tf_op jit(solution)/shard_map/ppermute | solution.py:606
  198.3 3.2 %collective-permute-done.28 = bf16[192,768]{1,0:T(8,128)(2,1)S(1)} collective-permute-done((bf16[192,768]{1,0:T(8,128)(2,1)S(1)}, bf16[192,768]{1,0:T(8,128)(2,1)S(1)}, u32[]{:S(2)}, u32[]{:S(2)}) %collective-permute-start.28) | collective-permute-done | bytes 294944 | tf_op jit(solution)/shard_map/ppermute | solution.py:606
  210.2 2.7 collective-permute-done.18
  213.6 2.5 collective-permute-done.39.refs_1_
  216.5 2.7 collective-permute-done.30.refs_2_
  219.7 2.9 %collective-permute-done.20.refs_1_ = bf16[208,768]{1,0:T(8,128)(2,1)S(1)} collective-permute-done((bf16[208,768]{1,0:T(8,128)(2,1)S(1)}, bf16[208,768]{1,0:T(8,128)(2,1)S(1)}, u32[]{:S(2)}, u32[]{:S(2)}) %collective-permute-start.20) | collective-permute-done | bytes 319520 | tf_op jit(solution)/shard_map/ppermute | solution.py:606
  223.1 2.7 collective-permute-done.40.refs_2_
  226.3 2.7 collective-permute-done.31.refs_3_
  229.4 2.9 %collective-permute-done.21.refs_2_ = bf16[208,768]{1,0:T(8,128)(2,1)S(1)} collective-permute-done((bf16[208,768]{1,0:T(8,128)(2,1)S(1)}, bf16[208,768]{1,0:T(8,128)(2,1)S(1)}, u32[]{:S(2)}, u32[]{:S(2)}) %collective-permute-start.21) | collective-permute-done | bytes 319520 | tf_op jit(solution)/shard_map/ppermute | solution.py:606
  232.9 2.7 collective-permute-done.41.refs_3_
  236.0 2.7 collective-permute-done.32.refs_4_
  239.2 2.9 %collective-permute-done.22.refs_3_ = bf16[208,768]{1,0:T(8,128)(2,1)S(1)} collective-permute-done((bf16[208,768]{1,0:T(8,128)(2,1)S(1)}, bf16[208,768]{1,0:T(8,128)(2,1)S(1)}, u32[]{:S(2)}, u32[]{:S(2)}) %collective-permute-start.22) | collective-permute-done | bytes 319520 | tf_op jit(solution)/shard_map/ppermute | solution.py:606
  242.6 2.7 collective-permute-done.42.refs_4_
  245.8 2.7 collective-permute-done.33.refs_5_
  248.9 2.9 %collective-permute-done.23.refs_4_ = bf16[208,768]{1,0:T(8,128)(2,1)S(1)} collective-permute-done((bf16[208,768]{1,0:T(8,128)(2,1)S(1)}, bf16[208,768]{1,0:T(8,128)(2,1)S(1)}, u32[]{:S(2)}, u32[]{:S(2)}) %collective-permute-start.23) | collective-permute-done | bytes 319520 | tf_op jit(solution)/shard_map/ppermute | solution.py:606
  252.4 2.8 collective-permute-done.43.refs_5_
  255.6 2.7 collective-permute-done.34.refs_6_
  259.4 5.5 %collective-permute-done.44.refs_6_ = bf16[192,768]{1,0:T(8,128)(2,1)} collective-permute-done((bf16[192,768]{1,0:T(8,128)(2,1)}, bf16[192,768]{1,0:T(8,128)(2,1)}, u32[]{:S(2)}, u32[]{:S(2)}) %collective-permute-start.44) | collective-permute-done | bytes 294944 | tf_op jit(solution)/shard_map/ppermute | solution.py:606
  268.0 4.1 %open_back.1 = f32[1536,768]{1,0:T(8,128)} custom-call(s32[8]{0:T(128)} %and_select_fusion.place_ref, bf16[192,768]{1,0:T(8,128)(2,1)} %copy-done.3, bf16[192,768]{1,0:T(8,128)(2,1)} %copy-done.20, bf16[192,768]{1,0:T(8,128)(2,1)} %copy-done.22, bf16[192,768]{1,0:T(8,128)(2,1)} %copy-done.25, bf16[192,768]{1,0:T(8,128)(2,1)} %copy-done.27, ...), custom_call_target="tpu_custom_call" | custom-call | flops 4000000000 | tf_op jit(solution)/shard_map/open_back/pallas_call | solution.py:265
  272.2 3.0 %collective-permute-done.25.refs_6_ = bf16[208,768]{1,0:T(8,128)(2,1)S(1)} collective-permute-done((bf16[208,768]{1,0:T(8,128)(2,1)S(1)}, bf16[208,768]{1,0:T(8,128)(2,1)S(1)}, u32[]{:S(2)}, u32[]{:S(2)}) %collective-permute-start.25) | collective-permute-done | bytes 319520 | tf_op jit(solution)/shard_map/ppermute | solution.py:606
  275.7 4.1 %open_inward.1 = f32[384,3072]{1,0:T(8,128)} custom-call(s32[8]{0:T(128)} %and_select_fusion.place_ref, bf16[192,768]{1,0:T(8,128)(2,1)} %copy-done.2, bf16[192,768]{1,0:T(8,128)(2,1)} %copy-done.21, bf16[192,768]{1,0:T(8,128)(2,1)} %copy-done.23, bf16[192,768]{1,0:T(8,128)(2,1)} %copy-done.24, bf16[192,768]{1,0:T(8,128)(2,1)} %copy-done.26, ...), custom_call_target="tpu_custom_call" | custom-call | flops 4000000000 | tf_op jit(solution)/shard_map/open_inward/pallas_call | solution.py:265
  279.8 2.4 collective-permute-done.36.refs_7_
  282.9 4.0 %open_rest.1 = (f32[384,2304]{1,0:T(8,128)}, f32[384,768]{1,0:T(8,128)}, f32[1,384]{1,0:T(1,128)}, f32[1,384]{1,0:T(1,128)}, f32[1,384]{1,0:T(1,128)}, /*index=5...) custom-call(s32[8]{0:T(128)} %and_select_fusion.place_ref, ...), custom_call_target="tpu_custom_call" | custom-call | flops 4000000000 | tf_op jit(solution)/shard_map/open_rest/pallas_call | solution.py:265
  (139 shorter events, 55.2 us)
Async XLA Ops:
  5.4 15.9 %collective-permute-start = (bf16[2,512,256]{2,1,0:T(8,128)(2,1)}, bf16[2,512,256]{2,1,0:T(8,128)(2,1)S(1)}, u32[]{:S(2)}, u32[]{:S(2)}) collective-permute-start(bf16[2,512,256]{2,1,0:T(8,128)(2,1)} %get-tuple-element.87), channel_id=1, source_target_pairs={{0,16},{16,0},{1,17},{17,1},{2,18},{18,2},{3,19},{19,3},{4,20},{20... | collective-permute-start | bytes 1572872 | tf_op jit(solution)/shard_map/ppermute | solution.py:596
  8.4 24.2 %collective-permute-start.1 = (bf16[2,512,256]{2,1,0:T(8,128)(2,1)}, bf16[2,512,256]{2,1,0:T(8,128)(2,1)S(1)}, u32[]{:S(2)}, u32[]{:S(2)}) collective-permute-start(bf16[2,512,256]{2,1,0:T(8,128)(2,1)} %get-tuple-element.93), channel_id=1, source_target_pairs={{0,16},{16,0},{1,17},{17,1},{2,18},{18,2},{3,19},{19,3},{4,20},{20... | collective-permute-start | bytes 1572872 | tf_op jit(solution)/shard_map/ppermute | solution.py:596
  8.4 34.6 %collective-permute-start.2 = (bf16[2,512,256]{2,1,0:T(8,128)(2,1)}, bf16[2,512,256]{2,1,0:T(8,128)(2,1)S(1)}, u32[]{:S(2)}, u32[]{:S(2)}) collective-permute-start(bf16[2,512,256]{2,1,0:T(8,128)(2,1)} %get-tuple-element.96), channel_id=1, source_target_pairs={{0,16},{16,0},{1,17},{17,1},{2,18},{18,2},{3,19},{19,3},{4,20},{20... | collective-permute-start | bytes 1572872 | tf_op jit(solution)/shard_map/ppermute | solution.py:596
  83.0 9.9 %collective-permute-start.3 = (bf16[8,384,768]{2,1,0:T(8,128)(2,1)}, bf16[8,384,768]{2,1,0:T(8,128)(2,1)}, u32[]{:S(2)}, u32[]{:S(2)}) collective-permute-start(bf16[8,384,768]{2,1,0:T(8,128)(2,1)} %get-tuple-element.103), channel_id=1, source_target_pairs={{0,1},{1,0},{2,3},{3,2},{4,5},{5,4},{6,7},{7,6},{8,9},{9,8},{10,11... | collective-permute-start | bytes 14155784 | tf_op jit(solution)/shard_map/ppermute | solution.py:683
  91.1 16.4 %collective-permute-start.6 = (bf16[2,512,256]{2,1,0:T(8,128)(2,1)}, bf16[2,512,256]{2,1,0:T(8,128)(2,1)S(1)}, u32[]{:S(2)}, u32[]{:S(2)}) collective-permute-start(bf16[2,512,256]{2,1,0:T(8,128)(2,1)} %get-tuple-element.115), channel_id=1, source_target_pairs={{0,16},{16,0},{1,17},{17,1},{2,18},{18,2},{3,19},{19,3},{4,20},{20... | collective-permute-start | bytes 1572872 | tf_op jit(solution)/shard_map/ppermute | solution.py:596
  94.2 10.2 %collective-permute-start.4 = (bf16[384,768]{1,0:T(8,128)(2,1)S(1)}, bf16[384,768]{1,0:T(8,128)(2,1)S(1)}, u32[]{:S(2)}, u32[]{:S(2)}) collective-permute-start(bf16[384,768]{1,0:T(8,128)(2,1)S(1)} %fusion.4), channel_id=1, source_target_pairs={{0,4},{1,3},{4,8},{5,1},{8,12},{9,5},{12,14},{13,9},{14,10},{15,13... | collective-permute-start | bytes 1769480 | tf_op jit(solution)/shard_map/ppermute | solution.py:606
  103.9 16.6 %collective-permute-start.8 = (bf16[2,512,256]{2,1,0:T(8,128)(2,1)}, bf16[2,512,256]{2,1,0:T(8,128)(2,1)S(1)}, u32[]{:S(2)}, u32[]{:S(2)}) collective-permute-start(bf16[2,512,256]{2,1,0:T(8,128)(2,1)} %get-tuple-element.119), channel_id=1, source_target_pairs={{0,16},{16,0},{1,17},{17,1},{2,18},{18,2},{3,19},{19,3},{4,20},{20... | collective-permute-start | bytes 1572872 | tf_op jit(solution)/shard_map/ppermute | solution.py:596
  105.9 9.9 %collective-permute-start.5 = (bf16[384,768]{1,0:T(8,128)(2,1)S(1)}, bf16[384,768]{1,0:T(8,128)(2,1)S(1)}, u32[]{:S(2)}, u32[]{:S(2)}) collective-permute-start(bf16[384,768]{1,0:T(8,128)(2,1)S(1)} %fusion.3), channel_id=1, source_target_pairs={{0,4},{1,3},{4,8},{5,1},{8,12},{9,5},{12,14},{13,9},{14,10},{15,13... | collective-permute-start | bytes 1769480 | tf_op jit(solution)/shard_map/ppermute | solution.py:606
  117.3 13.2 %collective-permute-start.9 = (bf16[2,512,256]{2,1,0:T(8,128)(2,1)S(1)}, bf16[2,512,256]{2,1,0:T(8,128)(2,1)S(1)}, u32[]{:S(2)}, u32[]{:S(2)}) collective-permute-start(bf16[2,512,256]{2,1,0:T(8,128)(2,1)S(1)} %copy-done.12), channel_id=1, source_target_pairs={{0,16},{16,0},{1,17},{17,1},{2,18},{18,2},{3,19},{19,3},{4,20},{20... | collective-permute-start | bytes 1572872 | tf_op jit(solution)/shard_map/ppermute | solution.py:596
  118.9 21.8 %collective-permute-start.7 = (bf16[384,768]{1,0:T(8,128)(2,1)S(1)}, bf16[384,768]{1,0:T(8,128)(2,1)S(1)}, u32[]{:S(2)}, u32[]{:S(2)}) collective-permute-start(bf16[384,768]{1,0:T(8,128)(2,1)S(1)} %fusion.2), channel_id=1, source_target_pairs={{0,4},{1,3},{4,8},{5,1},{8,12},{9,5},{12,14},{13,9},{14,10},{15,13... | collective-permute-start | bytes 1769480 | tf_op jit(solution)/shard_map/ppermute | solution.py:606
  142.2 11.5 %collective-permute-start.10 = (bf16[8,192,768]{2,1,0:T(8,128)(2,1)}, bf16[8,192,768]{2,1,0:T(8,128)(2,1)S(1)}, u32[]{:S(2)}, u32[]{:S(2)}) collective-permute-start(bf16[8,192,768]{2,1,0:T(8,128)(2,1)} %get-tuple-element.133), channel_id=1, source_target_pairs={{0,1},{1,0},{2,3},{3,2},{4,5},{5,4},{6,7},{7,6},{8,9},{9,8},{10,11... | collective-permute-start | bytes 7077896 | tf_op jit(solution)/shard_map/ppermute | solution.py:683
  142.3 9.9 %collective-permute-start.11 = (bf16[384,768]{1,0:T(8,128)(2,1)S(1)}, bf16[384,768]{1,0:T(8,128)(2,1)S(1)}, u32[]{:S(2)}, u32[]{:S(2)}) collective-permute-start(bf16[384,768]{1,0:T(8,128)(2,1)S(1)} %fusion.1), channel_id=1, source_target_pairs={{0,4},{1,3},{4,8},{5,1},{8,12},{9,5},{12,14},{13,9},{14,10},{15,13... | collective-permute-start | bytes 1769480 | tf_op jit(solution)/shard_map/ppermute | solution.py:606
  153.7 6.8 %collective-permute-start.12 = (bf16[192,768]{1,0:T(8,128)(2,1)S(1)}, bf16[192,768]{1,0:T(8,128)(2,1)S(1)}, u32[]{:S(2)}, u32[]{:S(2)}) collective-permute-start(bf16[192,768]{1,0:T(8,128)(2,1)S(1)} %fusion.18), channel_id=1, source_target_pairs={{0,4},{1,3},{4,8},{5,1},{8,12},{9,5},{12,14},{13,9},{14,10},{15,13... | collective-permute-start | bytes 884744 | tf_op jit(solution)/shard_map/ppermute | solution.py:606
  160.6 6.8 %collective-permute-start.13 = (bf16[192,768]{1,0:T(8,128)(2,1)S(1)}, bf16[192,768]{1,0:T(8,128)(2,1)S(1)}, u32[]{:S(2)}, u32[]{:S(2)}) collective-permute-start(bf16[192,768]{1,0:T(8,128)(2,1)S(1)} %fusion.17), channel_id=1, source_target_pairs={{0,4},{1,3},{4,8},{5,1},{8,12},{9,5},{12,14},{13,9},{14,10},{15,13... | collective-permute-start | bytes 884744 | tf_op jit(solution)/shard_map/ppermute | solution.py:606
  161.2 16.4 %collective-permute-start.26 = (bf16[384,768]{1,0:T(8,128)(2,1)S(1)}, bf16[384,768]{1,0:T(8,128)(2,1)S(1)}, u32[]{:S(2)}, u32[]{:S(2)}) collective-permute-start(bf16[384,768]{1,0:T(8,128)(2,1)S(1)} %fusion), channel_id=1, source_target_pairs={{0,4},{1,3},{4,8},{5,1},{8,12},{9,5},{12,14},{13,9},{14,10},{15,13... | collective-permute-start | bytes 1769480 | tf_op jit(solution)/shard_map/ppermute | solution.py:606
  167.5 9.4 %collective-permute-start.14 = (bf16[192,768]{1,0:T(8,128)(2,1)S(1)}, bf16[192,768]{1,0:T(8,128)(2,1)S(1)}, u32[]{:S(2)}, u32[]{:S(2)}) collective-permute-start(bf16[192,768]{1,0:T(8,128)(2,1)S(1)} %fusion.16), channel_id=1, source_target_pairs={{0,4},{1,3},{4,8},{5,1},{8,12},{9,5},{12,14},{13,9},{14,10},{15,13... | collective-permute-start | bytes 884744 | tf_op jit(solution)/shard_map/ppermute | solution.py:606
  177.0 6.8 %collective-permute-start.15 = (bf16[192,768]{1,0:T(8,128)(2,1)S(1)}, bf16[192,768]{1,0:T(8,128)(2,1)S(1)}, u32[]{:S(2)}, u32[]{:S(2)}) collective-permute-start(bf16[192,768]{1,0:T(8,128)(2,1)S(1)} %fusion.15), channel_id=1, source_target_pairs={{0,4},{1,3},{4,8},{5,1},{8,12},{9,5},{12,14},{13,9},{14,10},{15,13... | collective-permute-start | bytes 884744 | tf_op jit(solution)/shard_map/ppermute | solution.py:606
  179.0 7.9 %collective-permute-start.37 = (bf16[192,768]{1,0:T(8,128)(2,1)S(1)}, bf16[192,768]{1,0:T(8,128)(2,1)S(1)}, u32[]{:S(2)}, u32[]{:S(2)}) collective-permute-start(bf16[192,768]{1,0:T(8,128)(2,1)S(1)} %get-tuple-element.154), channel_id=1, source_target_pairs={{0,4},{1,3},{4,8},{5,1},{8,12},{9,5},{12,14},{13,9},{14,10},{15,13... | collective-permute-start | bytes 884744 | tf_op jit(solution)/shard_map/ppermute | solution.py:606
  180.6 9.5 %collective-permute-start.27 = (bf16[192,768]{1,0:T(8,128)(2,1)S(1)}, bf16[192,768]{1,0:T(8,128)(2,1)S(1)}, u32[]{:S(2)}, u32[]{:S(2)}) collective-permute-start(bf16[192,768]{1,0:T(8,128)(2,1)S(1)} %get-tuple-element.155), channel_id=1, source_target_pairs={{0,4},{1,3},{4,8},{5,1},{8,12},{9,5},{12,14},{13,9},{14,10},{15,13... | collective-permute-start | bytes 884744 | tf_op jit(solution)/shard_map/ppermute | solution.py:606
  183.9 9.7 %collective-permute-start.16 = (bf16[192,768]{1,0:T(8,128)(2,1)S(1)}, bf16[192,768]{1,0:T(8,128)(2,1)S(1)}, u32[]{:S(2)}, u32[]{:S(2)}) collective-permute-start(bf16[192,768]{1,0:T(8,128)(2,1)S(1)} %fusion.14), channel_id=1, source_target_pairs={{0,4},{1,3},{4,8},{5,1},{8,12},{9,5},{12,14},{13,9},{14,10},{15,13... | collective-permute-start | bytes 884744 | tf_op jit(solution)/shard_map/ppermute | solution.py:606
  191.6 6.8 %collective-permute-start.38 = (bf16[192,768]{1,0:T(8,128)(2,1)S(1)}, bf16[192,768]{1,0:T(8,128)(2,1)S(1)}, u32[]{:S(2)}, u32[]{:S(2)}) collective-permute-start(bf16[192,768]{1,0:T(8,128)(2,1)S(1)} %get-tuple-element.158), channel_id=1, source_target_pairs={{0,4},{1,3},{4,8},{5,1},{8,12},{9,5},{12,14},{13,9},{14,10},{15,13... | collective-permute-start | bytes 884744 | tf_op jit(solution)/shard_map/ppermute | solution.py:606
  192.1 9.4 %collective-permute-start.28 = (bf16[192,768]{1,0:T(8,128)(2,1)S(1)}, bf16[192,768]{1,0:T(8,128)(2,1)S(1)}, u32[]{:S(2)}, u32[]{:S(2)}) collective-permute-start(bf16[192,768]{1,0:T(8,128)(2,1)S(1)} %get-tuple-element.159), channel_id=1, source_target_pairs={{0,4},{1,3},{4,8},{5,1},{8,12},{9,5},{12,14},{13,9},{14,10},{15,13... | collective-permute-start | bytes 884744 | tf_op jit(solution)/shard_map/ppermute | solution.py:606
  193.7 10.9 %collective-permute-start.17 = (bf16[192,768]{1,0:T(8,128)(2,1)S(1)}, bf16[192,768]{1,0:T(8,128)(2,1)S(1)}, u32[]{:S(2)}, u32[]{:S(2)}) collective-permute-start(bf16[192,768]{1,0:T(8,128)(2,1)S(1)} %fusion.13), channel_id=1, source_target_pairs={{0,4},{1,3},{4,8},{5,1},{8,12},{9,5},{12,14},{13,9},{14,10},{15,13... | collective-permute-start | bytes 884744 | tf_op jit(solution)/shard_map/ppermute | solution.py:606
  202.9 65.1 %copy-start.3 = (bf16[192,768]{1,0:T(8,128)(2,1)}, bf16[192,768]{1,0:T(8,128)(2,1)S(1)}, u32[]{:S(2)}) copy-start(bf16[192,768]{1,0:T(8,128)(2,1)S(1)} %get-tuple-element.157.refs_0_) | copy-start | bytes 884740
  202.9 69.2 %copy-start.2 = (bf16[192,768]{1,0:T(8,128)(2,1)}, bf16[192,768]{1,0:T(8,128)(2,1)S(1)}, u32[]{:S(2)}) copy-start(bf16[192,768]{1,0:T(8,128)(2,1)S(1)} %get-tuple-element.156.refs_0_) | copy-start | bytes 884740
  203.0 6.8 %collective-permute-start.29 = (bf16[192,768]{1,0:T(8,128)(2,1)S(1)}, bf16[192,768]{1,0:T(8,128)(2,1)S(1)}, u32[]{:S(2)}, u32[]{:S(2)}) collective-permute-start(bf16[192,768]{1,0:T(8,128)(2,1)S(1)} %get-tuple-element.157.refs_0_), channel_id=1, source_target_pairs={{0,4},{1,3},{4,8},{5,1},{8,12},{9,5},{12,14},{13,9},{14,10},{15,13... | collective-permute-start | bytes 884744 | tf_op jit(solution)/shard_map/ppermute | solution.py:606
  204.8 8.1 %collective-permute-start.18 = (bf16[192,768]{1,0:T(8,128)(2,1)S(1)}, bf16[192,768]{1,0:T(8,128)(2,1)S(1)}, u32[]{:S(2)}, u32[]{:S(2)}) collective-permute-start(bf16[192,768]{1,0:T(8,128)(2,1)S(1)} %fusion.12), channel_id=1, source_target_pairs={{0,4},{1,3},{4,8},{5,1},{8,12},{9,5},{12,14},{13,9},{14,10},{15,13... | collective-permute-start | bytes 884744 | tf_op jit(solution)/shard_map/ppermute | solution.py:606
  205.3 1.2 collective-permute-start.19
  206.6 9.5 %collective-permute-start.39 = (bf16[192,768]{1,0:T(8,128)(2,1)S(1)}, bf16[192,768]{1,0:T(8,128)(2,1)S(1)}, u32[]{:S(2)}, u32[]{:S(2)}) collective-permute-start(bf16[192,768]{1,0:T(8,128)(2,1)S(1)} %get-tuple-element.156.refs_0_), channel_id=1, source_target_pairs={{0,4},{1,3},{4,8},{5,1},{8,12},{9,5},{12,14},{13,9},{14,10},{15,13... | collective-permute-start | bytes 884744 | tf_op jit(solution)/shard_map/ppermute | solution.py:606
  209.7 9.5 %collective-permute-start.30 = (bf16[192,768]{1,0:T(8,128)(2,1)S(1)}, bf16[192,768]{1,0:T(8,128)(2,1)S(1)}, u32[]{:S(2)}, u32[]{:S(2)}) collective-permute-start(bf16[192,768]{1,0:T(8,128)(2,1)S(1)} %collective-permute-done.29.refs_1_), channel_id=1, source_target_pairs={{0,4},{1,3},{4,8},{5,1},{8,12},{9,5},{12,14},{13,9},{14,10},{15,13... | collective-permute-start | bytes 884744 | tf_op jit(solution)/shard_map/ppermute | solution.py:606
  213.1 9.6 %collective-permute-start.20 = (bf16[208,768]{1,0:T(8,128)(2,1)S(1)}, bf16[208,768]{1,0:T(8,128)(2,1)S(1)}, u32[]{:S(2)}, u32[]{:S(2)}) collective-permute-start(bf16[208,768]{1,0:T(8,128)(2,1)S(1)} %pad_maximum_fusion.refs_0_), channel_id=1, source_target_pairs={{0,4},{1,3},{4,8},{5,1},{8,12},{9,5},{12,14},{13,9},{14,10},{15,13... | collective-permute-start | bytes 958472 | tf_op jit(solution)/shard_map/ppermute | solution.py:606
  216.1 9.7 %collective-permute-start.40 = (bf16[192,768]{1,0:T(8,128)(2,1)S(1)}, bf16[192,768]{1,0:T(8,128)(2,1)S(1)}, u32[]{:S(2)}, u32[]{:S(2)}) collective-permute-start(bf16[192,768]{1,0:T(8,128)(2,1)S(1)} %collective-permute-done.39.refs_1_), channel_id=1, source_target_pairs={{0,4},{1,3},{4,8},{5,1},{8,12},{9,5},{12,14},{13,9},{14,10},{15,13... | collective-permute-start | bytes 884744 | tf_op jit(solution)/shard_map/ppermute | solution.py:606
  219.2 9.7 %collective-permute-start.31 = (bf16[192,768]{1,0:T(8,128)(2,1)S(1)}, bf16[192,768]{1,0:T(8,128)(2,1)S(1)}, u32[]{:S(2)}, u32[]{:S(2)}) collective-permute-start(bf16[192,768]{1,0:T(8,128)(2,1)S(1)} %collective-permute-done.30.refs_2_), channel_id=1, source_target_pairs={{0,4},{1,3},{4,8},{5,1},{8,12},{9,5},{12,14},{13,9},{14,10},{15,13... | collective-permute-start | bytes 884744 | tf_op jit(solution)/shard_map/ppermute | solution.py:606
  222.6 9.7 %collective-permute-start.21 = (bf16[208,768]{1,0:T(8,128)(2,1)S(1)}, bf16[208,768]{1,0:T(8,128)(2,1)S(1)}, u32[]{:S(2)}, u32[]{:S(2)}) collective-permute-start(bf16[208,768]{1,0:T(8,128)(2,1)S(1)} %collective-permute-done.20.refs_1_), channel_id=1, source_target_pairs={{0,4},{1,3},{4,8},{5,1},{8,12},{9,5},{12,14},{13,9},{14,10},{15,13... | collective-permute-start | bytes 958472 | tf_op jit(solution)/shard_map/ppermute | solution.py:606
  225.8 9.7 %collective-permute-start.41 = (bf16[192,768]{1,0:T(8,128)(2,1)S(1)}, bf16[192,768]{1,0:T(8,128)(2,1)S(1)}, u32[]{:S(2)}, u32[]{:S(2)}) collective-permute-start(bf16[192,768]{1,0:T(8,128)(2,1)S(1)} %collective-permute-done.40.refs_2_), channel_id=1, source_target_pairs={{0,4},{1,3},{4,8},{5,1},{8,12},{9,5},{12,14},{13,9},{14,10},{15,13... | collective-permute-start | bytes 884744 | tf_op jit(solution)/shard_map/ppermute | solution.py:606
  229.0 9.7 %collective-permute-start.32 = (bf16[192,768]{1,0:T(8,128)(2,1)S(1)}, bf16[192,768]{1,0:T(8,128)(2,1)S(1)}, u32[]{:S(2)}, u32[]{:S(2)}) collective-permute-start(bf16[192,768]{1,0:T(8,128)(2,1)S(1)} %collective-permute-done.31.refs_3_), channel_id=1, source_target_pairs={{0,4},{1,3},{4,8},{5,1},{8,12},{9,5},{12,14},{13,9},{14,10},{15,13... | collective-permute-start | bytes 884744 | tf_op jit(solution)/shard_map/ppermute | solution.py:606
  232.4 9.7 %collective-permute-start.22 = (bf16[208,768]{1,0:T(8,128)(2,1)S(1)}, bf16[208,768]{1,0:T(8,128)(2,1)S(1)}, u32[]{:S(2)}, u32[]{:S(2)}) collective-permute-start(bf16[208,768]{1,0:T(8,128)(2,1)S(1)} %collective-permute-done.21.refs_2_), channel_id=1, source_target_pairs={{0,4},{1,3},{4,8},{5,1},{8,12},{9,5},{12,14},{13,9},{14,10},{15,13... | collective-permute-start | bytes 958472 | tf_op jit(solution)/shard_map/ppermute | solution.py:606
  235.5 9.7 %collective-permute-start.42 = (bf16[192,768]{1,0:T(8,128)(2,1)S(1)}, bf16[192,768]{1,0:T(8,128)(2,1)S(1)}, u32[]{:S(2)}, u32[]{:S(2)}) collective-permute-start(bf16[192,768]{1,0:T(8,128)(2,1)S(1)} %collective-permute-done.41.refs_3_), channel_id=1, source_target_pairs={{0,4},{1,3},{4,8},{5,1},{8,12},{9,5},{12,14},{13,9},{14,10},{15,13... | collective-permute-start | bytes 884744 | tf_op jit(solution)/shard_map/ppermute | solution.py:606
  238.7 9.7 %collective-permute-start.33 = (bf16[192,768]{1,0:T(8,128)(2,1)S(1)}, bf16[192,768]{1,0:T(8,128)(2,1)S(1)}, u32[]{:S(2)}, u32[]{:S(2)}) collective-permute-start(bf16[192,768]{1,0:T(8,128)(2,1)S(1)} %collective-permute-done.32.refs_4_), channel_id=1, source_target_pairs={{0,4},{1,3},{4,8},{5,1},{8,12},{9,5},{12,14},{13,9},{14,10},{15,13... | collective-permute-start | bytes 884744 | tf_op jit(solution)/shard_map/ppermute | solution.py:606
  242.1 9.7 %collective-permute-start.23 = (bf16[208,768]{1,0:T(8,128)(2,1)S(1)}, bf16[208,768]{1,0:T(8,128)(2,1)S(1)}, u32[]{:S(2)}, u32[]{:S(2)}) collective-permute-start(bf16[208,768]{1,0:T(8,128)(2,1)S(1)} %collective-permute-done.22.refs_3_), channel_id=1, source_target_pairs={{0,4},{1,3},{4,8},{5,1},{8,12},{9,5},{12,14},{13,9},{14,10},{15,13... | collective-permute-start | bytes 958472 | tf_op jit(solution)/shard_map/ppermute | solution.py:606
  245.3 9.8 %collective-permute-start.43 = (bf16[192,768]{1,0:T(8,128)(2,1)S(1)}, bf16[192,768]{1,0:T(8,128)(2,1)}, u32[]{:S(2)}, u32[]{:S(2)}) collective-permute-start(bf16[192,768]{1,0:T(8,128)(2,1)S(1)} %collective-permute-done.42.refs_4_), channel_id=1, source_target_pairs={{0,4},{1,3},{4,8},{5,1},{8,12},{9,5},{12,14},{13,9},{14,10},{15,13... | collective-permute-start | bytes 884744 | tf_op jit(solution)/shard_map/ppermute | solution.py:606
  248.4 9.8 %collective-permute-start.34 = (bf16[192,768]{1,0:T(8,128)(2,1)S(1)}, bf16[192,768]{1,0:T(8,128)(2,1)}, u32[]{:S(2)}, u32[]{:S(2)}) collective-permute-start(bf16[192,768]{1,0:T(8,128)(2,1)S(1)} %collective-permute-done.33.refs_5_), channel_id=1, source_target_pairs={{0,4},{1,3},{4,8},{5,1},{8,12},{9,5},{12,14},{13,9},{14,10},{15,13... | collective-permute-start | bytes 884744 | tf_op jit(solution)/shard_map/ppermute | solution.py:606
  251.9 13.5 %collective-permute-start.24 = (bf16[208,768]{1,0:T(8,128)(2,1)S(1)}, bf16[208,768]{1,0:T(8,128)(2,1)S(1)}, u32[]{:S(2)}, u32[]{:S(2)}) collective-permute-start(bf16[208,768]{1,0:T(8,128)(2,1)S(1)} %collective-permute-done.23.refs_4_), channel_id=1, source_target_pairs={{0,4},{1,3},{4,8},{5,1},{8,12},{9,5},{12,14},{13,9},{14,10},{15,13... | collective-permute-start | bytes 958472 | tf_op jit(solution)/shard_map/ppermute | solution.py:606
  255.1 9.7 %collective-permute-start.44 = (bf16[192,768]{1,0:T(8,128)(2,1)}, bf16[192,768]{1,0:T(8,128)(2,1)}, u32[]{:S(2)}, u32[]{:S(2)}) collective-permute-start(bf16[192,768]{1,0:T(8,128)(2,1)} %collective-permute-done.43.refs_5_), channel_id=1, source_target_pairs={{0,4},{1,3},{4,8},{5,1},{8,12},{9,5},{12,14},{13,9},{14,10},{15,13... | collective-permute-start | bytes 884744 | tf_op jit(solution)/shard_map/ppermute | solution.py:606
  258.3 9.7 %collective-permute-start.35 = (bf16[192,768]{1,0:T(8,128)(2,1)}, bf16[192,768]{1,0:T(8,128)(2,1)}, u32[]{:S(2)}, u32[]{:S(2)}) collective-permute-start(bf16[192,768]{1,0:T(8,128)(2,1)} %collective-permute-done.34.refs_6_), channel_id=1, source_target_pairs={{0,4},{1,3},{4,8},{5,1},{8,12},{9,5},{12,14},{13,9},{14,10},{15,13... | collective-permute-start | bytes 884744 | tf_op jit(solution)/shard_map/ppermute | solution.py:606
  264.9 10.9 %collective-permute-start.45 = (bf16[192,768]{1,0:T(8,128)(2,1)}, bf16[192,768]{1,0:T(8,128)(2,1)}, u32[]{:S(2)}, u32[]{:S(2)}) collective-permute-start(bf16[192,768]{1,0:T(8,128)(2,1)} %collective-permute-done.44.refs_6_), channel_id=1, source_target_pairs={{0,4},{1,3},{4,8},{5,1},{8,12},{9,5},{12,14},{13,9},{14,10},{15,13... | collective-permute-start | bytes 884744 | tf_op jit(solution)/shard_map/ppermute | solution.py:606
  265.4 9.9 %collective-permute-start.25 = (bf16[208,768]{1,0:T(8,128)(2,1)S(1)}, bf16[208,768]{1,0:T(8,128)(2,1)S(1)}, u32[]{:S(2)}, u32[]{:S(2)}) collective-permute-start(bf16[208,768]{1,0:T(8,128)(2,1)S(1)} %collective-permute-done.24.refs_5_), channel_id=1, source_target_pairs={{0,4},{1,3},{4,8},{5,1},{8,12},{9,5},{12,14},{13,9},{14,10},{15,13... | collective-permute-start | bytes 958472 | tf_op jit(solution)/shard_map/ppermute | solution.py:606
  275.2 7.0 %collective-permute-start.36 = (bf16[208,768]{1,0:T(8,128)(2,1)S(1)}, bf16[208,768]{1,0:T(8,128)(2,1)S(1)}, u32[]{:S(2)}, u32[]{:S(2)}) collective-permute-start(bf16[208,768]{1,0:T(8,128)(2,1)S(1)} %collective-permute-done.25.refs_6_), channel_id=1, source_target_pairs={{0,4},{1,3},{4,8},{5,1},{8,12},{9,5},{12,14},{13,9},{14,10},{15,13... | collective-permute-start | bytes 958472 | tf_op jit(solution)/shard_map/ppermute | solution.py:606
  (28 other events, 509.2 us)

commit v2 on v1

--- a/solution.py
+++ b/solution.py
@@ -99,6 +99,7 @@
     d_normed_ref,
     sums_ref,
     in_sum_ref,
+    stage_ref,
 ):
     step = pl.program_id(0)
     last = pl.num_programs(0) - 1
@@ -145,21 +146,22 @@
     total_ref[...] += dot_plain(act_ref[...], w_back_ref[...])
     d_normed_ref[...] += dot_back(d_pre_ref[...], w_in_ref[...])
     per_block = block // 192
-    back = dot_across(act_ref[...], cot_ref[...]).astype(jnp.bfloat16)
-    for piece in range(per_block):
-        place_chunk(
-            order_ref[step * per_block + piece],
-            mine_ref,
-            other_ref,
-            back[piece * 192 : piece * 192 + 192],
-            slice(0, 192),
-        )
-    inward = dot_plain(turned_ref[...], d_pre_ref[...]).astype(jnp.bfloat16)
     at_rows = pl.ds(pl.multiple_of(192 + step * 48, 16), 48)
-    for piece in range(16):
-        place_chunk(
-            order_ref[piece], mine_ref, other_ref, inward[piece * 48 : piece * 48 + 48], at_rows
-        )
+    stage_ref[0] = dot_across(act_ref[...], cot_ref[...]).astype(jnp.bfloat16)
+    stage_ref[1] = dot_plain(turned_ref[...], d_pre_ref[...]).astype(jnp.bfloat16)
+
+    def place_back(piece, carry):
+        value = stage_ref[0, pl.ds(pl.multiple_of(piece * 192, 16), 192), :]
+        place_chunk(order_ref[step * per_block + piece], mine_ref, other_ref, value, slice(0, 192))
+        return carry
+
+    def place_in(piece, carry):
+        value = stage_ref[1, pl.ds(pl.multiple_of(piece * 48, 16), 48), :]
+        place_chunk(order_ref[piece], mine_ref, other_ref, value, at_rows)
+        return carry
+
+    lax.fori_loop(0, per_block, place_back, 0)
+    lax.fori_loop(0, 16, place_in, 0)
     in_sum = jnp.sum(in_sum_ref[...], axis=0, keepdims=True)
     side = step // 2
     row = 8 + 2 * (step % 2)
@@ -225,7 +227,7 @@
                 vmem((rows, block), f32), vmem((rows, block), f32),
                 vmem((rows, block), bf16), vmem((rows, block), bf16),
                 vmem((rows, width), f32), vmem((rows, width), f32),
-                vmem((4, 8, width), f32), vmem((8, block), f32),
+                vmem((4, 8, width), f32), vmem((8, block), f32), vmem((2, width, width), bf16),
             ],
         ),
         compiler_params=pltpu.CompilerParams(vmem_limit_bytes=60 << 20),
@@ -661,6 +663,10 @@
         unringed_rows(rest[:, 144:]),
     )
     return [own_share(weight) for weight in weights], [own_share(vector) for vector in vectors]
+
+
+LAST_STEP = 3
+LAST_SPAN = 1
 
 
 class Ordered:
@@ -765,12 +771,11 @@
         feed.reduce()
         rest = Ring(queue, rest_mine, rest_other)
     side = lax.axis_index("dp").reshape(1)
-    g_tokens, *small = last_call(
-        side if ringed else jnp.zeros_like(side), tokens[0], ln1_gain, w_qkv[0], queue.after(d_middle), d_queries, backs, diagonals, small
-    )
+    if not ringed:
+        g_tokens, *small = last_call(
+            jnp.zeros_like(side), tokens[0], ln1_gain, w_qkv[0], d_middle, d_queries, backs, diagonals, small
+        )
     if ringed:
-        queue.mark = g_tokens
-        feed.reduce()
         rest.reduce()
         queue.free = True
         held_parts = []
@@ -793,7 +798,14 @@
             return value
 
         while rest.step < RING:
+            if rest.step == LAST_STEP + LAST_SPAN:
+                rest.arrived, g_tokens = lax.optimization_barrier((rest.arrived, g_tokens))
             rest_held = rest.reduce()
+            if rest.step == LAST_STEP:
+                ready = lax.optimization_barrier((d_middle, rest_held))[0]
+                g_tokens, *small = last_call(
+                    side, tokens[0], ln1_gain, w_qkv[0], ready, d_queries, backs, diagonals, small
+                )
         small_held = add_low(small[0], lax.ppermute(small[1], "dp", [(0, 1), (1, 0)]))
         rest_held = jnp.concatenate([rest_held, small_held], axis=0)
         rest_chunks = gather(rest_held, {6: back_turn, 7: in_turn})

time: 288 us -> 282 us (0.979)
  waiting for transfers between devices: 112 us -> 102 us
  other arithmetic: 14.2 us -> 18.2 us
    ppermute x37 -> x38, waiting for transfers between devices: 90.8 us -> 78.3 us  [ring_send(): return lax.ppermute(chunk, ('group', 'dp'), pairs)]
    ppermute x2, waiting for transfers between devices: 0.01 us -> 4.19 us  [__init__(): self.met = lax.ppermute(order.after(other), 'dp', [(0, 1), (1, 0)])]
    convert_element_type x17, other arithmetic: 12.4 us -> 16.4 us  [add_low(): sum((term.astype(jnp.float32) for term in terms)).astype(jnp.bfloat16)]
    ppermute x37 -> x38, starting transfers between devices: 29.6 us -> 31.2 us  [ring_send(): return lax.ppermute(chunk, ('group', 'dp'), pairs)]
  transfers between devices with their start and end apart: 46 -> 47, of which waited for: 35 -> 34; matrix products, arithmetic and copies ran while one was open for 4% -> 6% of each run, Pallas kernels for 24% -> 25%
where the time goes in v2:
time: 282 us; the launch traced here: 281 us
  Pallas kernels  116 us (41%)
  waiting for transfers between devices  102 us (36%)
  starting transfers between devices  40.2 us (14%)
  other arithmetic  18.2 us (6%)
  local copies, waits for them, and re-layouts  4.03 us (1%)
    pallas_call x13, Pallas kernels, kernel_call(): pl.pallas_call(kernel, out_shape=tuple(outs), in_specs=specs, out_specs=t...  85.4 us
    ppermute x38, waiting for transfers between devices, ring_send(): return lax.ppermute(chunk, ('group', 'dp'), pairs)  78.3 us
    ppermute x38, starting transfers between devices, ring_send(): return lax.ppermute(chunk, ('group', 'dp'), pairs)  31.2 us
    pallas_call x1, Pallas kernels, feed_call(): pl.pallas_call(feed_kernel, out_shape=(wide(bf16), wide(f32), wide(bf16),...  30.2 us
    ppermute x6, waiting for transfers between devices, partner_2(): lax.ppermute(shard, axis, [(i, i ^ 1 << distance) for i in range(lax.axis...  19.9 us
    convert_element_type x17, other arithmetic, add_low(): sum((term.astype(jnp.float32) for term in terms)).astype(jnp.bfloat16)  16.4 us
    ppermute x6, starting transfers between devices, partner_2(): lax.ppermute(shard, axis, [(i, i ^ 1 << distance) for i in range(lax.axis...  8.82 us
  transfers between devices with their start and end apart: 47, of which 34 were waited for; matrix products, arithmetic and copies ran while one was open for 6% of the time, Pallas kernels for 25%

profile of v2, /device:TPU:0, one launch (start us, length us, event | category | flops | bytes accessed | tf_op | source)
XLA Modules:
  0.0 281.4 jit_solution(1783930444550751418)
XLA Ops:
  0.7 4.7 %first.1 = (bf16[512,768]{1,0:T(8,128)(2,1)}, bf16[2,512,256]{2,1,0:T(8,128)(2,1)}, bf16[2,512,256]{2,1,0:T(8,128)(2,1)}, bf16[2,512,256]{2,1,0:T(8,128)(2,1)}) custom-call(bf16[512,768]{1,0:T(8,128)(2,1)} %bitcast.171, f32[1,768]{1,0:T(1,128)} %gain_ref.5, f32[1,768]{1,0:T(1,128)} %shift_ref.2, bf16[768,2304]{1,0:T(8,128)(2,1)} %bitcast.166, f32[1,768]{1,0:T(1,128)} %bias_ref.2), custom_call_target="tpu_custom_call" | custom-call | flops 5000000000 | tf_op jit(solution)/shard_map/first/pallas_call | solution.py:267
  5.4 3.0 %collective-permute-start = (bf16[2,512,256]{2,1,0:T(8,128)(2,1)}, bf16[2,512,256]{2,1,0:T(8,128)(2,1)S(1)}, u32[]{:S(2)}, u32[]{:S(2)}) collective-permute-start(bf16[2,512,256]{2,1,0:T(8,128)(2,1)} %get-tuple-element.88), channel_id=1, source_target_pairs={{0,16},{16,0},{1,17},{17,1},{2,18},{18,2},{3,19},{19,3},{4,20},{20... | collective-permute-start | bytes 1572872 | tf_op jit(solution)/shard_map/ppermute | solution.py:598
  8.4 2.0 collective-permute-start.2
  11.6 5.3 %prep.1 = (bf16[512,768]{1,0:T(8,128)(2,1)}, bf16[512,384]{1,0:T(8,128)(2,1)}, bf16[512,384]{1,0:T(8,128)(2,1)}, bf16[512,384]{1,0:T(8,128)(2,1)}, s32[1,512]{1,0:T(1,128)}, /*index=5*/bf16[36,128,128]{2,1,0:T(8,128)(2,1)}) custom-call(s32[1]{0:T(128)} %bitcast.1.stream_ref, s32[2,2,1,512]{3,2,1,0:T(1,128)} %box_ref.1, s32[2,1,512]{2,1,0:T(1,128)} %segment_ref.1, ...), custom_call_target="tpu_custom_call" | custom-call | flops 5000000000 | tf_op jit(solution)/shard_map/prep/pallas_call | solution.py:267
  16.9 4.5 %collective-permute-done.pair_ref = bf16[2,512,256]{2,1,0:T(8,128)(2,1)S(1)} collective-permute-done((bf16[2,512,256]{2,1,0:T(8,128)(2,1)}, bf16[2,512,256]{2,1,0:T(8,128)(2,1)S(1)}, u32[]{:S(2)}, u32[]{:S(2)}) %collective-permute-start) | collective-permute-done | bytes 524320 | tf_op jit(solution)/shard_map/ppermute | solution.py:598
  22.2 7.3 %attend_0.1 = (bf16[512,256]{1,0:T(8,128)(2,1)}, bf16[4,512,512]{2,1,0:T(8,128)(2,1)}) custom-call(bf16[512,768]{1,0:T(8,128)(2,1)} %get-tuple-element.87.queries_ref, bf16[2,512,256]{2,1,0:T(8,128)(2,1)} %copy-done.12, bf16[512,384]{1,0:T(8,128)(2,1)} %get-tuple-element.89.hot_ref, bf16[512,384]{1,0:T(8,128)(2,1)} %get-tuple-element.90.key_hot_ref, ...), custom_call_target="tpu_custom_call" | custom-call | flops 7000000000 | tf_op jit(solution)/shard_map/attend_0/pallas_call | solution.py:267
  29.5 3.1 %collective-permute-done.1.pair_ref = bf16[2,512,256]{2,1,0:T(8,128)(2,1)S(1)} collective-permute-done((bf16[2,512,256]{2,1,0:T(8,128)(2,1)}, bf16[2,512,256]{2,1,0:T(8,128)(2,1)S(1)}, u32[]{:S(2)}, u32[]{:S(2)}) %collective-permute-start.1) | collective-permute-done | bytes 524320 | tf_op jit(solution)/shard_map/ppermute | solution.py:598
  33.4 7.3 %attend_1.1 = (bf16[512,256]{1,0:T(8,128)(2,1)}, bf16[4,512,512]{2,1,0:T(8,128)(2,1)}) custom-call(bf16[512,768]{1,0:T(8,128)(2,1)} %get-tuple-element.87.queries_ref, bf16[2,512,256]{2,1,0:T(8,128)(2,1)} %copy-done.10, bf16[512,384]{1,0:T(8,128)(2,1)} %get-tuple-element.89.hot_ref, bf16[512,384]{1,0:T(8,128)(2,1)} %get-tuple-element.90.key_hot_ref, ...), custom_call_target="tpu_custom_call" | custom-call | flops 7000000000 | tf_op jit(solution)/shard_map/attend_1/pallas_call | solution.py:267
  40.7 2.2 collective-permute-done.2.pair_ref
  43.8 7.3 %attend_2.1 = (bf16[512,256]{1,0:T(8,128)(2,1)}, bf16[4,512,512]{2,1,0:T(8,128)(2,1)}) custom-call(bf16[512,768]{1,0:T(8,128)(2,1)} %get-tuple-element.87.queries_ref, bf16[2,512,256]{2,1,0:T(8,128)(2,1)} %copy-done.9, bf16[512,384]{1,0:T(8,128)(2,1)} %get-tuple-element.89.hot_ref, bf16[512,384]{1,0:T(8,128)(2,1)} %get-tuple-element.90.key_hot_ref, ...), custom_call_target="tpu_custom_call" | custom-call | flops 7000000000 | tf_op jit(solution)/shard_map/attend_2/pallas_call | solution.py:267
  51.1 30.2 %feed.1 = (bf16[512,768]{1,0:T(8,128)(2,1)}, f32[512,768]{1,0:T(8,128)}, bf16[512,768]{1,0:T(8,128)(2,1)}, bf16[512,768]{1,0:T(8,128)(2,1)}, bf16[8,384,768]{2,1...) custom-call(s32[16]{0:T(128)} %fusion.21.order_ref, bf16[512,768]{1,0:T(8,128)(2,1)} %bitcast.172, ...), custom_call_target="tpu_custom_call" | custom-call | flops 30000001024 | tf_op jit(solution)/shard_map/feed/pallas_call | solution.py:207
  81.3 8.1 %attend_back_0.1 = (bf16[512,256]{1,0:T(8,128)(2,1)}, bf16[2,512,256]{2,1,0:T(8,128)(2,1)}, f32[3,4,256]{2,1,0:T(4,128)}) custom-call(bf16[512,768]{1,0:T(8,128)(2,1)} %get-tuple-element.87.queries_ref, bf16[2,512,256]{2,1,0:T(8,128)(2,1)} %copy-done.12, bf16[512,384]{1,0:T(8,128)(2,1)} %get-tuple-element.104.turned_hot_ref, ...), custom_call_target="tpu_custom_call" | custom-call | flops 8000000000 | tf_op jit(solution)/shard_map/attend_back_0/pallas_call | solution.py:267
  89.4 1.7 collective-permute-start.6
  92.5 1.6 collective-permute-start.4
  94.2 8.1 %attend_back_1.1 = (bf16[512,256]{1,0:T(8,128)(2,1)}, bf16[2,512,256]{2,1,0:T(8,128)(2,1)}, f32[3,4,256]{2,1,0:T(4,128)}) custom-call(bf16[512,768]{1,0:T(8,128)(2,1)} %get-tuple-element.87.queries_ref, bf16[2,512,256]{2,1,0:T(8,128)(2,1)} %copy-done.10, bf16[512,384]{1,0:T(8,128)(2,1)} %get-tuple-element.104.turned_hot_ref, ...), custom_call_target="tpu_custom_call" | custom-call | flops 8000000000 | tf_op jit(solution)/shard_map/attend_back_1/pallas_call | solution.py:267
  104.2 1.6 collective-permute-start.5
  105.9 8.2 %attend_back_2.1 = (bf16[512,256]{1,0:T(8,128)(2,1)}, bf16[2,512,256]{2,1,0:T(8,128)(2,1)}, f32[3,4,256]{2,1,0:T(4,128)}) custom-call(bf16[512,768]{1,0:T(8,128)(2,1)} %get-tuple-element.87.queries_ref, bf16[2,512,256]{2,1,0:T(8,128)(2,1)} %copy-done.9, bf16[512,384]{1,0:T(8,128)(2,1)} %get-tuple-element.104.turned_hot_ref, ...), custom_call_target="tpu_custom_call" | custom-call | flops 8000000000 | tf_op jit(solution)/shard_map/attend_back_2/pallas_call | solution.py:267
  118.8 10.0 %collective-permute-done.8.back_2_ref = bf16[2,512,256]{2,1,0:T(8,128)(2,1)S(1)} collective-permute-done((bf16[2,512,256]{2,1,0:T(8,128)(2,1)S(1)}, bf16[2,512,256]{2,1,0:T(8,128)(2,1)S(1)}, u32[]{:S(2)}, u32[]{:S(2)}) %collective-permute-start.8) | collective-permute-done | bytes 524320 | tf_op jit(solution)/shard_map/ppermute | solution.py:598
  129.7 9.4 %weights.1 = (bf16[8,192,768]{2,1,0:T(8,128)(2,1)}, bf16[8,192,768]{2,1,0:T(8,128)(2,1)}) custom-call(s32[16]{0:T(128)} %fusion.21.order_ref, bf16[512,768]{1,0:T(8,128)(2,1)} %get-tuple-element.120.normed_ref, bf16[512,768]{1,0:T(8,128)(2,1)} %get-tuple-element.121.d_branch_ref, bf16[512,256]{1,0:T(8,128)(2,1)} %get-tuple-element.93.context_0_ref, ...), custom_call_target="tpu_custom_call" | custom-call | flops 7000000000 | tf_op jit(solution)/shard_map/weights/pallas_call | solution.py:267
  141.3 4.2 %collective-permute-done.10 = bf16[8,192,768]{2,1,0:T(8,128)(2,1)S(1)} collective-permute-done((bf16[8,192,768]{2,1,0:T(8,128)(2,1)}, bf16[8,192,768]{2,1,0:T(8,128)(2,1)S(1)}, u32[]{:S(2)}, u32[]{:S(2)}) %collective-permute-start.10) | collective-permute-done | bytes 2359328 | tf_op jit(solution)/shard_map/ppermute | solution.py:689
  146.1 7.7 %collective-permute-done.11 = bf16[192,768]{1,0:T(8,128)(2,1)S(1)} collective-permute-done((bf16[192,768]{1,0:T(8,128)(2,1)S(1)}, bf16[192,768]{1,0:T(8,128)(2,1)S(1)}, u32[]{:S(2)}, u32[]{:S(2)}) %collective-permute-start.11) | collective-permute-done | bytes 294944 | tf_op jit(solution)/shard_map/ppermute | solution.py:608
  161.4 2.5 collective-permute-done.37
  163.9 3.2 %collective-permute-done.26 = bf16[192,768]{1,0:T(8,128)(2,1)S(1)} collective-permute-done((bf16[192,768]{1,0:T(8,128)(2,1)S(1)}, bf16[192,768]{1,0:T(8,128)(2,1)S(1)}, u32[]{:S(2)}, u32[]{:S(2)}) %collective-permute-start.26) | collective-permute-done | bytes 294944 | tf_op jit(solution)/shard_map/ppermute | solution.py:608
  170.7 1.6 collective-permute-start.14
  172.3 7.5 %last.1 = (bf16[512,768]{1,0:T(8,128)(2,1)}, f32[16,768]{1,0:T(8,128)}, f32[16,768]{1,0:T(8,128)}) custom-call(s32[1]{0:T(128)} %bitcast.22.side_ref, bf16[512,768]{1,0:T(8,128)(2,1)} %bitcast.173, f32[1,768]{1,0:T(1,128)} %gain_ref.5, bf16[768,2304]{1,0:T(8,128)(2,1)} %bitcast.168, f32[512,768]{1,0:T(8,128)} %get-tuple-element.130.d_middle_ref, ...), custom_call_target="tpu_custom_call" | custom-call | flops 8000000000 | tf_op jit(solution)/shard_map/last/pallas_call | solution.py:267
  179.8 1.8 collective-permute-done.14
  192.6 3.2 %collective-permute-done.28 = bf16[192,768]{1,0:T(8,128)(2,1)S(1)} collective-permute-done((bf16[192,768]{1,0:T(8,128)(2,1)S(1)}, bf16[192,768]{1,0:T(8,128)(2,1)S(1)}, u32[]{:S(2)}, u32[]{:S(2)}) %collective-permute-start.28) | collective-permute-done | bytes 294944 | tf_op jit(solution)/shard_map/ppermute | solution.py:608
  202.1 1.9 collective-permute-done.29.refs_1_
  204.5 2.6 collective-permute-done.17
  210.8 2.7 collective-permute-done.30.refs_2_
  214.0 2.9 %collective-permute-done.19.refs_1_ = bf16[208,768]{1,0:T(8,128)(2,1)S(1)} collective-permute-done((bf16[208,768]{1,0:T(8,128)(2,1)S(1)}, bf16[208,768]{1,0:T(8,128)(2,1)S(1)}, u32[]{:S(2)}, u32[]{:S(2)}) %collective-permute-start.19) | collective-permute-done | bytes 319520 | tf_op jit(solution)/shard_map/ppermute | solution.py:608
  217.4 2.7 collective-permute-done.41.refs_2_
  220.6 2.7 collective-permute-done.31.refs_3_
  223.7 2.9 %collective-permute-done.20.refs_2_ = bf16[208,768]{1,0:T(8,128)(2,1)S(1)} collective-permute-done((bf16[208,768]{1,0:T(8,128)(2,1)S(1)}, bf16[208,768]{1,0:T(8,128)(2,1)S(1)}, u32[]{:S(2)}, u32[]{:S(2)}) %collective-permute-start.20) | collective-permute-done | bytes 319520 | tf_op jit(solution)/shard_map/ppermute | solution.py:608
  227.1 2.7 collective-permute-done.42.refs_3_
  230.3 2.7 collective-permute-done.32.refs_4_
  233.5 2.9 %collective-permute-done.21.refs_3_ = bf16[208,768]{1,0:T(8,128)(2,1)S(1)} collective-permute-done((bf16[208,768]{1,0:T(8,128)(2,1)S(1)}, bf16[208,768]{1,0:T(8,128)(2,1)S(1)}, u32[]{:S(2)}, u32[]{:S(2)}) %collective-permute-start.21) | collective-permute-done | bytes 319520 | tf_op jit(solution)/shard_map/ppermute | solution.py:608
  236.9 2.7 collective-permute-done.43.refs_4_
  240.0 2.7 collective-permute-done.33.refs_5_
  243.2 2.9 %collective-permute-done.22.refs_4_ = bf16[208,768]{1,0:T(8,128)(2,1)S(1)} collective-permute-done((bf16[208,768]{1,0:T(8,128)(2,1)S(1)}, bf16[208,768]{1,0:T(8,128)(2,1)S(1)}, u32[]{:S(2)}, u32[]{:S(2)}) %collective-permute-start.22) | collective-permute-done | bytes 319520 | tf_op jit(solution)/shard_map/ppermute | solution.py:608
  246.6 2.8 collective-permute-done.44.refs_5_
  249.9 2.7 collective-permute-done.34.refs_6_
  253.6 5.5 %collective-permute-done.45.refs_6_ = bf16[192,768]{1,0:T(8,128)(2,1)} collective-permute-done((bf16[192,768]{1,0:T(8,128)(2,1)}, bf16[192,768]{1,0:T(8,128)(2,1)}, u32[]{:S(2)}, u32[]{:S(2)}) %collective-permute-start.45) | collective-permute-done | bytes 294944 | tf_op jit(solution)/shard_map/ppermute | solution.py:608
  262.3 4.1 %open_back.1 = f32[1536,768]{1,0:T(8,128)} custom-call(s32[8]{0:T(128)} %and_select_fusion.place_ref, bf16[192,768]{1,0:T(8,128)(2,1)} %copy-done.4, bf16[192,768]{1,0:T(8,128)(2,1)} %copy-done.21, bf16[192,768]{1,0:T(8,128)(2,1)} %copy-done.23, bf16[192,768]{1,0:T(8,128)(2,1)} %copy-done.26, bf16[192,768]{1,0:T(8,128)(2,1)} %copy-done.28, ...), custom_call_target="tpu_custom_call" | custom-call | flops 4000000000 | tf_op jit(solution)/shard_map/open_back/pallas_call | solution.py:267
  266.5 3.0 %collective-permute-done.24.refs_6_ = bf16[208,768]{1,0:T(8,128)(2,1)S(1)} collective-permute-done((bf16[208,768]{1,0:T(8,128)(2,1)S(1)}, bf16[208,768]{1,0:T(8,128)(2,1)S(1)}, u32[]{:S(2)}, u32[]{:S(2)}) %collective-permute-start.24) | collective-permute-done | bytes 319520 | tf_op jit(solution)/shard_map/ppermute | solution.py:608
  270.0 4.1 %open_inward.1 = f32[384,3072]{1,0:T(8,128)} custom-call(s32[8]{0:T(128)} %and_select_fusion.place_ref, bf16[192,768]{1,0:T(8,128)(2,1)} %copy-done.3, bf16[192,768]{1,0:T(8,128)(2,1)} %copy-done.22, bf16[192,768]{1,0:T(8,128)(2,1)} %copy-done.24, bf16[192,768]{1,0:T(8,128)(2,1)} %copy-done.25, bf16[192,768]{1,0:T(8,128)(2,1)} %copy-done.27, ...), custom_call_target="tpu_custom_call" | custom-call | flops 4000000000 | tf_op jit(solution)/shard_map/open_inward/pallas_call | solution.py:267
  274.1 2.4 collective-permute-done.36.refs_7_
  277.2 4.0 %open_rest.1 = (f32[384,2304]{1,0:T(8,128)}, f32[384,768]{1,0:T(8,128)}, f32[1,384]{1,0:T(1,128)}, f32[1,384]{1,0:T(1,128)}, f32[1,384]{1,0:T(1,128)}, /*index=5...) custom-call(s32[8]{0:T(128)} %and_select_fusion.place_ref, ...), custom_call_target="tpu_custom_call" | custom-call | flops 4000000000 | tf_op jit(solution)/shard_map/open_rest/pallas_call | solution.py:267
  (143 shorter events, 59.4 us)
Async XLA Ops:
  5.4 15.9 %collective-permute-start = (bf16[2,512,256]{2,1,0:T(8,128)(2,1)}, bf16[2,512,256]{2,1,0:T(8,128)(2,1)S(1)}, u32[]{:S(2)}, u32[]{:S(2)}) collective-permute-start(bf16[2,512,256]{2,1,0:T(8,128)(2,1)} %get-tuple-element.88), channel_id=1, source_target_pairs={{0,16},{16,0},{1,17},{17,1},{2,18},{18,2},{3,19},{19,3},{4,20},{20... | collective-permute-start | bytes 1572872 | tf_op jit(solution)/shard_map/ppermute | solution.py:598
  8.4 24.2 %collective-permute-start.1 = (bf16[2,512,256]{2,1,0:T(8,128)(2,1)}, bf16[2,512,256]{2,1,0:T(8,128)(2,1)S(1)}, u32[]{:S(2)}, u32[]{:S(2)}) collective-permute-start(bf16[2,512,256]{2,1,0:T(8,128)(2,1)} %get-tuple-element.94), channel_id=1, source_target_pairs={{0,16},{16,0},{1,17},{17,1},{2,18},{18,2},{3,19},{19,3},{4,20},{20... | collective-permute-start | bytes 1572872 | tf_op jit(solution)/shard_map/ppermute | solution.py:598
  8.4 34.6 %collective-permute-start.2 = (bf16[2,512,256]{2,1,0:T(8,128)(2,1)}, bf16[2,512,256]{2,1,0:T(8,128)(2,1)S(1)}, u32[]{:S(2)}, u32[]{:S(2)}) collective-permute-start(bf16[2,512,256]{2,1,0:T(8,128)(2,1)} %get-tuple-element.97), channel_id=1, source_target_pairs={{0,16},{16,0},{1,17},{17,1},{2,18},{18,2},{3,19},{19,3},{4,20},{20... | collective-permute-start | bytes 1572872 | tf_op jit(solution)/shard_map/ppermute | solution.py:598
  81.3 9.9 %collective-permute-start.3 = (bf16[8,384,768]{2,1,0:T(8,128)(2,1)}, bf16[8,384,768]{2,1,0:T(8,128)(2,1)}, u32[]{:S(2)}, u32[]{:S(2)}) collective-permute-start(bf16[8,384,768]{2,1,0:T(8,128)(2,1)} %get-tuple-element.103), channel_id=1, source_target_pairs={{0,1},{1,0},{2,3},{3,2},{4,5},{5,4},{6,7},{7,6},{8,9},{9,8},{10,11... | collective-permute-start | bytes 14155784 | tf_op jit(solution)/shard_map/ppermute | solution.py:689
  89.4 16.5 %collective-permute-start.6 = (bf16[2,512,256]{2,1,0:T(8,128)(2,1)}, bf16[2,512,256]{2,1,0:T(8,128)(2,1)S(1)}, u32[]{:S(2)}, u32[]{:S(2)}) collective-permute-start(bf16[2,512,256]{2,1,0:T(8,128)(2,1)} %get-tuple-element.115), channel_id=1, source_target_pairs={{0,16},{16,0},{1,17},{17,1},{2,18},{18,2},{3,19},{19,3},{4,20},{20... | collective-permute-start | bytes 1572872 | tf_op jit(solution)/shard_map/ppermute | solution.py:598
  92.5 10.3 %collective-permute-start.4 = (bf16[384,768]{1,0:T(8,128)(2,1)S(1)}, bf16[384,768]{1,0:T(8,128)(2,1)S(1)}, u32[]{:S(2)}, u32[]{:S(2)}) collective-permute-start(bf16[384,768]{1,0:T(8,128)(2,1)S(1)} %fusion.3), channel_id=1, source_target_pairs={{0,4},{1,3},{4,8},{5,1},{8,12},{9,5},{12,14},{13,9},{14,10},{15,13... | collective-permute-start | bytes 1769480 | tf_op jit(solution)/shard_map/ppermute | solution.py:608
  102.2 16.6 %collective-permute-start.7 = (bf16[2,512,256]{2,1,0:T(8,128)(2,1)}, bf16[2,512,256]{2,1,0:T(8,128)(2,1)S(1)}, u32[]{:S(2)}, u32[]{:S(2)}) collective-permute-start(bf16[2,512,256]{2,1,0:T(8,128)(2,1)} %get-tuple-element.119), channel_id=1, source_target_pairs={{0,16},{16,0},{1,17},{17,1},{2,18},{18,2},{3,19},{19,3},{4,20},{20... | collective-permute-start | bytes 1572872 | tf_op jit(solution)/shard_map/ppermute | solution.py:598
  104.2 9.9 %collective-permute-start.5 = (bf16[384,768]{1,0:T(8,128)(2,1)S(1)}, bf16[384,768]{1,0:T(8,128)(2,1)S(1)}, u32[]{:S(2)}, u32[]{:S(2)}) collective-permute-start(bf16[384,768]{1,0:T(8,128)(2,1)S(1)} %fusion.2), channel_id=1, source_target_pairs={{0,4},{1,3},{4,8},{5,1},{8,12},{9,5},{12,14},{13,9},{14,10},{15,13... | collective-permute-start | bytes 1769480 | tf_op jit(solution)/shard_map/ppermute | solution.py:608
  115.7 13.2 %collective-permute-start.8 = (bf16[2,512,256]{2,1,0:T(8,128)(2,1)S(1)}, bf16[2,512,256]{2,1,0:T(8,128)(2,1)S(1)}, u32[]{:S(2)}, u32[]{:S(2)}) collective-permute-start(bf16[2,512,256]{2,1,0:T(8,128)(2,1)S(1)} %copy-done.13), channel_id=1, source_target_pairs={{0,16},{16,0},{1,17},{17,1},{2,18},{18,2},{3,19},{19,3},{4,20},{20... | collective-permute-start | bytes 1572872 | tf_op jit(solution)/shard_map/ppermute | solution.py:598
  117.3 21.8 %collective-permute-start.9 = (bf16[384,768]{1,0:T(8,128)(2,1)S(1)}, bf16[384,768]{1,0:T(8,128)(2,1)S(1)}, u32[]{:S(2)}, u32[]{:S(2)}) collective-permute-start(bf16[384,768]{1,0:T(8,128)(2,1)S(1)} %fusion.1), channel_id=1, source_target_pairs={{0,4},{1,3},{4,8},{5,1},{8,12},{9,5},{12,14},{13,9},{14,10},{15,13... | collective-permute-start | bytes 1769480 | tf_op jit(solution)/shard_map/ppermute | solution.py:608
  140.7 4.8 %collective-permute-start.10 = (bf16[8,192,768]{2,1,0:T(8,128)(2,1)}, bf16[8,192,768]{2,1,0:T(8,128)(2,1)S(1)}, u32[]{:S(2)}, u32[]{:S(2)}) collective-permute-start(bf16[8,192,768]{2,1,0:T(8,128)(2,1)} %get-tuple-element.127), channel_id=1, source_target_pairs={{0,1},{1,0},{2,3},{3,2},{4,5},{5,4},{6,7},{7,6},{8,9},{9,8},{10,11... | collective-permute-start | bytes 7077896 | tf_op jit(solution)/shard_map/ppermute | solution.py:689
  140.7 13.8 %collective-permute-start.25 = (bf16[384,768]{1,0:T(8,128)(2,1)S(1)}, bf16[384,768]{1,0:T(8,128)(2,1)S(1)}, u32[]{:S(2)}, u32[]{:S(2)}) collective-permute-start(bf16[384,768]{1,0:T(8,128)(2,1)S(1)} %fusion), channel_id=1, source_target_pairs={{0,4},{1,3},{4,8},{5,1},{8,12},{9,5},{12,14},{13,9},{14,10},{15,13... | collective-permute-start | bytes 1769480 | tf_op jit(solution)/shard_map/ppermute | solution.py:608
  145.5 8.3 %collective-permute-start.11 = (bf16[192,768]{1,0:T(8,128)(2,1)S(1)}, bf16[192,768]{1,0:T(8,128)(2,1)S(1)}, u32[]{:S(2)}, u32[]{:S(2)}) collective-permute-start(bf16[192,768]{1,0:T(8,128)(2,1)S(1)} %fusion.19), channel_id=1, source_target_pairs={{0,4},{1,3},{4,8},{5,1},{8,12},{9,5},{12,14},{13,9},{14,10},{15,13... | collective-permute-start | bytes 884744 | tf_op jit(solution)/shard_map/ppermute | solution.py:608
  153.9 6.8 %collective-permute-start.12 = (bf16[192,768]{1,0:T(8,128)(2,1)S(1)}, bf16[192,768]{1,0:T(8,128)(2,1)S(1)}, u32[]{:S(2)}, u32[]{:S(2)}) collective-permute-start(bf16[192,768]{1,0:T(8,128)(2,1)S(1)} %fusion.18), channel_id=1, source_target_pairs={{0,4},{1,3},{4,8},{5,1},{8,12},{9,5},{12,14},{13,9},{14,10},{15,13... | collective-permute-start | bytes 884744 | tf_op jit(solution)/shard_map/ppermute | solution.py:608
  155.9 7.9 %collective-permute-start.37 = (bf16[192,768]{1,0:T(8,128)(2,1)S(1)}, bf16[192,768]{1,0:T(8,128)(2,1)S(1)}, u32[]{:S(2)}, u32[]{:S(2)}) collective-permute-start(bf16[192,768]{1,0:T(8,128)(2,1)S(1)} %get-tuple-element.156), channel_id=1, source_target_pairs={{0,4},{1,3},{4,8},{5,1},{8,12},{9,5},{12,14},{13,9},{14,10},{15,13... | collective-permute-start | bytes 884744 | tf_op jit(solution)/shard_map/ppermute | solution.py:608
  157.5 9.5 %collective-permute-start.26 = (bf16[192,768]{1,0:T(8,128)(2,1)S(1)}, bf16[192,768]{1,0:T(8,128)(2,1)S(1)}, u32[]{:S(2)}, u32[]{:S(2)}) collective-permute-start(bf16[192,768]{1,0:T(8,128)(2,1)S(1)} %get-tuple-element.157), channel_id=1, source_target_pairs={{0,4},{1,3},{4,8},{5,1},{8,12},{9,5},{12,14},{13,9},{14,10},{15,13... | collective-permute-start | bytes 884744 | tf_op jit(solution)/shard_map/ppermute | solution.py:608
  160.8 9.7 %collective-permute-start.13 = (bf16[192,768]{1,0:T(8,128)(2,1)S(1)}, bf16[192,768]{1,0:T(8,128)(2,1)S(1)}, u32[]{:S(2)}, u32[]{:S(2)}) collective-permute-start(bf16[192,768]{1,0:T(8,128)(2,1)S(1)} %fusion.17), channel_id=1, source_target_pairs={{0,4},{1,3},{4,8},{5,1},{8,12},{9,5},{12,14},{13,9},{14,10},{15,13... | collective-permute-start | bytes 884744 | tf_op jit(solution)/shard_map/ppermute | solution.py:608
  168.5 14.7 %collective-permute-start.38 = (bf16[192,768]{1,0:T(8,128)(2,1)S(1)}, bf16[192,768]{1,0:T(8,128)(2,1)S(1)}, u32[]{:S(2)}, u32[]{:S(2)}) collective-permute-start(bf16[192,768]{1,0:T(8,128)(2,1)S(1)} %get-tuple-element.162), channel_id=1, source_target_pairs={{0,4},{1,3},{4,8},{5,1},{8,12},{9,5},{12,14},{13,9},{14,10},{15,13... | collective-permute-start | bytes 884744 | tf_op jit(solution)/shard_map/ppermute | solution.py:608
  169.0 14.2 %collective-permute-start.27 = (bf16[192,768]{1,0:T(8,128)(2,1)S(1)}, bf16[192,768]{1,0:T(8,128)(2,1)S(1)}, u32[]{:S(2)}, u32[]{:S(2)}) collective-permute-start(bf16[192,768]{1,0:T(8,128)(2,1)S(1)} %get-tuple-element.163), channel_id=1, source_target_pairs={{0,4},{1,3},{4,8},{5,1},{8,12},{9,5},{12,14},{13,9},{14,10},{15,13... | collective-permute-start | bytes 884744 | tf_op jit(solution)/shard_map/ppermute | solution.py:608
  170.7 10.9 %collective-permute-start.14 = (bf16[192,768]{1,0:T(8,128)(2,1)S(1)}, bf16[192,768]{1,0:T(8,128)(2,1)S(1)}, u32[]{:S(2)}, u32[]{:S(2)}) collective-permute-start(bf16[192,768]{1,0:T(8,128)(2,1)S(1)} %fusion.16), channel_id=1, source_target_pairs={{0,4},{1,3},{4,8},{5,1},{8,12},{9,5},{12,14},{13,9},{14,10},{15,13... | collective-permute-start | bytes 884744 | tf_op jit(solution)/shard_map/ppermute | solution.py:608
  182.7 6.8 %collective-permute-start.15 = (bf16[192,768]{1,0:T(8,128)(2,1)S(1)}, bf16[192,768]{1,0:T(8,128)(2,1)S(1)}, u32[]{:S(2)}, u32[]{:S(2)}) collective-permute-start(bf16[192,768]{1,0:T(8,128)(2,1)S(1)} %fusion.15), channel_id=1, source_target_pairs={{0,4},{1,3},{4,8},{5,1},{8,12},{9,5},{12,14},{13,9},{14,10},{15,13... | collective-permute-start | bytes 884744 | tf_op jit(solution)/shard_map/ppermute | solution.py:608
  184.7 7.9 %collective-permute-start.39 = (bf16[192,768]{1,0:T(8,128)(2,1)S(1)}, bf16[192,768]{1,0:T(8,128)(2,1)S(1)}, u32[]{:S(2)}, u32[]{:S(2)}) collective-permute-start(bf16[192,768]{1,0:T(8,128)(2,1)S(1)} %get-tuple-element.160), channel_id=1, source_target_pairs={{0,4},{1,3},{4,8},{5,1},{8,12},{9,5},{12,14},{13,9},{14,10},{15,13... | collective-permute-start | bytes 884744 | tf_op jit(solution)/shard_map/ppermute | solution.py:608
  186.2 9.5 %collective-permute-start.28 = (bf16[192,768]{1,0:T(8,128)(2,1)S(1)}, bf16[192,768]{1,0:T(8,128)(2,1)S(1)}, u32[]{:S(2)}, u32[]{:S(2)}) collective-permute-start(bf16[192,768]{1,0:T(8,128)(2,1)S(1)} %get-tuple-element.161), channel_id=1, source_target_pairs={{0,4},{1,3},{4,8},{5,1},{8,12},{9,5},{12,14},{13,9},{14,10},{15,13... | collective-permute-start | bytes 884744 | tf_op jit(solution)/shard_map/ppermute | solution.py:608
  190.5 8.4 %collective-permute-start.16 = (bf16[192,768]{1,0:T(8,128)(2,1)S(1)}, bf16[192,768]{1,0:T(8,128)(2,1)S(1)}, u32[]{:S(2)}, u32[]{:S(2)}) collective-permute-start(bf16[192,768]{1,0:T(8,128)(2,1)S(1)} %fusion.14), channel_id=1, source_target_pairs={{0,4},{1,3},{4,8},{5,1},{8,12},{9,5},{12,14},{13,9},{14,10},{15,13... | collective-permute-start | bytes 884744 | tf_op jit(solution)/shard_map/ppermute | solution.py:608
  197.2 69.2 %copy-start.3 = (bf16[192,768]{1,0:T(8,128)(2,1)}, bf16[192,768]{1,0:T(8,128)(2,1)S(1)}, u32[]{:S(2)}) copy-start(bf16[192,768]{1,0:T(8,128)(2,1)S(1)} %get-tuple-element.158.refs_0_) | copy-start | bytes 884740
  197.2 6.8 %collective-permute-start.29 = (bf16[192,768]{1,0:T(8,128)(2,1)S(1)}, bf16[192,768]{1,0:T(8,128)(2,1)S(1)}, u32[]{:S(2)}, u32[]{:S(2)}) collective-permute-start(bf16[192,768]{1,0:T(8,128)(2,1)S(1)} %get-tuple-element.159.refs_0_), channel_id=1, source_target_pairs={{0,4},{1,3},{4,8},{5,1},{8,12},{9,5},{12,14},{13,9},{14,10},{15,13... | collective-permute-start | bytes 884744 | tf_op jit(solution)/shard_map/ppermute | solution.py:608
  200.0 7.2 %collective-permute-start.17 = (bf16[192,768]{1,0:T(8,128)(2,1)S(1)}, bf16[192,768]{1,0:T(8,128)(2,1)S(1)}, u32[]{:S(2)}, u32[]{:S(2)}) collective-permute-start(bf16[192,768]{1,0:T(8,128)(2,1)S(1)} %fusion.13), channel_id=1, source_target_pairs={{0,4},{1,3},{4,8},{5,1},{8,12},{9,5},{12,14},{13,9},{14,10},{15,13... | collective-permute-start | bytes 884744 | tf_op jit(solution)/shard_map/ppermute | solution.py:608
  200.5 4.0 %collective-permute-start.18 = (f32[16,768]{1,0:T(8,128)S(1)}, f32[16,768]{1,0:T(8,128)S(1)}, u32[]{:S(2)}, u32[]{:S(2)}) collective-permute-start(f32[16,768]{1,0:T(8,128)S(1)} %copy-done.30), channel_id=1, source_target_pairs={{0,1},{1,0},{2,3},{3,2},{4,5},{5,4},{6,7},{7,6},{8,9},{9,8},{10,11... | collective-permute-start | bytes 147464 | tf_op jit(solution)/shard_map/ppermute | solution.py:809
  200.5 9.8 %collective-permute-start.40 = (bf16[192,768]{1,0:T(8,128)(2,1)S(1)}, bf16[192,768]{1,0:T(8,128)(2,1)S(1)}, u32[]{:S(2)}, u32[]{:S(2)}) collective-permute-start(bf16[192,768]{1,0:T(8,128)(2,1)S(1)} %get-tuple-element.158.refs_0_), channel_id=1, source_target_pairs={{0,4},{1,3},{4,8},{5,1},{8,12},{9,5},{12,14},{13,9},{14,10},{15,13... | collective-permute-start | bytes 884744 | tf_op jit(solution)/shard_map/ppermute | solution.py:608
  204.0 9.5 %collective-permute-start.30 = (bf16[192,768]{1,0:T(8,128)(2,1)S(1)}, bf16[192,768]{1,0:T(8,128)(2,1)S(1)}, u32[]{:S(2)}, u32[]{:S(2)}) collective-permute-start(bf16[192,768]{1,0:T(8,128)(2,1)S(1)} %collective-permute-done.29.refs_1_), channel_id=1, source_target_pairs={{0,4},{1,3},{4,8},{5,1},{8,12},{9,5},{12,14},{13,9},{14,10},{15,13... | collective-permute-start | bytes 884744 | tf_op jit(solution)/shard_map/ppermute | solution.py:608
  208.3 8.6 %collective-permute-start.19 = (bf16[208,768]{1,0:T(8,128)(2,1)S(1)}, bf16[208,768]{1,0:T(8,128)(2,1)S(1)}, u32[]{:S(2)}, u32[]{:S(2)}) collective-permute-start(bf16[208,768]{1,0:T(8,128)(2,1)S(1)} %pad_maximum_fusion.refs_0_), channel_id=1, source_target_pairs={{0,4},{1,3},{4,8},{5,1},{8,12},{9,5},{12,14},{13,9},{14,10},{15,13... | collective-permute-start | bytes 958472 | tf_op jit(solution)/shard_map/ppermute | solution.py:608
  210.3 9.7 %collective-permute-start.41 = (bf16[192,768]{1,0:T(8,128)(2,1)S(1)}, bf16[192,768]{1,0:T(8,128)(2,1)S(1)}, u32[]{:S(2)}, u32[]{:S(2)}) collective-permute-start(bf16[192,768]{1,0:T(8,128)(2,1)S(1)} %collective-permute-done.40.refs_1_), channel_id=1, source_target_pairs={{0,4},{1,3},{4,8},{5,1},{8,12},{9,5},{12,14},{13,9},{14,10},{15,13... | collective-permute-start | bytes 884744 | tf_op jit(solution)/shard_map/ppermute | solution.py:608
  213.5 9.7 %collective-permute-start.31 = (bf16[192,768]{1,0:T(8,128)(2,1)S(1)}, bf16[192,768]{1,0:T(8,128)(2,1)S(1)}, u32[]{:S(2)}, u32[]{:S(2)}) collective-permute-start(bf16[192,768]{1,0:T(8,128)(2,1)S(1)} %collective-permute-done.30.refs_2_), channel_id=1, source_target_pairs={{0,4},{1,3},{4,8},{5,1},{8,12},{9,5},{12,14},{13,9},{14,10},{15,13... | collective-permute-start | bytes 884744 | tf_op jit(solution)/shard_map/ppermute | solution.py:608
  216.9 9.7 %collective-permute-start.20 = (bf16[208,768]{1,0:T(8,128)(2,1)S(1)}, bf16[208,768]{1,0:T(8,128)(2,1)S(1)}, u32[]{:S(2)}, u32[]{:S(2)}) collective-permute-start(bf16[208,768]{1,0:T(8,128)(2,1)S(1)} %collective-permute-done.19.refs_1_), channel_id=1, source_target_pairs={{0,4},{1,3},{4,8},{5,1},{8,12},{9,5},{12,14},{13,9},{14,10},{15,13... | collective-permute-start | bytes 958472 | tf_op jit(solution)/shard_map/ppermute | solution.py:608
  220.1 9.7 %collective-permute-start.42 = (bf16[192,768]{1,0:T(8,128)(2,1)S(1)}, bf16[192,768]{1,0:T(8,128)(2,1)S(1)}, u32[]{:S(2)}, u32[]{:S(2)}) collective-permute-start(bf16[192,768]{1,0:T(8,128)(2,1)S(1)} %collective-permute-done.41.refs_2_), channel_id=1, source_target_pairs={{0,4},{1,3},{4,8},{5,1},{8,12},{9,5},{12,14},{13,9},{14,10},{15,13... | collective-permute-start | bytes 884744 | tf_op jit(solution)/shard_map/ppermute | solution.py:608
  223.2 9.7 %collective-permute-start.32 = (bf16[192,768]{1,0:T(8,128)(2,1)S(1)}, bf16[192,768]{1,0:T(8,128)(2,1)S(1)}, u32[]{:S(2)}, u32[]{:S(2)}) collective-permute-start(bf16[192,768]{1,0:T(8,128)(2,1)S(1)} %collective-permute-done.31.refs_3_), channel_id=1, source_target_pairs={{0,4},{1,3},{4,8},{5,1},{8,12},{9,5},{12,14},{13,9},{14,10},{15,13... | collective-permute-start | bytes 884744 | tf_op jit(solution)/shard_map/ppermute | solution.py:608
  226.6 9.7 %collective-permute-start.21 = (bf16[208,768]{1,0:T(8,128)(2,1)S(1)}, bf16[208,768]{1,0:T(8,128)(2,1)S(1)}, u32[]{:S(2)}, u32[]{:S(2)}) collective-permute-start(bf16[208,768]{1,0:T(8,128)(2,1)S(1)} %collective-permute-done.20.refs_2_), channel_id=1, source_target_pairs={{0,4},{1,3},{4,8},{5,1},{8,12},{9,5},{12,14},{13,9},{14,10},{15,13... | collective-permute-start | bytes 958472 | tf_op jit(solution)/shard_map/ppermute | solution.py:608
  229.8 9.7 %collective-permute-start.43 = (bf16[192,768]{1,0:T(8,128)(2,1)S(1)}, bf16[192,768]{1,0:T(8,128)(2,1)S(1)}, u32[]{:S(2)}, u32[]{:S(2)}) collective-permute-start(bf16[192,768]{1,0:T(8,128)(2,1)S(1)} %collective-permute-done.42.refs_3_), channel_id=1, source_target_pairs={{0,4},{1,3},{4,8},{5,1},{8,12},{9,5},{12,14},{13,9},{14,10},{15,13... | collective-permute-start | bytes 884744 | tf_op jit(solution)/shard_map/ppermute | solution.py:608
  233.0 9.7 %collective-permute-start.33 = (bf16[192,768]{1,0:T(8,128)(2,1)S(1)}, bf16[192,768]{1,0:T(8,128)(2,1)S(1)}, u32[]{:S(2)}, u32[]{:S(2)}) collective-permute-start(bf16[192,768]{1,0:T(8,128)(2,1)S(1)} %collective-permute-done.32.refs_4_), channel_id=1, source_target_pairs={{0,4},{1,3},{4,8},{5,1},{8,12},{9,5},{12,14},{13,9},{14,10},{15,13... | collective-permute-start | bytes 884744 | tf_op jit(solution)/shard_map/ppermute | solution.py:608
  236.4 9.7 %collective-permute-start.22 = (bf16[208,768]{1,0:T(8,128)(2,1)S(1)}, bf16[208,768]{1,0:T(8,128)(2,1)S(1)}, u32[]{:S(2)}, u32[]{:S(2)}) collective-permute-start(bf16[208,768]{1,0:T(8,128)(2,1)S(1)} %collective-permute-done.21.refs_3_), channel_id=1, source_target_pairs={{0,4},{1,3},{4,8},{5,1},{8,12},{9,5},{12,14},{13,9},{14,10},{15,13... | collective-permute-start | bytes 958472 | tf_op jit(solution)/shard_map/ppermute | solution.py:608
  239.5 9.8 %collective-permute-start.44 = (bf16[192,768]{1,0:T(8,128)(2,1)S(1)}, bf16[192,768]{1,0:T(8,128)(2,1)}, u32[]{:S(2)}, u32[]{:S(2)}) collective-permute-start(bf16[192,768]{1,0:T(8,128)(2,1)S(1)} %collective-permute-done.43.refs_4_), channel_id=1, source_target_pairs={{0,4},{1,3},{4,8},{5,1},{8,12},{9,5},{12,14},{13,9},{14,10},{15,13... | collective-permute-start | bytes 884744 | tf_op jit(solution)/shard_map/ppermute | solution.py:608
  242.7 9.8 %collective-permute-start.34 = (bf16[192,768]{1,0:T(8,128)(2,1)S(1)}, bf16[192,768]{1,0:T(8,128)(2,1)}, u32[]{:S(2)}, u32[]{:S(2)}) collective-permute-start(bf16[192,768]{1,0:T(8,128)(2,1)S(1)} %collective-permute-done.33.refs_5_), channel_id=1, source_target_pairs={{0,4},{1,3},{4,8},{5,1},{8,12},{9,5},{12,14},{13,9},{14,10},{15,13... | collective-permute-start | bytes 884744 | tf_op jit(solution)/shard_map/ppermute | solution.py:608
  246.1 13.5 %collective-permute-start.23 = (bf16[208,768]{1,0:T(8,128)(2,1)S(1)}, bf16[208,768]{1,0:T(8,128)(2,1)S(1)}, u32[]{:S(2)}, u32[]{:S(2)}) collective-permute-start(bf16[208,768]{1,0:T(8,128)(2,1)S(1)} %collective-permute-done.22.refs_4_), channel_id=1, source_target_pairs={{0,4},{1,3},{4,8},{5,1},{8,12},{9,5},{12,14},{13,9},{14,10},{15,13... | collective-permute-start | bytes 958472 | tf_op jit(solution)/shard_map/ppermute | solution.py:608
  249.4 9.7 %collective-permute-start.45 = (bf16[192,768]{1,0:T(8,128)(2,1)}, bf16[192,768]{1,0:T(8,128)(2,1)}, u32[]{:S(2)}, u32[]{:S(2)}) collective-permute-start(bf16[192,768]{1,0:T(8,128)(2,1)} %collective-permute-done.44.refs_5_), channel_id=1, source_target_pairs={{0,4},{1,3},{4,8},{5,1},{8,12},{9,5},{12,14},{13,9},{14,10},{15,13... | collective-permute-start | bytes 884744 | tf_op jit(solution)/shard_map/ppermute | solution.py:608
  252.6 9.7 %collective-permute-start.35 = (bf16[192,768]{1,0:T(8,128)(2,1)}, bf16[192,768]{1,0:T(8,128)(2,1)}, u32[]{:S(2)}, u32[]{:S(2)}) collective-permute-start(bf16[192,768]{1,0:T(8,128)(2,1)} %collective-permute-done.34.refs_6_), channel_id=1, source_target_pairs={{0,4},{1,3},{4,8},{5,1},{8,12},{9,5},{12,14},{13,9},{14,10},{15,13... | collective-permute-start | bytes 884744 | tf_op jit(solution)/shard_map/ppermute | solution.py:608
  259.1 10.9 %collective-permute-start.46 = (bf16[192,768]{1,0:T(8,128)(2,1)}, bf16[192,768]{1,0:T(8,128)(2,1)}, u32[]{:S(2)}, u32[]{:S(2)}) collective-permute-start(bf16[192,768]{1,0:T(8,128)(2,1)} %collective-permute-done.45.refs_6_), channel_id=1, source_target_pairs={{0,4},{1,3},{4,8},{5,1},{8,12},{9,5},{12,14},{13,9},{14,10},{15,13... | collective-permute-start | bytes 884744 | tf_op jit(solution)/shard_map/ppermute | solution.py:608
  259.6 9.9 %collective-permute-start.24 = (bf16[208,768]{1,0:T(8,128)(2,1)S(1)}, bf16[208,768]{1,0:T(8,128)(2,1)S(1)}, u32[]{:S(2)}, u32[]{:S(2)}) collective-permute-start(bf16[208,768]{1,0:T(8,128)(2,1)S(1)} %collective-permute-done.23.refs_5_), channel_id=1, source_target_pairs={{0,4},{1,3},{4,8},{5,1},{8,12},{9,5},{12,14},{13,9},{14,10},{15,13... | collective-permute-start | bytes 958472 | tf_op jit(solution)/shard_map/ppermute | solution.py:608
  269.5 7.0 %collective-permute-start.36 = (bf16[208,768]{1,0:T(8,128)(2,1)S(1)}, bf16[208,768]{1,0:T(8,128)(2,1)S(1)}, u32[]{:S(2)}, u32[]{:S(2)}) collective-permute-start(bf16[208,768]{1,0:T(8,128)(2,1)S(1)} %collective-permute-done.24.refs_6_), channel_id=1, source_target_pairs={{0,4},{1,3},{4,8},{5,1},{8,12},{9,5},{12,14},{13,9},{14,10},{15,13... | collective-permute-start | bytes 958472 | tf_op jit(solution)/shard_map/ppermute | solution.py:608
  (30 other events, 606.3 us)

commit v3 on v2

--- a/solution.py
+++ b/solution.py
@@ -447,41 +447,66 @@
                        queries, pair, turned_hot, key_hot, probs, d_context, scratch=scratch)
 
 
-def weights_kernel(
+def early_weights_kernel(
     order_ref, normed_ref, d_branch_ref, context_0_ref, context_1_ref, context_2_ref,
-    d_query_0_ref, d_query_1_ref, d_query_2_ref, back_0_ref, back_1_ref, back_2_ref,
-    mine_ref, other_ref, joined_ref, left_ref,
+    d_query_0_ref, d_query_1_ref, d_query_2_ref, mine_ref, other_ref, left_ref, right_ref,
 ):
     part = context_0_ref.shape[1]
-    queries = (d_query_0_ref, d_query_1_ref, d_query_2_ref)
-    backs = (back_0_ref, back_1_ref, back_2_ref)
-    contexts = (context_0_ref, context_1_ref, context_2_ref)
-    for group in range(GROUPS):
+    left_ref[0] = normed_ref[...]
+    right_ref[1] = d_branch_ref[...]
+    pairs = zip((d_query_0_ref, d_query_1_ref, d_query_2_ref), (context_0_ref, context_1_ref, context_2_ref))
+    for group, (query_ref, context_ref) in enumerate(pairs):
         lanes = slice(group * part, group * part + part)
-        joined_ref[0, :, lanes] = queries[group][...]
-        joined_ref[1, :, lanes] = backs[group][0]
-        joined_ref[2, :, lanes] = backs[group][1]
-        joined_ref[3, :, lanes] = contexts[group][...]
-    left_ref[0] = normed_ref[...]
-    left_ref[1] = joined_ref[3]
-    joined_ref[3] = d_branch_ref[...]
+        right_ref[0, :, lanes] = query_ref[...]
+        left_ref[1, :, lanes] = context_ref[...]
 
     def block_step(block, carry):
-        value = dot_across(left_ref[block // 3], joined_ref[block]).astype(jnp.bfloat16)
+        value = dot_across(left_ref[block], right_ref[block]).astype(jnp.bfloat16)
         rows = pl.ds(pl.multiple_of(block * 48, 16), 48)
         for piece in range(16):
             place_chunk(order_ref[piece], mine_ref, other_ref, value[piece * 48 : piece * 48 + 48], rows)
         return carry
 
-    lax.fori_loop(0, 4, block_step, 0)
-
-
-def weights_call(order, normed, d_branch, contexts, d_queries, backs):
+    lax.fori_loop(0, 2, block_step, 0)
+
+
+def weights_kernel(
+    order_ref, normed_ref, back_0_ref, back_1_ref, back_2_ref, early_mine_ref, early_other_ref,
+    mine_ref, other_ref, right_ref,
+):
+    part = back_0_ref.shape[2]
+    for group, back_ref in enumerate((back_0_ref, back_1_ref, back_2_ref)):
+        lanes = slice(group * part, group * part + part)
+        right_ref[0, :, lanes] = back_ref[0]
+        right_ref[1, :, lanes] = back_ref[1]
+    for early_ref, out_ref in ((early_mine_ref, mine_ref), (early_other_ref, other_ref)):
+        out_ref[:, 0:48, :] = early_ref[:, 0:48, :]
+        out_ref[:, 144:192, :] = early_ref[:, 48:96, :]
+
+    def block_step(block, carry):
+        value = dot_across(normed_ref[...], right_ref[block]).astype(jnp.bfloat16)
+        rows = pl.ds(pl.multiple_of(48 + block * 48, 16), 48)
+        for piece in range(16):
+            place_chunk(order_ref[piece], mine_ref, other_ref, value[piece * 48 : piece * 48 + 48], rows)
+        return carry
+
+    lax.fori_loop(0, 2, block_step, 0)
+
+
+def early_weights_call(order, normed, d_branch, contexts, d_queries):
+    rows, width = normed.shape
+    ring = jax.ShapeDtypeStruct((RING, 96, width), jnp.bfloat16)
+    scratch = [pltpu.VMEM((2, rows, width), jnp.bfloat16), pltpu.VMEM((2, rows, width), jnp.bfloat16)]
+    return kernel_call(early_weights_kernel, "early_weights", 5, [ring, ring], order, normed, d_branch,
+                       *contexts, *d_queries, scratch=scratch, smem=1)
+
+
+def weights_call(order, normed, backs, early):
     rows, width = normed.shape
     ring = jax.ShapeDtypeStruct((RING, 192, width), jnp.bfloat16)
-    scratch = [pltpu.VMEM((4, rows, width), jnp.bfloat16), pltpu.VMEM((2, rows, width), jnp.bfloat16)]
-    return kernel_call(weights_kernel, "weights", 7, [ring, ring], order, normed, d_branch,
-                       *contexts, *d_queries, *backs, scratch=scratch, smem=1)
+    scratch = [pltpu.VMEM((2, rows, width), jnp.bfloat16)]
+    return kernel_call(weights_kernel, "weights", 5, [ring, ring], order, normed, *backs, *early,
+                       scratch=scratch, smem=1)
 
 
 def last_kernel(
@@ -761,11 +786,12 @@
             backs[group] = partner_2(d_pair, "stream", 0)
             if group < GROUPS - 1:
                 feed.reduce()
-            if group:
-                queue.wait(backs[group - 1])
+            if group == 1:
+                queue.wait(backs[0])
         else:
             backs[group] = partner_2(d_pair, "stream", 0)
-    rest_mine, rest_other = weights_call(order, queue.after(normed), d_branch, contexts, d_queries, backs)
+    early = early_weights_call(order, queue.after(normed), d_branch, contexts, d_queries)
+    rest_mine, rest_other = weights_call(order, normed, backs, early)
     if ringed:
         queue.mark = rest_mine
         feed.reduce()

time: 282 us -> 280 us (level)
  waiting for transfers between devices: 102 us -> 96.6 us
  Pallas kernels: 116 us -> 119 us
    ppermute x6, waiting for transfers between devices: 19.9 us -> 14.2 us  [partner_2(): lax.ppermute(shard, axis, [(i, i ^ 1 << distance) for i in range(lax.axis...]
    pallas_call x13 -> x14, Pallas kernels: 85.4 us -> 88.8 us  [kernel_call(): pl.pallas_call(kernel, out_shape=tuple(outs), in_specs=specs, out_specs=t...]
  transfers between devices with their start and end apart: 47 -> 47, of which waited for: 34 -> 34; matrix products, arithmetic and copies ran while one was open for 6% -> 6% of each run, Pallas kernels for 25% -> 26%
where the time goes in v3:
time: 280 us; the launch traced here: 279 us
  Pallas kernels  119 us (42%)
  waiting for transfers between devices  96.6 us (34%)
  starting transfers between devices  40.2 us (14%)
  other arithmetic  18.2 us (6%)
  local copies, waits for them, and re-layouts  4.11 us (1%)
    pallas_call x14, Pallas kernels, kernel_call(): pl.pallas_call(kernel, out_shape=tuple(outs), in_specs=specs, out_specs=t...  88.8 us
    ppermute x38, waiting for transfers between devices, ring_send(): return lax.ppermute(chunk, ('group', 'dp'), pairs)  78.3 us
    ppermute x38, starting transfers between devices, ring_send(): return lax.ppermute(chunk, ('group', 'dp'), pairs)  31.3 us
    pallas_call x1, Pallas kernels, feed_call(): pl.pallas_call(feed_kernel, out_shape=(wide(bf16), wide(f32), wide(bf16),...  30.2 us
    convert_element_type x17, other arithmetic, add_low(): sum((term.astype(jnp.float32) for term in terms)).astype(jnp.bfloat16)  16.4 us
    ppermute x6, waiting for transfers between devices, partner_2(): lax.ppermute(shard, axis, [(i, i ^ 1 << distance) for i in range(lax.axis...  14.2 us
    ppermute x6, starting transfers between devices, partner_2(): lax.ppermute(shard, axis, [(i, i ^ 1 << distance) for i in range(lax.axis...  8.82 us
  transfers between devices with their start and end apart: 47, of which 34 were waited for; matrix products, arithmetic and copies ran while one was open for 6% of the time, Pallas kernels for 26%

profile of v3, /device:TPU:0, one launch (start us, length us, event | category | flops | bytes accessed | tf_op | source)
XLA Modules:
  0.0 279.2 jit_solution(15722344840711466094)
XLA Ops:
  0.7 4.7 %first.1 = (bf16[512,768]{1,0:T(8,128)(2,1)}, bf16[2,512,256]{2,1,0:T(8,128)(2,1)}, bf16[2,512,256]{2,1,0:T(8,128)(2,1)}, bf16[2,512,256]{2,1,0:T(8,128)(2,1)}) custom-call(bf16[512,768]{1,0:T(8,128)(2,1)} %bitcast.171, f32[1,768]{1,0:T(1,128)} %gain_ref.5, f32[1,768]{1,0:T(1,128)} %shift_ref.2, bf16[768,2304]{1,0:T(8,128)(2,1)} %bitcast.166, f32[1,768]{1,0:T(1,128)} %bias_ref.2), custom_call_target="tpu_custom_call" | custom-call | flops 5000000000 | tf_op jit(solution)/shard_map/first/pallas_call | solution.py:267
  5.4 3.0 %collective-permute-start = (bf16[2,512,256]{2,1,0:T(8,128)(2,1)}, bf16[2,512,256]{2,1,0:T(8,128)(2,1)S(1)}, u32[]{:S(2)}, u32[]{:S(2)}) collective-permute-start(bf16[2,512,256]{2,1,0:T(8,128)(2,1)} %get-tuple-element.90), channel_id=1, source_target_pairs={{0,16},{16,0},{1,17},{17,1},{2,18},{18,2},{3,19},{19,3},{4,20},{20... | collective-permute-start | bytes 1572872 | tf_op jit(solution)/shard_map/ppermute | solution.py:623
  8.4 2.0 collective-permute-start.2
  11.6 5.3 %prep.1 = (bf16[512,768]{1,0:T(8,128)(2,1)}, bf16[512,384]{1,0:T(8,128)(2,1)}, bf16[512,384]{1,0:T(8,128)(2,1)}, bf16[512,384]{1,0:T(8,128)(2,1)}, s32[1,512]{1,0:T(1,128)}, /*index=5*/bf16[36,128,128]{2,1,0:T(8,128)(2,1)}) custom-call(s32[1]{0:T(128)} %bitcast.1.stream_ref, s32[2,2,1,512]{3,2,1,0:T(1,128)} %box_ref.1, s32[2,1,512]{2,1,0:T(1,128)} %segment_ref.1, ...), custom_call_target="tpu_custom_call" | custom-call | flops 5000000000 | tf_op jit(solution)/shard_map/prep/pallas_call | solution.py:267
  16.9 4.5 %collective-permute-done.pair_ref = bf16[2,512,256]{2,1,0:T(8,128)(2,1)S(1)} collective-permute-done((bf16[2,512,256]{2,1,0:T(8,128)(2,1)}, bf16[2,512,256]{2,1,0:T(8,128)(2,1)S(1)}, u32[]{:S(2)}, u32[]{:S(2)}) %collective-permute-start) | collective-permute-done | bytes 524320 | tf_op jit(solution)/shard_map/ppermute | solution.py:623
  22.2 7.3 %attend_0.1 = (bf16[512,256]{1,0:T(8,128)(2,1)}, bf16[4,512,512]{2,1,0:T(8,128)(2,1)}) custom-call(bf16[512,768]{1,0:T(8,128)(2,1)} %get-tuple-element.89.queries_ref, bf16[2,512,256]{2,1,0:T(8,128)(2,1)} %copy-done.12, bf16[512,384]{1,0:T(8,128)(2,1)} %get-tuple-element.91.hot_ref, bf16[512,384]{1,0:T(8,128)(2,1)} %get-tuple-element.92.key_hot_ref, ...), custom_call_target="tpu_custom_call" | custom-call | flops 7000000000 | tf_op jit(solution)/shard_map/attend_0/pallas_call | solution.py:267
  29.5 3.1 %collective-permute-done.1.pair_ref = bf16[2,512,256]{2,1,0:T(8,128)(2,1)S(1)} collective-permute-done((bf16[2,512,256]{2,1,0:T(8,128)(2,1)}, bf16[2,512,256]{2,1,0:T(8,128)(2,1)S(1)}, u32[]{:S(2)}, u32[]{:S(2)}) %collective-permute-start.1) | collective-permute-done | bytes 524320 | tf_op jit(solution)/shard_map/ppermute | solution.py:623
  33.4 7.3 %attend_1.1 = (bf16[512,256]{1,0:T(8,128)(2,1)}, bf16[4,512,512]{2,1,0:T(8,128)(2,1)}) custom-call(bf16[512,768]{1,0:T(8,128)(2,1)} %get-tuple-element.89.queries_ref, bf16[2,512,256]{2,1,0:T(8,128)(2,1)} %copy-done.11, bf16[512,384]{1,0:T(8,128)(2,1)} %get-tuple-element.91.hot_ref, bf16[512,384]{1,0:T(8,128)(2,1)} %get-tuple-element.92.key_hot_ref, ...), custom_call_target="tpu_custom_call" | custom-call | flops 7000000000 | tf_op jit(solution)/shard_map/attend_1/pallas_call | solution.py:267
  40.7 2.2 collective-permute-done.2.pair_ref
  43.8 7.4 %attend_2.1 = (bf16[512,256]{1,0:T(8,128)(2,1)}, bf16[4,512,512]{2,1,0:T(8,128)(2,1)}) custom-call(bf16[512,768]{1,0:T(8,128)(2,1)} %get-tuple-element.89.queries_ref, bf16[2,512,256]{2,1,0:T(8,128)(2,1)} %copy-done.9, bf16[512,384]{1,0:T(8,128)(2,1)} %get-tuple-element.91.hot_ref, bf16[512,384]{1,0:T(8,128)(2,1)} %get-tuple-element.92.key_hot_ref, ...), custom_call_target="tpu_custom_call" | custom-call | flops 7000000000 | tf_op jit(solution)/shard_map/attend_2/pallas_call | solution.py:267
  51.1 30.2 %feed.1 = (bf16[512,768]{1,0:T(8,128)(2,1)}, f32[512,768]{1,0:T(8,128)}, bf16[512,768]{1,0:T(8,128)(2,1)}, bf16[512,768]{1,0:T(8,128)(2,1)}, bf16[8,384,768]{2,1...) custom-call(s32[16]{0:T(128)} %fusion.21.order_ref, bf16[512,768]{1,0:T(8,128)(2,1)} %bitcast.172, ...), custom_call_target="tpu_custom_call" | custom-call | flops 30000001024 | tf_op jit(solution)/shard_map/feed/pallas_call | solution.py:207
  81.4 8.1 %attend_back_0.1 = (bf16[512,256]{1,0:T(8,128)(2,1)}, bf16[2,512,256]{2,1,0:T(8,128)(2,1)}, f32[3,4,256]{2,1,0:T(4,128)}) custom-call(bf16[512,768]{1,0:T(8,128)(2,1)} %get-tuple-element.89.queries_ref, bf16[2,512,256]{2,1,0:T(8,128)(2,1)} %copy-done.12, bf16[512,384]{1,0:T(8,128)(2,1)} %get-tuple-element.103.turned_hot_ref, ...), custom_call_target="tpu_custom_call" | custom-call | flops 8000000000 | tf_op jit(solution)/shard_map/attend_back_0/pallas_call | solution.py:267
  89.5 1.7 collective-permute-start.3
  92.6 1.6 collective-permute-start.6
  94.2 8.1 %attend_back_1.1 = (bf16[512,256]{1,0:T(8,128)(2,1)}, bf16[2,512,256]{2,1,0:T(8,128)(2,1)}, f32[3,4,256]{2,1,0:T(4,128)}) custom-call(bf16[512,768]{1,0:T(8,128)(2,1)} %get-tuple-element.89.queries_ref, bf16[2,512,256]{2,1,0:T(8,128)(2,1)} %copy-done.11, bf16[512,384]{1,0:T(8,128)(2,1)} %get-tuple-element.103.turned_hot_ref, ...), custom_call_target="tpu_custom_call" | custom-call | flops 8000000000 | tf_op jit(solution)/shard_map/attend_back_1/pallas_call | solution.py:267
  104.3 1.7 collective-permute-start.7
  106.0 8.2 %attend_back_2.1 = (bf16[512,256]{1,0:T(8,128)(2,1)}, bf16[2,512,256]{2,1,0:T(8,128)(2,1)}, f32[3,4,256]{2,1,0:T(4,128)}) custom-call(bf16[512,768]{1,0:T(8,128)(2,1)} %get-tuple-element.89.queries_ref, bf16[2,512,256]{2,1,0:T(8,128)(2,1)} %copy-done.9, bf16[512,384]{1,0:T(8,128)(2,1)} %get-tuple-element.103.turned_hot_ref, ...), custom_call_target="tpu_custom_call" | custom-call | flops 8000000000 | tf_op jit(solution)/shard_map/attend_back_2/pallas_call | solution.py:267
  118.9 5.7 %early_weights.1 = (bf16[8,96,768]{2,1,0:T(8,128)(2,1)}, bf16[8,96,768]{2,1,0:T(8,128)(2,1)}) custom-call(s32[16]{0:T(128)} %fusion.21.order_ref, bf16[512,768]{1,0:T(8,128)(2,1)} %get-tuple-element.124.normed_ref, bf16[512,768]{1,0:T(8,128)(2,1)} %get-tuple-element.125.d_branch_ref, bf16[512,256]{1,0:T(8,128)(2,1)} %get-tuple-element.95.context_0_ref, ...), custom_call_target="tpu_custom_call" | custom-call | flops 5000000000 | tf_op jit(solution)/shard_map/early_weights/pallas_call | solution.py:267
  124.6 4.3 %collective-permute-done.8.back_2_ref = bf16[2,512,256]{2,1,0:T(8,128)(2,1)S(1)} collective-permute-done((bf16[2,512,256]{2,1,0:T(8,128)(2,1)S(1)}, bf16[2,512,256]{2,1,0:T(8,128)(2,1)S(1)}, u32[]{:S(2)}, u32[]{:S(2)}) %collective-permute-start.8) | collective-permute-done | bytes 524320 | tf_op jit(solution)/shard_map/ppermute | solution.py:623
  129.8 7.0 %weights.1 = (bf16[8,192,768]{2,1,0:T(8,128)(2,1)}, bf16[8,192,768]{2,1,0:T(8,128)(2,1)}) custom-call(s32[16]{0:T(128)} %fusion.21.order_ref, bf16[512,768]{1,0:T(8,128)(2,1)} %get-tuple-element.124.normed_ref, bf16[2,512,256]{2,1,0:T(8,128)(2,1)} %copy-done.7, bf16[2,512,256]{2,1,0:T(8,128)(2,1)} %copy-done.8, bf16[2,512,256]{2,1,0:T(8,128)(2,1)} %copy-done.10, ...), custom_call_target="tpu_custom_call" | custom-call | flops 5000000000 | tf_op jit(solution)/shard_map/weights/pallas_call | solution.py:267
  139.1 4.2 %collective-permute-done.10 = bf16[8,192,768]{2,1,0:T(8,128)(2,1)S(1)} collective-permute-done((bf16[8,192,768]{2,1,0:T(8,128)(2,1)}, bf16[8,192,768]{2,1,0:T(8,128)(2,1)S(1)}, u32[]{:S(2)}, u32[]{:S(2)}) %collective-permute-start.10) | collective-permute-done | bytes 2359328 | tf_op jit(solution)/shard_map/ppermute | solution.py:714
  143.9 7.7 %collective-permute-done.11 = bf16[192,768]{1,0:T(8,128)(2,1)S(1)} collective-permute-done((bf16[192,768]{1,0:T(8,128)(2,1)S(1)}, bf16[192,768]{1,0:T(8,128)(2,1)S(1)}, u32[]{:S(2)}, u32[]{:S(2)}) %collective-permute-start.11) | collective-permute-done | bytes 294944 | tf_op jit(solution)/shard_map/ppermute | solution.py:633
  159.2 2.5 collective-permute-done.37
  161.7 3.2 %collective-permute-done.26 = bf16[192,768]{1,0:T(8,128)(2,1)S(1)} collective-permute-done((bf16[192,768]{1,0:T(8,128)(2,1)S(1)}, bf16[192,768]{1,0:T(8,128)(2,1)S(1)}, u32[]{:S(2)}, u32[]{:S(2)}) %collective-permute-start.26) | collective-permute-done | bytes 294944 | tf_op jit(solution)/shard_map/ppermute | solution.py:633
  170.1 7.5 %last.1 = (bf16[512,768]{1,0:T(8,128)(2,1)}, f32[16,768]{1,0:T(8,128)}, f32[16,768]{1,0:T(8,128)}) custom-call(s32[1]{0:T(128)} %bitcast.22.side_ref, bf16[512,768]{1,0:T(8,128)(2,1)} %bitcast.173, f32[1,768]{1,0:T(1,128)} %gain_ref.5, bf16[768,2304]{1,0:T(8,128)(2,1)} %bitcast.168, f32[512,768]{1,0:T(8,128)} %get-tuple-element.134.d_middle_ref, ...), custom_call_target="tpu_custom_call" | custom-call | flops 8000000000 | tf_op jit(solution)/shard_map/last/pallas_call | solution.py:267
  177.6 1.8 collective-permute-done.14
  190.4 3.2 %collective-permute-done.28 = bf16[192,768]{1,0:T(8,128)(2,1)S(1)} collective-permute-done((bf16[192,768]{1,0:T(8,128)(2,1)S(1)}, bf16[192,768]{1,0:T(8,128)(2,1)S(1)}, u32[]{:S(2)}, u32[]{:S(2)}) %collective-permute-start.28) | collective-permute-done | bytes 294944 | tf_op jit(solution)/shard_map/ppermute | solution.py:633
  199.9 1.9 collective-permute-done.29.refs_1_
  202.3 2.6 collective-permute-done.17
  208.6 2.7 collective-permute-done.30.refs_2_
  211.8 2.9 %collective-permute-done.19.refs_1_ = bf16[208,768]{1,0:T(8,128)(2,1)S(1)} collective-permute-done((bf16[208,768]{1,0:T(8,128)(2,1)S(1)}, bf16[208,768]{1,0:T(8,128)(2,1)S(1)}, u32[]{:S(2)}, u32[]{:S(2)}) %collective-permute-start.19) | collective-permute-done | bytes 319520 | tf_op jit(solution)/shard_map/ppermute | solution.py:633
  215.2 2.7 collective-permute-done.41.refs_2_
  218.4 2.7 collective-permute-done.31.refs_3_
  221.5 2.9 %collective-permute-done.20.refs_2_ = bf16[208,768]{1,0:T(8,128)(2,1)S(1)} collective-permute-done((bf16[208,768]{1,0:T(8,128)(2,1)S(1)}, bf16[208,768]{1,0:T(8,128)(2,1)S(1)}, u32[]{:S(2)}, u32[]{:S(2)}) %collective-permute-start.20) | collective-permute-done | bytes 319520 | tf_op jit(solution)/shard_map/ppermute | solution.py:633
  224.9 2.7 collective-permute-done.42.refs_3_
  228.1 2.7 collective-permute-done.32.refs_4_
  231.3 2.9 %collective-permute-done.21.refs_3_ = bf16[208,768]{1,0:T(8,128)(2,1)S(1)} collective-permute-done((bf16[208,768]{1,0:T(8,128)(2,1)S(1)}, bf16[208,768]{1,0:T(8,128)(2,1)S(1)}, u32[]{:S(2)}, u32[]{:S(2)}) %collective-permute-start.21) | collective-permute-done | bytes 319520 | tf_op jit(solution)/shard_map/ppermute | solution.py:633
  234.7 2.7 collective-permute-done.43.refs_4_
  237.8 2.7 collective-permute-done.33.refs_5_
  241.0 2.9 %collective-permute-done.22.refs_4_ = bf16[208,768]{1,0:T(8,128)(2,1)S(1)} collective-permute-done((bf16[208,768]{1,0:T(8,128)(2,1)S(1)}, bf16[208,768]{1,0:T(8,128)(2,1)S(1)}, u32[]{:S(2)}, u32[]{:S(2)}) %collective-permute-start.22) | collective-permute-done | bytes 319520 | tf_op jit(solution)/shard_map/ppermute | solution.py:633
  244.4 2.8 collective-permute-done.44.refs_5_
  247.7 2.7 collective-permute-done.34.refs_6_
  251.4 5.6 %collective-permute-done.45.refs_6_ = bf16[192,768]{1,0:T(8,128)(2,1)} collective-permute-done((bf16[192,768]{1,0:T(8,128)(2,1)}, bf16[192,768]{1,0:T(8,128)(2,1)}, u32[]{:S(2)}, u32[]{:S(2)}) %collective-permute-start.45) | collective-permute-done | bytes 294944 | tf_op jit(solution)/shard_map/ppermute | solution.py:633
  260.1 4.1 %open_back.1 = f32[1536,768]{1,0:T(8,128)} custom-call(s32[8]{0:T(128)} %and_select_fusion.place_ref, bf16[192,768]{1,0:T(8,128)(2,1)} %copy-done.4, bf16[192,768]{1,0:T(8,128)(2,1)} %copy-done.21, bf16[192,768]{1,0:T(8,128)(2,1)} %copy-done.23, bf16[192,768]{1,0:T(8,128)(2,1)} %copy-done.26, bf16[192,768]{1,0:T(8,128)(2,1)} %copy-done.28, ...), custom_call_target="tpu_custom_call" | custom-call | flops 4000000000 | tf_op jit(solution)/shard_map/open_back/pallas_call | solution.py:267
  264.3 3.0 %collective-permute-done.24.refs_6_ = bf16[208,768]{1,0:T(8,128)(2,1)S(1)} collective-permute-done((bf16[208,768]{1,0:T(8,128)(2,1)S(1)}, bf16[208,768]{1,0:T(8,128)(2,1)S(1)}, u32[]{:S(2)}, u32[]{:S(2)}) %collective-permute-start.24) | collective-permute-done | bytes 319520 | tf_op jit(solution)/shard_map/ppermute | solution.py:633
  267.8 4.1 %open_inward.1 = f32[384,3072]{1,0:T(8,128)} custom-call(s32[8]{0:T(128)} %and_select_fusion.place_ref, bf16[192,768]{1,0:T(8,128)(2,1)} %copy-done.3, bf16[192,768]{1,0:T(8,128)(2,1)} %copy-done.22, bf16[192,768]{1,0:T(8,128)(2,1)} %copy-done.24, bf16[192,768]{1,0:T(8,128)(2,1)} %copy-done.25, bf16[192,768]{1,0:T(8,128)(2,1)} %copy-done.27, ...), custom_call_target="tpu_custom_call" | custom-call | flops 4000000000 | tf_op jit(solution)/shard_map/open_inward/pallas_call | solution.py:267
  271.9 2.4 collective-permute-done.36.refs_7_
  275.0 4.0 %open_rest.1 = (f32[384,2304]{1,0:T(8,128)}, f32[384,768]{1,0:T(8,128)}, f32[1,384]{1,0:T(1,128)}, f32[1,384]{1,0:T(1,128)}, f32[1,384]{1,0:T(1,128)}, /*index=5...) custom-call(s32[8]{0:T(128)} %and_select_fusion.place_ref, ...), custom_call_target="tpu_custom_call" | custom-call | flops 4000000000 | tf_op jit(solution)/shard_map/open_rest/pallas_call | solution.py:267
  (144 shorter events, 61.1 us)
Async XLA Ops:
  5.4 15.9 %collective-permute-start = (bf16[2,512,256]{2,1,0:T(8,128)(2,1)}, bf16[2,512,256]{2,1,0:T(8,128)(2,1)S(1)}, u32[]{:S(2)}, u32[]{:S(2)}) collective-permute-start(bf16[2,512,256]{2,1,0:T(8,128)(2,1)} %get-tuple-element.90), channel_id=1, source_target_pairs={{0,16},{16,0},{1,17},{17,1},{2,18},{18,2},{3,19},{19,3},{4,20},{20... | collective-permute-start | bytes 1572872 | tf_op jit(solution)/shard_map/ppermute | solution.py:623
  8.4 24.2 %collective-permute-start.1 = (bf16[2,512,256]{2,1,0:T(8,128)(2,1)}, bf16[2,512,256]{2,1,0:T(8,128)(2,1)S(1)}, u32[]{:S(2)}, u32[]{:S(2)}) collective-permute-start(bf16[2,512,256]{2,1,0:T(8,128)(2,1)} %get-tuple-element.96), channel_id=1, source_target_pairs={{0,16},{16,0},{1,17},{17,1},{2,18},{18,2},{3,19},{19,3},{4,20},{20... | collective-permute-start | bytes 1572872 | tf_op jit(solution)/shard_map/ppermute | solution.py:623
  8.4 34.6 %collective-permute-start.2 = (bf16[2,512,256]{2,1,0:T(8,128)(2,1)}, bf16[2,512,256]{2,1,0:T(8,128)(2,1)S(1)}, u32[]{:S(2)}, u32[]{:S(2)}) collective-permute-start(bf16[2,512,256]{2,1,0:T(8,128)(2,1)} %get-tuple-element.99), channel_id=1, source_target_pairs={{0,16},{16,0},{1,17},{17,1},{2,18},{18,2},{3,19},{19,3},{4,20},{20... | collective-permute-start | bytes 1572872 | tf_op jit(solution)/shard_map/ppermute | solution.py:623
  81.3 9.9 %collective-permute-start.4 = (bf16[8,384,768]{2,1,0:T(8,128)(2,1)}, bf16[8,384,768]{2,1,0:T(8,128)(2,1)}, u32[]{:S(2)}, u32[]{:S(2)}) collective-permute-start(bf16[8,384,768]{2,1,0:T(8,128)(2,1)} %get-tuple-element.111), channel_id=1, source_target_pairs={{0,1},{1,0},{2,3},{3,2},{4,5},{5,4},{6,7},{7,6},{8,9},{9,8},{10,11... | collective-permute-start | bytes 14155784 | tf_op jit(solution)/shard_map/ppermute | solution.py:714
  89.5 16.5 %collective-permute-start.3 = (bf16[2,512,256]{2,1,0:T(8,128)(2,1)}, bf16[2,512,256]{2,1,0:T(8,128)(2,1)S(1)}, u32[]{:S(2)}, u32[]{:S(2)}) collective-permute-start(bf16[2,512,256]{2,1,0:T(8,128)(2,1)} %get-tuple-element.107), channel_id=1, source_target_pairs={{0,16},{16,0},{1,17},{17,1},{2,18},{18,2},{3,19},{19,3},{4,20},{20... | collective-permute-start | bytes 1572872 | tf_op jit(solution)/shard_map/ppermute | solution.py:623
  92.6 10.2 %collective-permute-start.6 = (bf16[384,768]{1,0:T(8,128)(2,1)S(1)}, bf16[384,768]{1,0:T(8,128)(2,1)S(1)}, u32[]{:S(2)}, u32[]{:S(2)}) collective-permute-start(bf16[384,768]{1,0:T(8,128)(2,1)S(1)} %fusion.3), channel_id=1, source_target_pairs={{0,4},{1,3},{4,8},{5,1},{8,12},{9,5},{12,14},{13,9},{14,10},{15,13... | collective-permute-start | bytes 1769480 | tf_op jit(solution)/shard_map/ppermute | solution.py:633
  102.3 22.3 %collective-permute-start.5 = (bf16[2,512,256]{2,1,0:T(8,128)(2,1)}, bf16[2,512,256]{2,1,0:T(8,128)(2,1)S(1)}, u32[]{:S(2)}, u32[]{:S(2)}) collective-permute-start(bf16[2,512,256]{2,1,0:T(8,128)(2,1)} %get-tuple-element.115), channel_id=1, source_target_pairs={{0,16},{16,0},{1,17},{17,1},{2,18},{18,2},{3,19},{19,3},{4,20},{20... | collective-permute-start | bytes 1572872 | tf_op jit(solution)/shard_map/ppermute | solution.py:623
  104.3 9.9 %collective-permute-start.7 = (bf16[384,768]{1,0:T(8,128)(2,1)S(1)}, bf16[384,768]{1,0:T(8,128)(2,1)S(1)}, u32[]{:S(2)}, u32[]{:S(2)}) collective-permute-start(bf16[384,768]{1,0:T(8,128)(2,1)S(1)} %fusion.2), channel_id=1, source_target_pairs={{0,4},{1,3},{4,8},{5,1},{8,12},{9,5},{12,14},{13,9},{14,10},{15,13... | collective-permute-start | bytes 1769480 | tf_op jit(solution)/shard_map/ppermute | solution.py:633
  115.8 13.2 %collective-permute-start.8 = (bf16[2,512,256]{2,1,0:T(8,128)(2,1)S(1)}, bf16[2,512,256]{2,1,0:T(8,128)(2,1)S(1)}, u32[]{:S(2)}, u32[]{:S(2)}) collective-permute-start(bf16[2,512,256]{2,1,0:T(8,128)(2,1)S(1)} %copy-done.13), channel_id=1, source_target_pairs={{0,16},{16,0},{1,17},{17,1},{2,18},{18,2},{3,19},{19,3},{4,20},{20... | collective-permute-start | bytes 1572872 | tf_op jit(solution)/shard_map/ppermute | solution.py:623
  117.3 19.5 %collective-permute-start.9 = (bf16[384,768]{1,0:T(8,128)(2,1)S(1)}, bf16[384,768]{1,0:T(8,128)(2,1)S(1)}, u32[]{:S(2)}, u32[]{:S(2)}) collective-permute-start(bf16[384,768]{1,0:T(8,128)(2,1)S(1)} %fusion.1), channel_id=1, source_target_pairs={{0,4},{1,3},{4,8},{5,1},{8,12},{9,5},{12,14},{13,9},{14,10},{15,13... | collective-permute-start | bytes 1769480 | tf_op jit(solution)/shard_map/ppermute | solution.py:633
  138.4 4.8 %collective-permute-start.10 = (bf16[8,192,768]{2,1,0:T(8,128)(2,1)}, bf16[8,192,768]{2,1,0:T(8,128)(2,1)S(1)}, u32[]{:S(2)}, u32[]{:S(2)}) collective-permute-start(bf16[8,192,768]{2,1,0:T(8,128)(2,1)} %get-tuple-element.131), channel_id=1, source_target_pairs={{0,1},{1,0},{2,3},{3,2},{4,5},{5,4},{6,7},{7,6},{8,9},{9,8},{10,11... | collective-permute-start | bytes 7077896 | tf_op jit(solution)/shard_map/ppermute | solution.py:714
  138.5 13.8 %collective-permute-start.25 = (bf16[384,768]{1,0:T(8,128)(2,1)S(1)}, bf16[384,768]{1,0:T(8,128)(2,1)S(1)}, u32[]{:S(2)}, u32[]{:S(2)}) collective-permute-start(bf16[384,768]{1,0:T(8,128)(2,1)S(1)} %fusion), channel_id=1, source_target_pairs={{0,4},{1,3},{4,8},{5,1},{8,12},{9,5},{12,14},{13,9},{14,10},{15,13... | collective-permute-start | bytes 1769480 | tf_op jit(solution)/shard_map/ppermute | solution.py:633
  143.3 8.3 %collective-permute-start.11 = (bf16[192,768]{1,0:T(8,128)(2,1)S(1)}, bf16[192,768]{1,0:T(8,128)(2,1)S(1)}, u32[]{:S(2)}, u32[]{:S(2)}) collective-permute-start(bf16[192,768]{1,0:T(8,128)(2,1)S(1)} %fusion.19), channel_id=1, source_target_pairs={{0,4},{1,3},{4,8},{5,1},{8,12},{9,5},{12,14},{13,9},{14,10},{15,13... | collective-permute-start | bytes 884744 | tf_op jit(solution)/shard_map/ppermute | solution.py:633
  151.7 6.8 %collective-permute-start.12 = (bf16[192,768]{1,0:T(8,128)(2,1)S(1)}, bf16[192,768]{1,0:T(8,128)(2,1)S(1)}, u32[]{:S(2)}, u32[]{:S(2)}) collective-permute-start(bf16[192,768]{1,0:T(8,128)(2,1)S(1)} %fusion.18), channel_id=1, source_target_pairs={{0,4},{1,3},{4,8},{5,1},{8,12},{9,5},{12,14},{13,9},{14,10},{15,13... | collective-permute-start | bytes 884744 | tf_op jit(solution)/shard_map/ppermute | solution.py:633
  153.7 7.9 %collective-permute-start.37 = (bf16[192,768]{1,0:T(8,128)(2,1)S(1)}, bf16[192,768]{1,0:T(8,128)(2,1)S(1)}, u32[]{:S(2)}, u32[]{:S(2)}) collective-permute-start(bf16[192,768]{1,0:T(8,128)(2,1)S(1)} %get-tuple-element.160), channel_id=1, source_target_pairs={{0,4},{1,3},{4,8},{5,1},{8,12},{9,5},{12,14},{13,9},{14,10},{15,13... | collective-permute-start | bytes 884744 | tf_op jit(solution)/shard_map/ppermute | solution.py:633
  155.3 9.5 %collective-permute-start.26 = (bf16[192,768]{1,0:T(8,128)(2,1)S(1)}, bf16[192,768]{1,0:T(8,128)(2,1)S(1)}, u32[]{:S(2)}, u32[]{:S(2)}) collective-permute-start(bf16[192,768]{1,0:T(8,128)(2,1)S(1)} %get-tuple-element.161), channel_id=1, source_target_pairs={{0,4},{1,3},{4,8},{5,1},{8,12},{9,5},{12,14},{13,9},{14,10},{15,13... | collective-permute-start | bytes 884744 | tf_op jit(solution)/shard_map/ppermute | solution.py:633
  158.6 9.7 %collective-permute-start.13 = (bf16[192,768]{1,0:T(8,128)(2,1)S(1)}, bf16[192,768]{1,0:T(8,128)(2,1)S(1)}, u32[]{:S(2)}, u32[]{:S(2)}) collective-permute-start(bf16[192,768]{1,0:T(8,128)(2,1)S(1)} %fusion.17), channel_id=1, source_target_pairs={{0,4},{1,3},{4,8},{5,1},{8,12},{9,5},{12,14},{13,9},{14,10},{15,13... | collective-permute-start | bytes 884744 | tf_op jit(solution)/shard_map/ppermute | solution.py:633
  166.3 14.7 %collective-permute-start.38 = (bf16[192,768]{1,0:T(8,128)(2,1)S(1)}, bf16[192,768]{1,0:T(8,128)(2,1)S(1)}, u32[]{:S(2)}, u32[]{:S(2)}) collective-permute-start(bf16[192,768]{1,0:T(8,128)(2,1)S(1)} %get-tuple-element.166), channel_id=1, source_target_pairs={{0,4},{1,3},{4,8},{5,1},{8,12},{9,5},{12,14},{13,9},{14,10},{15,13... | collective-permute-start | bytes 884744 | tf_op jit(solution)/shard_map/ppermute | solution.py:633
  166.8 14.2 %collective-permute-start.27 = (bf16[192,768]{1,0:T(8,128)(2,1)S(1)}, bf16[192,768]{1,0:T(8,128)(2,1)S(1)}, u32[]{:S(2)}, u32[]{:S(2)}) collective-permute-start(bf16[192,768]{1,0:T(8,128)(2,1)S(1)} %get-tuple-element.167), channel_id=1, source_target_pairs={{0,4},{1,3},{4,8},{5,1},{8,12},{9,5},{12,14},{13,9},{14,10},{15,13... | collective-permute-start | bytes 884744 | tf_op jit(solution)/shard_map/ppermute | solution.py:633
  168.5 10.9 %collective-permute-start.14 = (bf16[192,768]{1,0:T(8,128)(2,1)S(1)}, bf16[192,768]{1,0:T(8,128)(2,1)S(1)}, u32[]{:S(2)}, u32[]{:S(2)}) collective-permute-start(bf16[192,768]{1,0:T(8,128)(2,1)S(1)} %fusion.16), channel_id=1, source_target_pairs={{0,4},{1,3},{4,8},{5,1},{8,12},{9,5},{12,14},{13,9},{14,10},{15,13... | collective-permute-start | bytes 884744 | tf_op jit(solution)/shard_map/ppermute | solution.py:633
  180.5 6.8 %collective-permute-start.15 = (bf16[192,768]{1,0:T(8,128)(2,1)S(1)}, bf16[192,768]{1,0:T(8,128)(2,1)S(1)}, u32[]{:S(2)}, u32[]{:S(2)}) collective-permute-start(bf16[192,768]{1,0:T(8,128)(2,1)S(1)} %fusion.15), channel_id=1, source_target_pairs={{0,4},{1,3},{4,8},{5,1},{8,12},{9,5},{12,14},{13,9},{14,10},{15,13... | collective-permute-start | bytes 884744 | tf_op jit(solution)/shard_map/ppermute | solution.py:633
  182.5 7.9 %collective-permute-start.39 = (bf16[192,768]{1,0:T(8,128)(2,1)S(1)}, bf16[192,768]{1,0:T(8,128)(2,1)S(1)}, u32[]{:S(2)}, u32[]{:S(2)}) collective-permute-start(bf16[192,768]{1,0:T(8,128)(2,1)S(1)} %get-tuple-element.164), channel_id=1, source_target_pairs={{0,4},{1,3},{4,8},{5,1},{8,12},{9,5},{12,14},{13,9},{14,10},{15,13... | collective-permute-start | bytes 884744 | tf_op jit(solution)/shard_map/ppermute | solution.py:633
  184.0 9.5 %collective-permute-start.28 = (bf16[192,768]{1,0:T(8,128)(2,1)S(1)}, bf16[192,768]{1,0:T(8,128)(2,1)S(1)}, u32[]{:S(2)}, u32[]{:S(2)}) collective-permute-start(bf16[192,768]{1,0:T(8,128)(2,1)S(1)} %get-tuple-element.165), channel_id=1, source_target_pairs={{0,4},{1,3},{4,8},{5,1},{8,12},{9,5},{12,14},{13,9},{14,10},{15,13... | collective-permute-start | bytes 884744 | tf_op jit(solution)/shard_map/ppermute | solution.py:633
  188.3 8.4 %collective-permute-start.16 = (bf16[192,768]{1,0:T(8,128)(2,1)S(1)}, bf16[192,768]{1,0:T(8,128)(2,1)S(1)}, u32[]{:S(2)}, u32[]{:S(2)}) collective-permute-start(bf16[192,768]{1,0:T(8,128)(2,1)S(1)} %fusion.14), channel_id=1, source_target_pairs={{0,4},{1,3},{4,8},{5,1},{8,12},{9,5},{12,14},{13,9},{14,10},{15,13... | collective-permute-start | bytes 884744 | tf_op jit(solution)/shard_map/ppermute | solution.py:633
  195.0 69.2 %copy-start.3 = (bf16[192,768]{1,0:T(8,128)(2,1)}, bf16[192,768]{1,0:T(8,128)(2,1)S(1)}, u32[]{:S(2)}) copy-start(bf16[192,768]{1,0:T(8,128)(2,1)S(1)} %get-tuple-element.162.refs_0_) | copy-start | bytes 884740
  195.0 6.8 %collective-permute-start.29 = (bf16[192,768]{1,0:T(8,128)(2,1)S(1)}, bf16[192,768]{1,0:T(8,128)(2,1)S(1)}, u32[]{:S(2)}, u32[]{:S(2)}) collective-permute-start(bf16[192,768]{1,0:T(8,128)(2,1)S(1)} %get-tuple-element.163.refs_0_), channel_id=1, source_target_pairs={{0,4},{1,3},{4,8},{5,1},{8,12},{9,5},{12,14},{13,9},{14,10},{15,13... | collective-permute-start | bytes 884744 | tf_op jit(solution)/shard_map/ppermute | solution.py:633
  197.8 7.2 %collective-permute-start.17 = (bf16[192,768]{1,0:T(8,128)(2,1)S(1)}, bf16[192,768]{1,0:T(8,128)(2,1)S(1)}, u32[]{:S(2)}, u32[]{:S(2)}) collective-permute-start(bf16[192,768]{1,0:T(8,128)(2,1)S(1)} %fusion.13), channel_id=1, source_target_pairs={{0,4},{1,3},{4,8},{5,1},{8,12},{9,5},{12,14},{13,9},{14,10},{15,13... | collective-permute-start | bytes 884744 | tf_op jit(solution)/shard_map/ppermute | solution.py:633
  198.3 4.0 %collective-permute-start.18 = (f32[16,768]{1,0:T(8,128)S(1)}, f32[16,768]{1,0:T(8,128)S(1)}, u32[]{:S(2)}, u32[]{:S(2)}) collective-permute-start(f32[16,768]{1,0:T(8,128)S(1)} %copy-done.30), channel_id=1, source_target_pairs={{0,1},{1,0},{2,3},{3,2},{4,5},{5,4},{6,7},{7,6},{8,9},{9,8},{10,11... | collective-permute-start | bytes 147464 | tf_op jit(solution)/shard_map/ppermute | solution.py:835
  198.3 9.8 %collective-permute-start.40 = (bf16[192,768]{1,0:T(8,128)(2,1)S(1)}, bf16[192,768]{1,0:T(8,128)(2,1)S(1)}, u32[]{:S(2)}, u32[]{:S(2)}) collective-permute-start(bf16[192,768]{1,0:T(8,128)(2,1)S(1)} %get-tuple-element.162.refs_0_), channel_id=1, source_target_pairs={{0,4},{1,3},{4,8},{5,1},{8,12},{9,5},{12,14},{13,9},{14,10},{15,13... | collective-permute-start | bytes 884744 | tf_op jit(solution)/shard_map/ppermute | solution.py:633
  201.8 9.5 %collective-permute-start.30 = (bf16[192,768]{1,0:T(8,128)(2,1)S(1)}, bf16[192,768]{1,0:T(8,128)(2,1)S(1)}, u32[]{:S(2)}, u32[]{:S(2)}) collective-permute-start(bf16[192,768]{1,0:T(8,128)(2,1)S(1)} %collective-permute-done.29.refs_1_), channel_id=1, source_target_pairs={{0,4},{1,3},{4,8},{5,1},{8,12},{9,5},{12,14},{13,9},{14,10},{15,13... | collective-permute-start | bytes 884744 | tf_op jit(solution)/shard_map/ppermute | solution.py:633
  206.1 8.6 %collective-permute-start.19 = (bf16[208,768]{1,0:T(8,128)(2,1)S(1)}, bf16[208,768]{1,0:T(8,128)(2,1)S(1)}, u32[]{:S(2)}, u32[]{:S(2)}) collective-permute-start(bf16[208,768]{1,0:T(8,128)(2,1)S(1)} %pad_maximum_fusion.refs_0_), channel_id=1, source_target_pairs={{0,4},{1,3},{4,8},{5,1},{8,12},{9,5},{12,14},{13,9},{14,10},{15,13... | collective-permute-start | bytes 958472 | tf_op jit(solution)/shard_map/ppermute | solution.py:633
  208.1 9.7 %collective-permute-start.41 = (bf16[192,768]{1,0:T(8,128)(2,1)S(1)}, bf16[192,768]{1,0:T(8,128)(2,1)S(1)}, u32[]{:S(2)}, u32[]{:S(2)}) collective-permute-start(bf16[192,768]{1,0:T(8,128)(2,1)S(1)} %collective-permute-done.40.refs_1_), channel_id=1, source_target_pairs={{0,4},{1,3},{4,8},{5,1},{8,12},{9,5},{12,14},{13,9},{14,10},{15,13... | collective-permute-start | bytes 884744 | tf_op jit(solution)/shard_map/ppermute | solution.py:633
  211.3 9.7 %collective-permute-start.31 = (bf16[192,768]{1,0:T(8,128)(2,1)S(1)}, bf16[192,768]{1,0:T(8,128)(2,1)S(1)}, u32[]{:S(2)}, u32[]{:S(2)}) collective-permute-start(bf16[192,768]{1,0:T(8,128)(2,1)S(1)} %collective-permute-done.30.refs_2_), channel_id=1, source_target_pairs={{0,4},{1,3},{4,8},{5,1},{8,12},{9,5},{12,14},{13,9},{14,10},{15,13... | collective-permute-start | bytes 884744 | tf_op jit(solution)/shard_map/ppermute | solution.py:633
  214.7 9.7 %collective-permute-start.20 = (bf16[208,768]{1,0:T(8,128)(2,1)S(1)}, bf16[208,768]{1,0:T(8,128)(2,1)S(1)}, u32[]{:S(2)}, u32[]{:S(2)}) collective-permute-start(bf16[208,768]{1,0:T(8,128)(2,1)S(1)} %collective-permute-done.19.refs_1_), channel_id=1, source_target_pairs={{0,4},{1,3},{4,8},{5,1},{8,12},{9,5},{12,14},{13,9},{14,10},{15,13... | collective-permute-start | bytes 958472 | tf_op jit(solution)/shard_map/ppermute | solution.py:633
  217.9 9.7 %collective-permute-start.42 = (bf16[192,768]{1,0:T(8,128)(2,1)S(1)}, bf16[192,768]{1,0:T(8,128)(2,1)S(1)}, u32[]{:S(2)}, u32[]{:S(2)}) collective-permute-start(bf16[192,768]{1,0:T(8,128)(2,1)S(1)} %collective-permute-done.41.refs_2_), channel_id=1, source_target_pairs={{0,4},{1,3},{4,8},{5,1},{8,12},{9,5},{12,14},{13,9},{14,10},{15,13... | collective-permute-start | bytes 884744 | tf_op jit(solution)/shard_map/ppermute | solution.py:633
  221.0 9.7 %collective-permute-start.32 = (bf16[192,768]{1,0:T(8,128)(2,1)S(1)}, bf16[192,768]{1,0:T(8,128)(2,1)S(1)}, u32[]{:S(2)}, u32[]{:S(2)}) collective-permute-start(bf16[192,768]{1,0:T(8,128)(2,1)S(1)} %collective-permute-done.31.refs_3_), channel_id=1, source_target_pairs={{0,4},{1,3},{4,8},{5,1},{8,12},{9,5},{12,14},{13,9},{14,10},{15,13... | collective-permute-start | bytes 884744 | tf_op jit(solution)/shard_map/ppermute | solution.py:633
  224.4 9.7 %collective-permute-start.21 = (bf16[208,768]{1,0:T(8,128)(2,1)S(1)}, bf16[208,768]{1,0:T(8,128)(2,1)S(1)}, u32[]{:S(2)}, u32[]{:S(2)}) collective-permute-start(bf16[208,768]{1,0:T(8,128)(2,1)S(1)} %collective-permute-done.20.refs_2_), channel_id=1, source_target_pairs={{0,4},{1,3},{4,8},{5,1},{8,12},{9,5},{12,14},{13,9},{14,10},{15,13... | collective-permute-start | bytes 958472 | tf_op jit(solution)/shard_map/ppermute | solution.py:633
  227.6 9.7 %collective-permute-start.43 = (bf16[192,768]{1,0:T(8,128)(2,1)S(1)}, bf16[192,768]{1,0:T(8,128)(2,1)S(1)}, u32[]{:S(2)}, u32[]{:S(2)}) collective-permute-start(bf16[192,768]{1,0:T(8,128)(2,1)S(1)} %collective-permute-done.42.refs_3_), channel_id=1, source_target_pairs={{0,4},{1,3},{4,8},{5,1},{8,12},{9,5},{12,14},{13,9},{14,10},{15,13... | collective-permute-start | bytes 884744 | tf_op jit(solution)/shard_map/ppermute | solution.py:633
  230.8 9.7 %collective-permute-start.33 = (bf16[192,768]{1,0:T(8,128)(2,1)S(1)}, bf16[192,768]{1,0:T(8,128)(2,1)S(1)}, u32[]{:S(2)}, u32[]{:S(2)}) collective-permute-start(bf16[192,768]{1,0:T(8,128)(2,1)S(1)} %collective-permute-done.32.refs_4_), channel_id=1, source_target_pairs={{0,4},{1,3},{4,8},{5,1},{8,12},{9,5},{12,14},{13,9},{14,10},{15,13... | collective-permute-start | bytes 884744 | tf_op jit(solution)/shard_map/ppermute | solution.py:633
  234.2 9.7 %collective-permute-start.22 = (bf16[208,768]{1,0:T(8,128)(2,1)S(1)}, bf16[208,768]{1,0:T(8,128)(2,1)S(1)}, u32[]{:S(2)}, u32[]{:S(2)}) collective-permute-start(bf16[208,768]{1,0:T(8,128)(2,1)S(1)} %collective-permute-done.21.refs_3_), channel_id=1, source_target_pairs={{0,4},{1,3},{4,8},{5,1},{8,12},{9,5},{12,14},{13,9},{14,10},{15,13... | collective-permute-start | bytes 958472 | tf_op jit(solution)/shard_map/ppermute | solution.py:633
  237.3 9.8 %collective-permute-start.44 = (bf16[192,768]{1,0:T(8,128)(2,1)S(1)}, bf16[192,768]{1,0:T(8,128)(2,1)}, u32[]{:S(2)}, u32[]{:S(2)}) collective-permute-start(bf16[192,768]{1,0:T(8,128)(2,1)S(1)} %collective-permute-done.43.refs_4_), channel_id=1, source_target_pairs={{0,4},{1,3},{4,8},{5,1},{8,12},{9,5},{12,14},{13,9},{14,10},{15,13... | collective-permute-start | bytes 884744 | tf_op jit(solution)/shard_map/ppermute | solution.py:633
  240.5 9.8 %collective-permute-start.34 = (bf16[192,768]{1,0:T(8,128)(2,1)S(1)}, bf16[192,768]{1,0:T(8,128)(2,1)}, u32[]{:S(2)}, u32[]{:S(2)}) collective-permute-start(bf16[192,768]{1,0:T(8,128)(2,1)S(1)} %collective-permute-done.33.refs_5_), channel_id=1, source_target_pairs={{0,4},{1,3},{4,8},{5,1},{8,12},{9,5},{12,14},{13,9},{14,10},{15,13... | collective-permute-start | bytes 884744 | tf_op jit(solution)/shard_map/ppermute | solution.py:633
  243.9 13.5 %collective-permute-start.23 = (bf16[208,768]{1,0:T(8,128)(2,1)S(1)}, bf16[208,768]{1,0:T(8,128)(2,1)S(1)}, u32[]{:S(2)}, u32[]{:S(2)}) collective-permute-start(bf16[208,768]{1,0:T(8,128)(2,1)S(1)} %collective-permute-done.22.refs_4_), channel_id=1, source_target_pairs={{0,4},{1,3},{4,8},{5,1},{8,12},{9,5},{12,14},{13,9},{14,10},{15,13... | collective-permute-start | bytes 958472 | tf_op jit(solution)/shard_map/ppermute | solution.py:633
  247.2 9.7 %collective-permute-start.45 = (bf16[192,768]{1,0:T(8,128)(2,1)}, bf16[192,768]{1,0:T(8,128)(2,1)}, u32[]{:S(2)}, u32[]{:S(2)}) collective-permute-start(bf16[192,768]{1,0:T(8,128)(2,1)} %collective-permute-done.44.refs_5_), channel_id=1, source_target_pairs={{0,4},{1,3},{4,8},{5,1},{8,12},{9,5},{12,14},{13,9},{14,10},{15,13... | collective-permute-start | bytes 884744 | tf_op jit(solution)/shard_map/ppermute | solution.py:633
  250.4 9.7 %collective-permute-start.35 = (bf16[192,768]{1,0:T(8,128)(2,1)}, bf16[192,768]{1,0:T(8,128)(2,1)}, u32[]{:S(2)}, u32[]{:S(2)}) collective-permute-start(bf16[192,768]{1,0:T(8,128)(2,1)} %collective-permute-done.34.refs_6_), channel_id=1, source_target_pairs={{0,4},{1,3},{4,8},{5,1},{8,12},{9,5},{12,14},{13,9},{14,10},{15,13... | collective-permute-start | bytes 884744 | tf_op jit(solution)/shard_map/ppermute | solution.py:633
  256.9 10.9 %collective-permute-start.46 = (bf16[192,768]{1,0:T(8,128)(2,1)}, bf16[192,768]{1,0:T(8,128)(2,1)}, u32[]{:S(2)}, u32[]{:S(2)}) collective-permute-start(bf16[192,768]{1,0:T(8,128)(2,1)} %collective-permute-done.45.refs_6_), channel_id=1, source_target_pairs={{0,4},{1,3},{4,8},{5,1},{8,12},{9,5},{12,14},{13,9},{14,10},{15,13... | collective-permute-start | bytes 884744 | tf_op jit(solution)/shard_map/ppermute | solution.py:633
  257.4 9.9 %collective-permute-start.24 = (bf16[208,768]{1,0:T(8,128)(2,1)S(1)}, bf16[208,768]{1,0:T(8,128)(2,1)S(1)}, u32[]{:S(2)}, u32[]{:S(2)}) collective-permute-start(bf16[208,768]{1,0:T(8,128)(2,1)S(1)} %collective-permute-done.23.refs_5_), channel_id=1, source_target_pairs={{0,4},{1,3},{4,8},{5,1},{8,12},{9,5},{12,14},{13,9},{14,10},{15,13... | collective-permute-start | bytes 958472 | tf_op jit(solution)/shard_map/ppermute | solution.py:633
  267.3 7.0 %collective-permute-start.36 = (bf16[208,768]{1,0:T(8,128)(2,1)S(1)}, bf16[208,768]{1,0:T(8,128)(2,1)S(1)}, u32[]{:S(2)}, u32[]{:S(2)}) collective-permute-start(bf16[208,768]{1,0:T(8,128)(2,1)S(1)} %collective-permute-done.24.refs_6_), channel_id=1, source_target_pairs={{0,4},{1,3},{4,8},{5,1},{8,12},{9,5},{12,14},{13,9},{14,10},{15,13... | collective-permute-start | bytes 958472 | tf_op jit(solution)/shard_map/ppermute | solution.py:633
  (30 other events, 600.7 us)
